TPU v7x, 32 devices: a whole 2x2x4 slice. The times are simulated.
32 devices in a mesh: dp: 16 (over z, y, x), tensor: 2 (over core).
Axes of the slice: x: 2, y: 2, z: 4, core: 2. Of those that a mesh axis runs over, the one named last changes fastest.
Arguments:
- tokens: bfloat16 [32, 256, 1536], P('dp'), may hold values from -6 to 6
- context: bfloat16 [32, 130, 768], P('dp'), may hold values from -6 to 6
- live_count: int32 [16], P('dp'), may hold values from 1 to 2, as said below
- cotangent: bfloat16 [32, 256, 1536], P('dp'), may hold values from -6 to 6
- triple_weight: bfloat16 [1536, 3, 1536], P('dp', None, 'tensor'), may hold values from -0.15625 to 0.15625
- attn_out_weight: bfloat16 [1536, 1536], P('tensor', 'dp'), may hold values from -0.4375 to 0.4375
- cross_query_weight: bfloat16 [1536, 1536], P('dp', 'tensor'), may hold values from -0.15625 to 0.15625
- cross_pair_weight: bfloat16 [768, 2, 1536], P('dp', None, 'tensor'), may hold values from -0.21875 to 0.21875
- cross_out_weight: bfloat16 [1536, 1536], P('tensor', 'dp'), may hold values from -0.4375 to 0.4375
- gate_up_weight: bfloat16 [1536, 2, 6144], P('dp', None, 'tensor'), may hold values from -0.15625 to 0.15625
- down_weight: bfloat16 [6144, 1536], P('tensor', 'dp'), may hold values from -0.078125 to 0.078125
- norm_gains: bfloat16 [3, 1536], P(None, 'dp'), may hold values from 0.099609375 to 1.8984375
- norm_shifts: bfloat16 [3, 1536], P(None, 'dp'), may hold values from -3 to 3
Outputs:
- mixed: bfloat16 [32, 256, 1536], P('dp')
- grad_tokens: float32 [32, 256, 1536], P('dp')
- grad_context: float32 [32, 130, 768], P('dp')
- grad_triple: float32 [1536, 3, 1536], P('dp', None, 'tensor')
- grad_attn_out: float32 [1536, 1536], P('tensor', 'dp')
- grad_cross_query: float32 [1536, 1536], P('dp', 'tensor')
- grad_cross_pair: float32 [768, 2, 1536], P('dp', None, 'tensor')
- grad_cross_out: float32 [1536, 1536], P('tensor', 'dp')
- grad_gate_up: float32 [1536, 2, 6144], P('dp', None, 'tensor')
- grad_down: float32 [6144, 1536], P('tensor', 'dp')
- grad_gains: float32 [3, 1536], P(None, 'dp')
- grad_shifts: float32 [3, 1536], P(None, 'dp')
Inputs may be any that keep to these rules, and one draw needn't show every extreme that they name: Slot m of a dp index is live exactly when m < its live_count; some index has 2 live slots and some has 1.
All inputs are finite; a program needn't handle non-finite values.
Results may differ from a plain program's by a relative error of at most 0.023.
Values may be sent and summed in bfloat16 or wider, within the bound.
No kernel may reach another device: no remote copies, remote signals or barrier semaphores. Data moves between devices by JAX's collectives and lax.ppermute only.
A program may use at most 256 MiB of HBM per device.

v0:
```python
import jax
import jax.numpy as jnp
from jax import lax
from jax.sharding import PartitionSpec as P

HD = 64
ROT = 32


EPSILON = 1e-05


def norm_forward(values, gain_row, shift_row):
    average = jnp.mean(values, axis=-1, keepdims=True)
    centred = values - average
    spread = jnp.mean(centred * centred, axis=-1, keepdims=True)
    factor = lax.rsqrt(spread + EPSILON)
    normed = centred * factor
    return (normed * gain_row + shift_row, normed, factor)


def norm_backward(grad_rows, normed, factor, gain_row):
    scaled = grad_rows * gain_row
    first_mean = jnp.mean(scaled, axis=-1, keepdims=True)
    second_mean = jnp.mean(scaled * normed, axis=-1, keepdims=True)
    grad_values = factor * (scaled - first_mean - normed * second_mean)
    return (grad_values, jnp.sum(grad_rows * normed, axis=0), jnp.sum(grad_rows, axis=0))


def rotary_tables(length):
    half_dim = ROT // 2
    freqs = 10000.0 ** (-(2.0 * jnp.arange(half_dim, dtype=jnp.float32) / ROT))
    angles = jnp.arange(length, dtype=jnp.float32)[:, None] * freqs[None, :]
    return (jnp.cos(angles)[:, None, :], jnp.sin(angles)[:, None, :])


def rotate(values, cos_table, sin_table):
    half_dim = ROT // 2
    former = values[..., :half_dim]
    latter = values[..., half_dim:ROT]
    rest = values[..., ROT:]
    return jnp.concatenate(
        [former * cos_table - latter * sin_table, latter * cos_table + former * sin_table, rest],
        axis=-1,
    )


def attend(queries, key_rows, value_rows):
    scores = jnp.einsum(
        "qhd,khd->hqk", queries, key_rows, preferred_element_type=jnp.float32
    ) * HD ** (-0.5)
    row_max = jnp.max(scores, axis=-1, keepdims=True)
    exponent = jnp.exp(scores - row_max)
    row_sum = jnp.sum(exponent, axis=-1, keepdims=True)
    prob_rows = (exponent / row_sum).astype(jnp.bfloat16)
    mixed_rows = jnp.einsum(
        "hqk,khd->qhd", prob_rows, value_rows, preferred_element_type=jnp.float32
    )
    return (mixed_rows.astype(jnp.bfloat16), row_max + jnp.log(row_sum))


def attend_back(queries, key_rows, value_rows, grad_mixed, logsum):
    scores = jnp.einsum(
        "qhd,khd->hqk", queries, key_rows, preferred_element_type=jnp.float32
    ) * HD ** (-0.5)
    prob_rows = jnp.exp(scores - logsum)
    grad_probs = jnp.einsum(
        "qhd,khd->hqk", grad_mixed, value_rows, preferred_element_type=jnp.float32
    )
    centre = jnp.sum(prob_rows * grad_probs, axis=-1, keepdims=True)
    grad_scores = (prob_rows * (grad_probs - centre)).astype(jnp.bfloat16)
    grad_queries = jnp.einsum(
        "hqk,khd->qhd", grad_scores, key_rows, preferred_element_type=jnp.float32
    ) * HD ** (-0.5)
    grad_keys = jnp.einsum(
        "hqk,qhd->khd", grad_scores, queries, preferred_element_type=jnp.float32
    ) * HD ** (-0.5)
    grad_values = jnp.einsum(
        "hqk,qhd->khd",
        prob_rows.astype(jnp.bfloat16),
        grad_mixed,
        preferred_element_type=jnp.float32,
    )
    return (grad_queries, grad_keys, grad_values)


def head_sum(partial_rows):
    return lax.psum(partial_rows, "tensor")


def norm_sum(partial_rows):
    return lax.psum(partial_rows.astype(jnp.bfloat16), "tensor").astype(jnp.float32)


def forward_slot(params, start_rows, context, cos_table, sin_table):
    (
        triple_w,
        attn_out_w,
        cross_query_w,
        cross_pair_w,
        cross_out_w,
        gate_up_w,
        down_w,
        gains,
        shifts,
    ) = params
    length = start_rows.shape[0]
    context_len = context.shape[0]
    local_width = triple_w.shape[2]
    head_count = local_width // HD
    gain_all = gains.astype(jnp.float32)
    shift_all = shifts.astype(jnp.float32)
    start = start_rows.astype(jnp.float32)
    normed_one, hat_one, factor_one = norm_forward(start, gain_all[0], shift_all[0])
    input_one = normed_one.astype(jnp.bfloat16)
    triple = jnp.einsum("sd,dtf->stf", input_one, triple_w, preferred_element_type=jnp.float32)
    queries = rotate(triple[:, 0].reshape(length, head_count, HD), cos_table, sin_table).astype(
        jnp.bfloat16
    )
    key_rows = rotate(triple[:, 1].reshape(length, head_count, HD), cos_table, sin_table).astype(
        jnp.bfloat16
    )
    value_rows = triple[:, 2].reshape(length, head_count, HD).astype(jnp.bfloat16)
    mixed_one, logsum_one = attend(queries, key_rows, value_rows)
    mixed_one = mixed_one.reshape(length, local_width)
    first_sum = start + head_sum(jnp.dot(mixed_one, attn_out_w, preferred_element_type=jnp.float32))
    normed_two, hat_two, factor_two = norm_forward(first_sum, gain_all[1], shift_all[1])
    input_two = normed_two.astype(jnp.bfloat16)
    cross_queries = (
        jnp.dot(input_two, cross_query_w, preferred_element_type=jnp.float32)
        .astype(jnp.bfloat16)
        .reshape(length, head_count, HD)
    )
    pair_rows = jnp.einsum("cd,dtf->ctf", context, cross_pair_w, preferred_element_type=jnp.float32)
    cross_keys = pair_rows[:, 0].reshape(context_len, head_count, HD).astype(jnp.bfloat16)
    cross_values = pair_rows[:, 1].reshape(context_len, head_count, HD).astype(jnp.bfloat16)
    mixed_two, logsum_two = attend(cross_queries, cross_keys, cross_values)
    mixed_two = mixed_two.reshape(length, local_width)
    second_sum = first_sum + head_sum(
        jnp.dot(mixed_two, cross_out_w, preferred_element_type=jnp.float32)
    )
    normed_three, hat_three, factor_three = norm_forward(second_sum, gain_all[2], shift_all[2])
    input_three = normed_three.astype(jnp.bfloat16)
    gate_up = jnp.einsum("sd,dtf->stf", input_three, gate_up_w, preferred_element_type=jnp.float32)
    gate_rows = gate_up[:, 0]
    upper_rows = gate_up[:, 1]
    hidden = (jax.nn.silu(gate_rows) * upper_rows).astype(jnp.bfloat16)
    final = second_sum + head_sum(jnp.dot(hidden, down_w, preferred_element_type=jnp.float32))
    saved = {
        "hat_one": hat_one,
        "factor_one": factor_one,
        "input_one": input_one,
        "queries": queries,
        "key_rows": key_rows,
        "value_rows": value_rows,
        "mixed_one": mixed_one,
        "logsum_one": logsum_one,
        "hat_two": hat_two,
        "factor_two": factor_two,
        "input_two": input_two,
        "cross_queries": cross_queries,
        "cross_keys": cross_keys,
        "cross_values": cross_values,
        "mixed_two": mixed_two,
        "logsum_two": logsum_two,
        "hat_three": hat_three,
        "factor_three": factor_three,
        "input_three": input_three,
        "gate_rows": gate_rows,
        "upper_rows": upper_rows,
        "hidden": hidden,
    }
    return (final, saved)


def backward_slot(params, saved, grad_out, context, cos_table, sin_table):
    (
        triple_w,
        attn_out_w,
        cross_query_w,
        cross_pair_w,
        cross_out_w,
        gate_up_w,
        down_w,
        gains,
        shifts,
    ) = params
    gain_all = gains.astype(jnp.float32)
    length = grad_out.shape[0]
    context_len = context.shape[0]
    local_width = triple_w.shape[2]
    head_count = local_width // HD
    grad_branch = grad_out.astype(jnp.bfloat16)
    grad_down = jnp.einsum(
        "sf,sd->fd", saved["hidden"], grad_branch, preferred_element_type=jnp.float32
    )
    grad_hidden = jnp.einsum("sd,fd->sf", grad_branch, down_w, preferred_element_type=jnp.float32)
    gate_rows = saved["gate_rows"]
    sigmoid_rows = jax.nn.sigmoid(gate_rows)
    grad_gate = (
        grad_hidden
        * saved["upper_rows"]
        * (sigmoid_rows * (1.0 + gate_rows * (1.0 - sigmoid_rows)))
    )
    grad_upper = grad_hidden * (gate_rows * sigmoid_rows)
    grad_pair_rows = jnp.stack([grad_gate, grad_upper], axis=1).astype(jnp.bfloat16)
    grad_gate_up = jnp.einsum(
        "sd,stf->dtf", saved["input_three"], grad_pair_rows, preferred_element_type=jnp.float32
    )
    grad_normed = norm_sum(
        jnp.einsum("stf,dtf->sd", grad_pair_rows, gate_up_w, preferred_element_type=jnp.float32)
    )
    back_rows, gain_three, shift_three = norm_backward(
        grad_normed, saved["hat_three"], saved["factor_three"], gain_all[2]
    )
    grad_second = grad_out + back_rows
    grad_branch = grad_second.astype(jnp.bfloat16)
    grad_cross_out = jnp.einsum(
        "sf,sd->fd", saved["mixed_two"], grad_branch, preferred_element_type=jnp.float32
    )
    grad_mixed = jnp.einsum(
        "sd,fd->sf", grad_branch, cross_out_w, preferred_element_type=jnp.float32
    )
    grad_mixed = grad_mixed.astype(jnp.bfloat16).reshape(length, head_count, HD)
    grad_cq, grad_ck, grad_cv = attend_back(
        saved["cross_queries"],
        saved["cross_keys"],
        saved["cross_values"],
        grad_mixed,
        saved["logsum_two"],
    )
    grad_cq = grad_cq.reshape(length, local_width).astype(jnp.bfloat16)
    grad_context_pair = jnp.stack(
        [grad_ck.reshape(context_len, local_width), grad_cv.reshape(context_len, local_width)],
        axis=1,
    ).astype(jnp.bfloat16)
    grad_cross_query = jnp.einsum(
        "sd,sf->df", saved["input_two"], grad_cq, preferred_element_type=jnp.float32
    )
    grad_cross_pair = jnp.einsum(
        "cd,ctf->dtf", context, grad_context_pair, preferred_element_type=jnp.float32
    )
    normed_part = jnp.einsum(
        "sf,df->sd", grad_cq, cross_query_w, preferred_element_type=jnp.float32
    )
    context_part = jnp.einsum(
        "ctf,dtf->cd", grad_context_pair, cross_pair_w, preferred_element_type=jnp.float32
    )
    grad_normed, grad_context = (
        lax.psum(normed_part.astype(jnp.bfloat16), "tensor").astype(jnp.float32),
        lax.psum(context_part.astype(jnp.bfloat16), "tensor").astype(jnp.float32),
    )
    back_rows, gain_two, shift_two = norm_backward(
        grad_normed, saved["hat_two"], saved["factor_two"], gain_all[1]
    )
    grad_first = grad_second + back_rows
    grad_branch = grad_first.astype(jnp.bfloat16)
    grad_attn_out = jnp.einsum(
        "sf,sd->fd", saved["mixed_one"], grad_branch, preferred_element_type=jnp.float32
    )
    grad_mixed = jnp.einsum(
        "sd,fd->sf", grad_branch, attn_out_w, preferred_element_type=jnp.float32
    )
    grad_mixed = grad_mixed.astype(jnp.bfloat16).reshape(length, head_count, HD)
    grad_sq, grad_sk, grad_sv = attend_back(
        saved["queries"], saved["key_rows"], saved["value_rows"], grad_mixed, saved["logsum_one"]
    )
    grad_sq = rotate(grad_sq, cos_table, -sin_table)
    grad_sk = rotate(grad_sk, cos_table, -sin_table)
    grad_triple_rows = jnp.stack(
        [
            grad_sq.reshape(length, local_width),
            grad_sk.reshape(length, local_width),
            grad_sv.reshape(length, local_width),
        ],
        axis=1,
    ).astype(jnp.bfloat16)
    grad_triple = jnp.einsum(
        "sd,stf->dtf", saved["input_one"], grad_triple_rows, preferred_element_type=jnp.float32
    )
    grad_normed = norm_sum(
        jnp.einsum("stf,dtf->sd", grad_triple_rows, triple_w, preferred_element_type=jnp.float32)
    )
    back_rows, gain_one, shift_one = norm_backward(
        grad_normed, saved["hat_one"], saved["factor_one"], gain_all[0]
    )
    grad_tokens = grad_first + back_rows
    grad_gains = jnp.stack([gain_one, gain_two, gain_three], axis=0)
    grad_shifts = jnp.stack([shift_one, shift_two, shift_three], axis=0)
    weight_grads = (
        grad_triple,
        grad_attn_out,
        grad_cross_query,
        grad_cross_pair,
        grad_cross_out,
        grad_gate_up,
        grad_down,
        grad_gains,
        grad_shifts,
    )
    return (grad_tokens, grad_context, weight_grads)


def on_device(
    tokens,
    context,
    live_count,
    cotangent,
    triple_weight,
    attn_out_weight,
    cross_query_weight,
    cross_pair_weight,
    cross_out_weight,
    gate_up_weight,
    down_weight,
    norm_gains,
    norm_shifts,
):
    slot_count = tokens.shape[0]
    cos_table, sin_table = rotary_tables(tokens.shape[1])
    outputs = []
    saved_all = []
    for slot in range(slot_count):
        params = (
            lax.all_gather(triple_weight, "dp", axis=0, tiled=True),
            lax.all_gather(attn_out_weight, "dp", axis=1, tiled=True),
            lax.all_gather(cross_query_weight, "dp", axis=0, tiled=True),
            lax.all_gather(cross_pair_weight, "dp", axis=0, tiled=True),
            lax.all_gather(cross_out_weight, "dp", axis=1, tiled=True),
            lax.all_gather(gate_up_weight, "dp", axis=0, tiled=True),
            lax.all_gather(down_weight, "dp", axis=1, tiled=True),
            lax.all_gather(norm_gains, "dp", axis=1, tiled=True),
            lax.all_gather(norm_shifts, "dp", axis=1, tiled=True),
        )
        live_mask = (live_count[0] > slot).astype(jnp.float32)
        final, saved = forward_slot(params, tokens[slot], context[slot], cos_table, sin_table)
        outputs.append((final * live_mask).astype(jnp.bfloat16))
        saved_all.append(saved)
    grads_in = []
    grads_context = []
    totals = None
    for slot in range(slot_count):
        params = (
            lax.all_gather(triple_weight, "dp", axis=0, tiled=True),
            lax.all_gather(attn_out_weight, "dp", axis=1, tiled=True),
            lax.all_gather(cross_query_weight, "dp", axis=0, tiled=True),
            lax.all_gather(cross_pair_weight, "dp", axis=0, tiled=True),
            lax.all_gather(cross_out_weight, "dp", axis=1, tiled=True),
            lax.all_gather(gate_up_weight, "dp", axis=0, tiled=True),
            lax.all_gather(down_weight, "dp", axis=1, tiled=True),
            lax.all_gather(norm_gains, "dp", axis=1, tiled=True),
            lax.all_gather(norm_shifts, "dp", axis=1, tiled=True),
        )
        live_mask = (live_count[0] > slot).astype(jnp.float32)
        grad_out = cotangent[slot].astype(jnp.float32) * live_mask
        grad_tokens, grad_context, weight_grads = backward_slot(
            params, saved_all[slot], grad_out, context[slot], cos_table, sin_table
        )
        grads_in.append(grad_tokens)
        grads_context.append(grad_context)
        totals = weight_grads if totals is None else jax.tree.map(jnp.add, totals, weight_grads)
    (
        sum_triple,
        sum_attn_out,
        sum_cross_query,
        sum_cross_pair,
        sum_cross_out,
        sum_gate_up,
        sum_down,
        sum_gains,
        sum_shifts,
    ) = totals
    final_grads = (
        lax.psum_scatter(sum_triple, "dp", scatter_dimension=0, tiled=True),
        lax.psum_scatter(sum_attn_out, "dp", scatter_dimension=1, tiled=True),
        lax.psum_scatter(sum_cross_query, "dp", scatter_dimension=0, tiled=True),
        lax.psum_scatter(sum_cross_pair, "dp", scatter_dimension=0, tiled=True),
        lax.psum_scatter(sum_cross_out, "dp", scatter_dimension=1, tiled=True),
        lax.psum_scatter(sum_gate_up, "dp", scatter_dimension=0, tiled=True),
        lax.psum_scatter(sum_down, "dp", scatter_dimension=1, tiled=True),
        lax.psum_scatter(sum_gains, "dp", scatter_dimension=1, tiled=True),
        lax.psum_scatter(sum_shifts, "dp", scatter_dimension=1, tiled=True),
    )
    (
        grad_triple,
        grad_attn_out,
        grad_cross_query,
        grad_cross_pair,
        grad_cross_out,
        grad_gate_up,
        grad_down,
        grad_gains,
        grad_shifts,
    ) = final_grads
    return (
        jnp.stack(outputs, axis=0),
        jnp.stack(grads_in, axis=0),
        jnp.stack(grads_context, axis=0),
        grad_triple,
        grad_attn_out,
        grad_cross_query,
        grad_cross_pair,
        grad_cross_out,
        grad_gate_up,
        grad_down,
        grad_gains,
        grad_shifts,
    )


def solution(mesh):
    placed = (
        P("dp", None, None),
        P("dp", None, None),
        P("dp"),
        P("dp", None, None),
        P("dp", None, "tensor"),
        P("tensor", "dp"),
        P("dp", "tensor"),
        P("dp", None, "tensor"),
        P("tensor", "dp"),
        P("dp", None, "tensor"),
        P("tensor", "dp"),
        P(None, "dp"),
        P(None, "dp"),
    )
    return jax.shard_map(
        on_device,
        mesh=mesh,
        in_specs=placed,
        out_specs=(
            P("dp", None, None),
            P("dp", None, None),
            P("dp", None, None),
            P("dp", None, "tensor"),
            P("tensor", "dp"),
            P("dp", "tensor"),
            P("dp", None, "tensor"),
            P("tensor", "dp"),
            P("dp", None, "tensor"),
            P("tensor", "dp"),
            P(None, "dp"),
            P(None, "dp"),
        ),
        check_vma=False,
    )
```

profile of v0, /device:TPU:0, one launch (start us, length us, event | category | flops | bytes accessed | tf_op | source)
XLA Modules:
  0.0 2914.1 jit_solution(211931205918084677)
XLA Ops:
  12.7 42.6 %all-gather.1 = bf16[16,96,3]{1,2,0:T(4,128)(2,1)S(1)} all-gather(bf16[1,96,3]{1,2,0:T(4,128)(2,1)S(1)} %bitcast.481), channel_id=1, replica_groups=mesh['dp'=16,'tensor'=2] {'dp'}, dimensions={0}, use_global_device_ids=true | all-gather | bytes 9792 | tf_op jit(solution)/shard_map/all_gather | solution.py:333
  56.0 35.9 %all-gather = bf16[16,96,3]{1,2,0:T(4,128)(2,1)S(1)} all-gather(bf16[1,96,3]{1,2,0:T(4,128)(2,1)S(1)} %bitcast.482), channel_id=1, replica_groups=mesh['dp'=16,'tensor'=2] {'dp'}, dimensions={0}, use_global_device_ids=true | all-gather | bytes 9792 | tf_op jit(solution)/shard_map/all_gather | solution.py:332
  93.4 21.6 all-gather.10.cloned.1.call-done
  142.9 35.5 %all-gather.12.cloned.1.call-done = bf16[768,1536]{0,1:T(8,128)(2,1)} async-done(((bf16[768,96]{0,1:T(8,128)(2,1)}), bf16[768,1536]{0,1:T(8,128)(2,1)}) %all-gather.12.cloned.1.call-update) | async-done | bytes 2359312 | tf_op jit(solution)/shard_map/all_gather | solution.py:326
  187.8 55.1 %all-gather.14.cloned.1.call-done = bf16[768,2,768]{2,0,1:T(8,128)(2,1)} async-done(((bf16[48,2,768]{2,0,1:T(8,128)(2,1)}), bf16[768,2,768]{2,0,1:T(8,128)(2,1)}) %all-gather.14.cloned.1.call-update) | async-done | bytes 2359312 | tf_op jit(solution)/shard_map/all_gather | solution.py:328
  250.4 17.9 all-reduce.21.cloned.1.call-done
  273.7 61.1 %all-gather.16.cloned.1.call-done = bf16[1536,768]{1,0:T(8,128)(2,1)} async-done(((bf16[96,768]{1,0:T(8,128)(2,1)}), bf16[1536,768]{1,0:T(8,128)(2,1)}) %all-gather.16.cloned.1.call-update) | async-done | bytes 2359312 | tf_op jit(solution)/shard_map/all_gather | solution.py:327
  347.7 51.3 %all-gather.18.cloned.1.call-done = bf16[768,1536]{0,1:T(8,128)(2,1)} async-done(((bf16[768,96]{0,1:T(8,128)(2,1)}), bf16[768,1536]{0,1:T(8,128)(2,1)}) %all-gather.18.cloned.1.call-update) | async-done | bytes 2359312 | tf_op jit(solution)/shard_map/all_gather | solution.py:329
  409.3 17.8 all-reduce.19.cloned.1.call-done
  431.0 212.0 %all-gather.20.cloned.1.call-done = bf16[1536,2,3072]{2,0,1:T(8,128)(2,1)} async-done(((bf16[96,2,3072]{2,0,1:T(8,128)(2,1)}), bf16[1536,2,3072]{2,0,1:T(8,128)(2,1)}) %all-gather.20.cloned.1.call-update) | async-done | bytes 18874384 | tf_op jit(solution)/shard_map/all_gather | solution.py:330
  643.0 13.6 fusion.208
  664.2 102.3 %all-gather.22.cloned.1.call-done = bf16[3072,1536]{0,1:T(8,128)(2,1)} async-done(((bf16[3072,96]{0,1:T(8,128)(2,1)}), bf16[3072,1536]{0,1:T(8,128)(2,1)}) %all-gather.22.cloned.1.call-update) | async-done | bytes 9437200 | tf_op jit(solution)/shard_map/all_gather | solution.py:331
  766.5 10.8 fusion.115
  777.4 10.8 fusion.20
  788.2 9.6 fusion.114
  797.8 10.6 fusion.18
  808.5 9.9 fusion.101
  818.4 9.6 fusion.99
  833.4 20.8 all-reduce.17.cloned.1.call-done
  953.6 18.2 all-reduce.23.cloned.1.call-done
  992.9 17.1 fusion.42
  1010.0 28.7 convolution_add_fusion
  1069.1 12.3 fusion.104
  1081.4 17.4 convolution_add_fusion.1
  1110.1 117.6 %reduce-scatter.27.cloned.1.call-done = f32[96,3]{1,0:T(8,128)} async-done(((f32[1536,3]{1,0:T(8,128)}), f32[96,3]{1,0:T(8,128)}) %reduce-scatter.27.cloned.1.call-update) | async-done | bytes 1168
  1229.1 184.0 %all-reduce.15.cloned.1.call-done = f32[768,2,768]{2,1,0:T(2,128)} async-done(((f32[768,2,768]{2,1,0:T(2,128)}), f32[768,2,768]{2,1,0:T(2,128)}) %all-reduce.15.cloned.1.call-update) | async-done | bytes 4718608
  1414.8 546.7 %reduce-scatter.21.cloned.1.call-done = f32[96,2,3072]{2,0,1:T(8,128)} async-done(((f32[1536,2,3072]{2,0,1:T(8,128)}), f32[96,2,3072]{2,0,1:T(8,128)}) %reduce-scatter.21.cloned.1.call-update) | async-done | bytes 2359312 | tf_op jit(solution)/shard_map/reduce_scatter | solution.py:379
  1966.3 136.7 %reduce-scatter.17.cloned.1.call-done = f32[96,768]{1,0:T(8,128)} async-done(((f32[1536,768]{1,0:T(8,128)}), f32[96,768]{1,0:T(8,128)}) %reduce-scatter.17.cloned.1.call-update) | async-done | bytes 294928 | tf_op jit(solution)/shard_map/reduce_scatter | solution.py:376
  2103.0 143.1 %reduce-scatter.19.cloned.1.call-done = f32[768,96]{0,1:T(8,128)} async-done(((f32[768,1536]{0,1:T(8,128)}), f32[768,96]{0,1:T(8,128)}) %reduce-scatter.19.cloned.1.call-update) | async-done | bytes 294928 | tf_op jit(solution)/shard_map/reduce_scatter | solution.py:378
  2246.1 141.7 %reduce-scatter.15.cloned.1.call-done = f32[768,96]{0,1:T(8,128)} async-done(((f32[768,1536]{0,1:T(8,128)}), f32[768,96]{0,1:T(8,128)}) %reduce-scatter.15.cloned.1.call-update) | async-done | bytes 294928 | tf_op jit(solution)/shard_map/reduce_scatter | solution.py:375
  2387.8 227.6 %reduce-scatter.13.cloned.1.call-done = f32[96,3,768]{2,0,1:T(8,128)} async-done(((f32[1536,3,768]{2,0,1:T(8,128)}), f32[96,3,768]{2,0,1:T(8,128)}) %reduce-scatter.13.cloned.1.call-update) | async-done | bytes 884752 | tf_op jit(solution)/shard_map/reduce_scatter | solution.py:374
  2615.5 291.4 %reduce-scatter.23.cloned.1.call-done = f32[3072,96]{0,1:T(8,128)} async-done(((f32[3072,1536]{0,1:T(8,128)}), f32[3072,96]{0,1:T(8,128)}) %reduce-scatter.23.cloned.1.call-update) | async-done | bytes 1179664 | tf_op jit(solution)/shard_map/reduce_scatter | solution.py:380
  (669 shorter events, 264.2 us)
Async XLA Ops:
  7.2 107.8 %all-gather.10.cloned.1.call-start = ((), (), s32[]{:S(2)}) async-start(), calls=%async_computation.8 | async-start | bytes 7520256 | tf_op jit(solution)/shard_map/all_gather | solution.py:325
  7.9 170.5 %all-gather.12.cloned.1.call-start = ((), (), s32[]{:S(2)}) async-start(), calls=%async_computation.9 | async-start | bytes 2506752 | tf_op jit(solution)/shard_map/all_gather | solution.py:326
  8.7 234.2 %all-gather.14.cloned.1.call-start = ((), (), s32[]{:S(2)}) async-start(), calls=%async_computation.10 | async-start | bytes 2506752 | tf_op jit(solution)/shard_map/all_gather | solution.py:328
  10.3 258.0 %all-reduce.21.cloned.1.call-start = ((), (), s32[]{:S(2)}) async-start(), calls=%async_computation.26 | async-start | bytes 6291456 | tf_op jit(solution)/shard_map/psum | solution.py:88
  12.1 114.2 %copy-start.187 = (f32[256]{0:T(256)}, f32[256]{0:T(256)S(1)}, u32[]{:S(2)}) copy-start(f32[256]{0:T(256)S(1)} %broadcast_multiply_fusion.17) | copy-start | bytes 3076
  12.1 108.1 %copy-start.183 = (f32[256]{0:T(256)}, f32[256]{0:T(256)S(1)}, u32[]{:S(2)}) copy-start(f32[256]{0:T(256)S(1)} %broadcast_multiply_fusion.14) | copy-start | bytes 3076
  12.7 107.5 %copy-start.195 = (f32[256]{0:T(256)}, f32[256]{0:T(256)S(1)}, u32[]{:S(2)}) copy-start(f32[256]{0:T(256)S(1)} %add_rsqrt_fusion.2) | copy-start | bytes 3076
  185.8 149.1 %all-gather.16.cloned.1.call-start = ((), (), s32[]{:S(2)}) async-start(), calls=%async_computation.11 | async-start | bytes 2506752 | tf_op jit(solution)/shard_map/all_gather | solution.py:327
  186.4 212.7 %all-gather.18.cloned.1.call-start = ((), (), s32[]{:S(2)}) async-start(), calls=%async_computation.12 | async-start | bytes 2506752 | tf_op jit(solution)/shard_map/all_gather | solution.py:329
  186.9 240.1 %all-reduce.19.cloned.1.call-start = ((), (), s32[]{:S(2)}) async-start(), calls=%async_computation.25 | async-start | bytes 6291456 | tf_op jit(solution)/shard_map/psum | solution.py:88
  250.4 94.5 %copy-start.49 = (bf16[130,1,768]{0,2,1:T(8,128)(2,1)}, bf16[130,1,768]{0,2,1:T(8,128)(2,1)S(1)}, u32[]{:S(2)}) copy-start(bf16[130,1,768]{0,2,1:T(8,128)(2,1)S(1)} %copy.260) | copy-start | bytes 599044
  404.8 238.2 %all-gather.20.cloned.1.call-start = ((), (), s32[]{:S(2)}) async-start(), calls=%async_computation.13 | async-start | bytes 20054016 | tf_op jit(solution)/shard_map/all_gather | solution.py:330
  407.4 359.2 %all-gather.22.cloned.1.call-start = ((), (), s32[]{:S(2)}) async-start(), calls=%async_computation.14 | async-start | bytes 10027008 | tf_op jit(solution)/shard_map/all_gather | solution.py:331
  408.1 422.0 %all-reduce.27.cloned.1.call-start = ((), (), s32[]{:S(2)}) async-start(), calls=%async_computation.29 | async-start | bytes 3145728 | tf_op jit(solution)/shard_map/psum | solution.py:92
  430.3 424.0 %copy-start.6 = (f32[256,1536]{1,0:T(8,128)}, f32[256,1536]{1,0:T(8,128)S(1)}, u32[]{:S(2)}) copy-start(f32[256,1536]{1,0:T(8,128)S(1)} %get-tuple-element.193) | copy-start | bytes 4718596
  430.3 424.0 %copy-start.8 = (f32[256,1536]{1,0:T(8,128)}, f32[256,1536]{1,0:T(8,128)S(1)}, u32[]{:S(2)}) copy-start(f32[256,1536]{1,0:T(8,128)S(1)} %get-tuple-element.111) | copy-start | bytes 4718596
  430.3 423.9 %copy-start.156 = (f32[256]{0:T(256)}, f32[256]{0:T(256)S(1)}, u32[]{:S(2)}) copy-start(f32[256]{0:T(256)S(1)} %broadcast_multiply_fusion.12) | copy-start | bytes 3076
  430.7 423.6 %copy-start.158 = (f32[256]{0:T(256)}, f32[256]{0:T(256)S(1)}, u32[]{:S(2)}) copy-start(f32[256]{0:T(256)S(1)} %broadcast_multiply_fusion.15) | copy-start | bytes 3076
  431.0 423.3 %copy-start.165 = (f32[256]{0:T(256)}, f32[256]{0:T(256)S(1)}, u32[]{:S(2)}) copy-start(f32[256]{0:T(256)S(1)} %add_rsqrt_fusion) | copy-start | bytes 3076
  431.0 423.3 %copy-start.173 = (f32[256]{0:T(256)}, f32[256]{0:T(256)S(1)}, u32[]{:S(2)}) copy-start(f32[256]{0:T(256)S(1)} %add_rsqrt_fusion.3) | copy-start | bytes 3076
  808.5 45.8 %all-reduce.17.cloned.1.call-start = ((), (), s32[]{:S(2)}) async-start(), calls=%async_computation.24 | async-start | bytes 6291456 | tf_op jit(solution)/shard_map/psum | solution.py:88
  828.1 70.1 %all-reduce.25.cloned.1.call-start = ((), (), s32[]{:S(2)}) async-start(), calls=%async_computation.28 | async-start | bytes 3145728 | tf_op jit(solution)/shard_map/psum | solution.py:250
  876.4 95.4 %all-reduce.23.cloned.1.call-start = ((), (), s32[]{:S(2)}) async-start(), calls=%async_computation.27 | async-start | bytes 3981312 | tf_op jit(solution)/shard_map/psum | solution.py:92
  949.3 159.4 %reduce-scatter.25.cloned.1.call-start = ((), (), s32[]{:S(2)}) async-start(), calls=%async_computation.21 | async-start | bytes 835584
  976.5 251.1 %reduce-scatter.27.cloned.1.call-start = ((), (), s32[]{:S(2)}) async-start(), calls=%async_computation.22 | async-start | bytes 835584
  977.8 435.2 %all-reduce.15.cloned.1.call-start = ((), (), s32[]{:S(2)}) async-start(), calls=%async_computation.23 | async-start | bytes 9437184
  991.5 969.9 %reduce-scatter.21.cloned.1.call-start = ((), (), s32[]{:S(2)}) async-start(), calls=%async_computation.19 | async-start | bytes 40108032 | tf_op jit(solution)/shard_map/reduce_scatter | solution.py:379
  1038.7 1064.3 %reduce-scatter.17.cloned.1.call-start = ((), (), s32[]{:S(2)}) async-start(), calls=%async_computation.17 | async-start | bytes 5013504 | tf_op jit(solution)/shard_map/reduce_scatter | solution.py:376
  1045.4 1200.7 %reduce-scatter.19.cloned.1.call-start = ((), (), s32[]{:S(2)}) async-start(), calls=%async_computation.18 | async-start | bytes 5013504 | tf_op jit(solution)/shard_map/reduce_scatter | solution.py:378
  1051.0 1336.8 %reduce-scatter.15.cloned.1.call-start = ((), (), s32[]{:S(2)}) async-start(), calls=%async_computation.16 | async-start | bytes 5013504 | tf_op jit(solution)/shard_map/reduce_scatter | solution.py:375
  1056.6 1558.9 %reduce-scatter.13.cloned.1.call-start = ((), (), s32[]{:S(2)}) async-start(), calls=%async_computation.15 | async-start | bytes 15040512 | tf_op jit(solution)/shard_map/reduce_scatter | solution.py:374
  1069.0 1837.9 %reduce-scatter.23.cloned.1.call-start = ((), (), s32[]{:S(2)}) async-start(), calls=%async_computation.20 | async-start | bytes 20054016 | tf_op jit(solution)/shard_map/reduce_scatter | solution.py:380
  (206 other events, 1258.5 us)
Sparse Core Ops, SparseCore 0:
  10.7 104.2 all-gather.9
  117.8 60.5 all-gather.11
  181.6 61.1 all-gather.13
  246.2 22.0 all-reduce.20
  271.3 63.4 all-gather.15
  337.9 61.1 all-gather.17
  405.0 22.0 all-reduce.18
  430.3 212.6 all-gather.19
  645.8 120.6 all-gather.21
  808.6 18.6 all-reduce.26
  829.8 24.4 all-reduce.16
  876.5 21.6 all-reduce.24
  949.4 22.3 all-reduce.22
  977.1 123.6 reduce-scatter.24
  1106.0 121.5 reduce-scatter.26
  1234.2 178.8 all-reduce.14
  1418.9 542.4 reduce-scatter.20
  1967.0 135.9 reduce-scatter.16
  2109.6 136.4 reduce-scatter.18
  2251.7 136.0 reduce-scatter.14
  2395.2 220.2 reduce-scatter.12
  2621.8 284.9 reduce-scatter.22
where the time goes:
time: 2930 us; the launch traced here: 2910 us
  waiting for transfers between devices  2410 us (82%)
  matrix products  275 us (9%)
  local copies, waits for them, and re-layouts  82.5 us (3%)
  blocking collectives  78.5 us (3%)
  other arithmetic  47 us (2%)
    reduce_scatter x1, waiting for transfers between devices, on_device(): lax.psum_scatter(sum_gate_up, 'dp', scatter_dimension=0, tiled=True)  547 us
    unnamed x25, waiting for transfers between devices  305 us
    reduce_scatter x1, waiting for transfers between devices, on_device(): lax.psum_scatter(sum_down, 'dp', scatter_dimension=1, tiled=True)  291 us
    reduce_scatter x1, waiting for transfers between devices, on_device(): lax.psum_scatter(sum_triple, 'dp', scatter_dimension=0, tiled=True)  228 us
    all_gather x1, waiting for transfers between devices, on_device(): lax.all_gather(gate_up_weight, 'dp', axis=0, tiled=True)  212 us
    reduce_scatter x1, waiting for transfers between devices, on_device(): lax.psum_scatter(sum_cross_out, 'dp', scatter_dimension=1, tiled=True)  143 us
    reduce_scatter x1, waiting for transfers between devices, on_device(): lax.psum_scatter(sum_attn_out, 'dp', scatter_dimension=1, tiled=True)  142 us
    reduce_scatter x1, waiting for transfers between devices, on_device(): lax.psum_scatter(sum_cross_query, 'dp', scatter_dimension=0, tiled=True)  137 us
  transfers between devices with their start and end apart: 22, of which 20 were waited for; matrix products, arithmetic and copies ran while one was open for 9% of the time, Pallas kernels for 0%

commit v1 on v0

v1 whole, which is shorter than its diff:
```python
import jax
import jax.numpy as jnp
import numpy as np
from jax import lax
from jax.sharding import Mesh
from jax.sharding import PartitionSpec as P

HD = 64
ROT = 32
EPSILON = 1e-05
F32 = jnp.float32
BF16 = jnp.bfloat16
DP = ("A", "B", "C")
T = "T"
FLIP = [(0, 1), (1, 0)]


def swap(value, axis):
    return lax.ppermute(value, axis, FLIP)


def dot(left, right, dims):
    return lax.dot_general(left, right, (dims, ((), ())), preferred_element_type=F32)


def nn(left, right):
    return dot(left, right, ((1,), (0,)))


def nt(left, right):
    return dot(left, right, ((1,), (1,)))


def tn(left, right):
    return dot(left, right, ((0,), (0,)))


def pick(flag, when_zero, when_one):
    return jnp.where(flag == 0, when_zero, when_one)


def to_rel(values, outer, b, c):
    lead = values.shape[:-1]
    n = len(lead)
    v = values.reshape(lead + (outer, 2, 2, -1))
    v = pick(b, v, jnp.flip(v, n + 1))
    v = pick(c, v, jnp.flip(v, n + 2))
    v = jnp.transpose(v, tuple(range(n)) + (n + 2, n + 1, n, n + 3))
    return v.reshape(values.shape)


def from_rel(values, outer, b, c):
    lead = values.shape[:-1]
    n = len(lead)
    v = values.reshape(lead + (2, 2, outer, -1))
    v = jnp.transpose(v, tuple(range(n)) + (n + 2, n + 1, n, n + 3))
    v = pick(b, v, jnp.flip(v, n + 1))
    v = pick(c, v, jnp.flip(v, n + 2))
    return v.reshape(values.shape)


def flip_half(values):
    half = values.shape[-1] // 2
    return jnp.concatenate([values[..., half:], values[..., :half]], axis=-1)


def gather_z(shard):
    return lax.all_gather(shard, "A", axis=0, tiled=True)


def scatter_z(rows):
    return lax.psum_scatter(rows, "A", scatter_dimension=0, tiled=True)


def gather_full(first):
    over_c = swap(first, "C")
    over_b = swap(first, "B")
    both = swap(over_b, "C")
    return jnp.concatenate([first, over_b, over_c, both], axis=0)


def gather_half(first):
    over_b = swap(first, "B")
    n = first.shape[1] // 2
    return jnp.concatenate([first[:, :n], over_b[:, :n], first[:, n:], over_b[:, n:]], axis=0)


def scatter_full(left, right):
    rows = left.shape[1]
    sent = swap(tn(left[:, rows // 2 :], right).astype(BF16), "C")
    q = rows // 4
    far = tn(left[:, q : 2 * q], right) + sent[q:].astype(F32)
    far = swap(far.astype(BF16), "B")
    near = tn(left[:, :q], right) + sent[:q].astype(F32) + far.astype(F32)
    return scatter_z(near.astype(BF16))


def scatter_half(left, right):
    rows = left.shape[1]
    q = rows // 4
    far = jnp.concatenate(
        [tn(left[:, q : 2 * q], right).astype(BF16), tn(left[:, 3 * q :], right).astype(BF16)],
        axis=1,
    )
    far = swap(far, "B")
    n = right.shape[1]
    near = jnp.concatenate(
        [
            (tn(left[:, :q], right) + far[:, :n].astype(F32)).astype(BF16),
            (tn(left[:, 2 * q : 3 * q], right) + far[:, n:].astype(F32)).astype(BF16),
        ],
        axis=1,
    )
    return scatter_z(near)


def norm_forward(values, gain_row, shift_row):
    average = jnp.mean(values, axis=-1, keepdims=True)
    centred = values - average
    spread = jnp.mean(centred * centred, axis=-1, keepdims=True)
    factor = lax.rsqrt(spread + EPSILON)
    normed = centred * factor
    return ((normed * gain_row + shift_row).astype(BF16), normed, factor)


def norm_backward(grad_rows, normed, factor, gain_row):
    scaled = grad_rows * gain_row
    first_mean = jnp.mean(scaled, axis=-1, keepdims=True)
    second_mean = jnp.mean(scaled * normed, axis=-1, keepdims=True)
    grad_values = factor * (scaled - first_mean - normed * second_mean)
    return (grad_values, jnp.sum(grad_rows * normed, axis=0), jnp.sum(grad_rows, axis=0))


def rotary_tables(length):
    half_dim = ROT // 2
    freqs = 10000.0 ** (-(2.0 * np.arange(half_dim, dtype=np.float32) / ROT))
    angles = np.arange(length, dtype=np.float32)[:, None] * freqs[None, :].astype(np.float32)
    return (
        jnp.asarray(np.cos(angles))[None, :, None, :],
        jnp.asarray(np.sin(angles))[None, :, None, :],
    )


def rotate(values, cos_table, sin_table):
    half_dim = ROT // 2
    former = values[..., :half_dim]
    latter = values[..., half_dim:ROT]
    rest = values[..., ROT:]
    return jnp.concatenate(
        [former * cos_table - latter * sin_table, latter * cos_table + former * sin_table, rest],
        axis=-1,
    )


def attend(q, k, v):
    scores = jnp.einsum("lqhd,lkhd->lhqk", q, k, preferred_element_type=F32) * HD ** (-0.5)
    row_max = jnp.max(scores, axis=-1, keepdims=True)
    exponent = jnp.exp(scores - row_max)
    row_sum = jnp.sum(exponent, axis=-1, keepdims=True)
    prob = (exponent / row_sum).astype(BF16)
    mixed = jnp.einsum("lhqk,lkhd->lqhd", prob, v, preferred_element_type=F32)
    return (mixed.astype(BF16), row_max + jnp.log(row_sum))


def attend_back(q, k, v, grad, logsum):
    scale = HD ** (-0.5)
    scores = jnp.einsum("lqhd,lkhd->lhqk", q, k, preferred_element_type=F32) * scale
    prob = jnp.exp(scores - logsum)
    grad_prob = jnp.einsum("lqhd,lkhd->lhqk", grad, v, preferred_element_type=F32)
    centre = jnp.sum(prob * grad_prob, axis=-1, keepdims=True)
    grad_scores = (prob * (grad_prob - centre)).astype(BF16)
    grad_q = jnp.einsum("lhqk,lkhd->lqhd", grad_scores, k, preferred_element_type=F32) * scale
    grad_k = jnp.einsum("lhqk,lqhd->lkhd", grad_scores, q, preferred_element_type=F32) * scale
    grad_v = jnp.einsum(
        "lhqk,lqhd->lkhd", prob.astype(BF16), grad, preferred_element_type=F32
    )
    return (grad_q, grad_k, grad_v)


def pair_sum(part):
    mine = lax.optimization_barrier(part.astype(BF16))
    return mine.astype(F32) + swap(mine, T).astype(F32)


def on_device(
    tokens,
    context,
    live_count,
    cotangent,
    triple_weight,
    attn_out_weight,
    cross_query_weight,
    cross_pair_weight,
    cross_out_weight,
    gate_up_weight,
    down_weight,
    norm_gains,
    norm_shifts,
):
    b = lax.axis_index("B")
    c = lax.axis_index("C")
    t = lax.axis_index(T)
    outer = lax.axis_size("A")
    slots, length, width = tokens.shape
    rows = slots * length
    half = rows // 2
    cond = context.shape[1]
    block = triple_weight.shape[0]
    local = triple_weight.shape[2]
    heads = local // HD
    units = gate_up_weight.shape[2]
    part_units = units // 2
    q_rows = width // 4

    def halves(w):
        k = w.shape[1]
        w = w.reshape(block, k, 2, part_units)
        own = pick(c, w[:, :, 0], w[:, :, 1]).reshape(block, k * part_units)
        other = pick(c, w[:, :, 1], w[:, :, 0]).reshape(block, k * part_units)
        return (own, other)

    gu_own, gu_other = halves(gate_up_weight)
    down_own, down_other = halves(down_weight.T.reshape(block, 1, units))
    norm_cols = jnp.concatenate([norm_gains, norm_shifts], axis=0).T
    norm_cols = jnp.pad(norm_cols, ((0, 0), (0, 128 - norm_cols.shape[1])))
    pack_one = jnp.concatenate(
        [triple_weight.reshape(block, 3 * local), attn_out_weight.T, norm_cols], axis=1
    )
    pack_two = jnp.concatenate(
        [
            jnp.concatenate([cross_query_weight, cross_out_weight.T], axis=1),
            cross_pair_weight.reshape(cross_pair_weight.shape[0], 2 * local),
        ],
        axis=0,
    )
    down_in = jnp.concatenate([down_own, swap(down_other, "C")], axis=1)
    gu_in = jnp.concatenate([gu_own, swap(gu_other, "C")], axis=1)
    z_one = gather_z(pack_one)
    z_two = gather_z(pack_two)
    z_down = gather_z(down_in)
    z_gu = gather_z(gu_in)
    w_one = gather_full(z_one)
    z_two = z_two.reshape(outer, pack_two.shape[0], 2 * local)
    w_two = gather_full(z_two[:, :block].reshape(outer * block, 2 * local))
    w_pair = gather_full(z_two[:, block:].reshape(-1, 2 * local))
    w_down = gather_half(z_down)
    w_gu = gather_half(z_gu)
    w_triple = w_one[:, : 3 * local]
    w_attn = w_one[:, 3 * local : 4 * local]
    norms = w_one[:, 4 * local : 4 * local + 6].T.astype(F32)
    w_cq = w_two[:, :local]
    w_cross = w_two[:, local:]

    live = (live_count[0] > jnp.arange(slots)).astype(F32)
    live_rows = jnp.repeat(live, length)[:, None]
    start = to_rel(tokens.reshape(rows, width), outer, b, c).astype(F32)
    grad_top = to_rel(cotangent.reshape(rows, width), outer, b, c).astype(F32) * live_rows
    ctx = to_rel(context.reshape(slots * cond, -1), outer, b, c)

    def by_core(value):
        return (
            pick(t, value[:half], value[half:]),
            pick(t, value[half:], value[:half]),
        )

    def from_core(mine, other):
        return jnp.concatenate([pick(t, mine, other), pick(t, other, mine)], axis=0)

    def spread(value):
        mine, other = by_core(value)
        far = flip_half(swap(mine, "C"))
        return jnp.concatenate([mine, other, far, swap(far, T)], axis=0)

    def collect(part):
        part = part.astype(BF16)
        send = jnp.concatenate([part[half : 2 * half], part[3 * half :]], axis=0)
        got = swap(send, T).astype(F32)
        near = part[:half].astype(F32) + got[:half]
        far = part[2 * half : 3 * half].astype(F32) + got[half:]
        return near + swap(flip_half(far.astype(BF16)), "C").astype(F32)

    grad_all = spread(grad_top.astype(BF16))

    cos_table, sin_table = rotary_tables(length)
    n1, hat_one, factor_one = norm_forward(start, norms[0], norms[3])
    raw = nn(n1, w_triple).reshape(slots, length, 3, heads, HD)
    q = rotate(raw[:, :, 0], cos_table, sin_table).astype(BF16)
    k = rotate(raw[:, :, 1], cos_table, sin_table).astype(BF16)
    v = raw[:, :, 2].astype(BF16)
    o1, logsum_one = attend(q, k, v)
    o1 = o1.reshape(rows, local)
    h1 = start + pair_sum(nt(o1, w_attn))
    n2, hat_two, factor_two = norm_forward(h1, norms[1], norms[4])
    cq = nn(n2, w_cq).astype(BF16).reshape(slots, length, heads, HD)
    pair = nn(ctx, w_pair).astype(BF16).reshape(slots, cond, 2, heads, HD)
    ck, cv = pair[:, :, 0], pair[:, :, 1]
    o2, logsum_two = attend(cq, ck, cv)
    o2 = o2.reshape(rows, local)
    h2 = h1 + pair_sum(nt(o2, w_cross))
    n3, hat_three, factor_three = norm_forward(h2, norms[2], norms[5])
    n3_all = spread(n3)
    gate = nn(n3_all, w_gu[:, :part_units])
    upper = nn(n3_all, w_gu[:, part_units:])
    sig = jax.nn.sigmoid(gate)
    silu = gate * sig
    hidden = (silu * upper).astype(BF16)

    g_down = scatter_half(grad_all, hidden)
    dhid = nn(grad_all, w_down)
    dgu = jnp.concatenate(
        [
            (dhid * upper * (sig * (1.0 + gate * (1.0 - sig)))).astype(BF16),
            (dhid * silu).astype(BF16),
        ],
        axis=1,
    )
    g_gu = scatter_half(n3_all, dgu)
    dn3 = collect(nt(dgu, w_gu)).astype(BF16)
    dn3 = lax.optimization_barrier(dn3)
    dn3 = from_core(dn3, swap(dn3, T)).astype(F32)
    back, gain_three, shift_three = norm_backward(dn3, hat_three, factor_three, norms[2])
    dh2 = grad_top + back

    out_half = collect(nt(hidden, w_down)) + by_core(h2)[0]
    out_half = (out_half * pick(t, live_rows[:half], live_rows[half:])).astype(BF16)
    out_half = lax.optimization_barrier(out_half)
    mixed = from_core(out_half, swap(out_half, T))

    dc = dh2.astype(BF16)
    g_cross = scatter_full(dc, o2)
    grad_o = nn(dc, w_cross).astype(BF16).reshape(slots, length, heads, HD)
    dcq, dck, dcv = attend_back(cq, ck, cv, grad_o, logsum_two)
    dcq = dcq.astype(BF16).reshape(rows, local)
    dpair = jnp.concatenate(
        [
            dck.astype(BF16).reshape(slots * cond, local),
            dcv.astype(BF16).reshape(slots * cond, local),
        ],
        axis=1,
    )
    g_cq = scatter_full(n2, dcq)
    g_pair = scatter_full(ctx, dpair)
    dn2 = pair_sum(nt(dcq, w_cq))
    dctx = pair_sum(nt(dpair, w_pair))
    back, gain_two, shift_two = norm_backward(dn2, hat_two, factor_two, norms[1])
    dh1 = dh2 + back

    da = dh1.astype(BF16)
    g_attn = scatter_full(da, o1)
    grad_o = nn(da, w_attn).astype(BF16).reshape(slots, length, heads, HD)
    dq, dk, dv = attend_back(q, k, v, grad_o, logsum_one)
    draw = jnp.concatenate(
        [
            rotate(dq, cos_table, -sin_table).astype(BF16).reshape(rows, local),
            rotate(dk, cos_table, -sin_table).astype(BF16).reshape(rows, local),
            dv.astype(BF16).reshape(rows, local),
        ],
        axis=1,
    )
    g_triple = scatter_full(n1, draw)
    dn1 = pair_sum(nt(draw, w_triple))
    back, gain_one, shift_one = norm_backward(dn1, hat_one, factor_one, norms[0])
    dtok = dh1 + back

    g_norm = jnp.stack([gain_one, gain_two, gain_three, shift_one, shift_two, shift_three], axis=1)
    g_norm = jnp.pad(g_norm, ((0, 0), (0, 128 - g_norm.shape[1])))
    sent = swap(g_norm[2 * q_rows :], "C")
    g_norm = g_norm[: 2 * q_rows] + sent
    sent = swap(g_norm[q_rows:], "B")
    g_norm = scatter_z(g_norm[:q_rows] + sent)

    def units_back(g, k):
        n = g.shape[1] // 2
        far = swap(g[:, n:], "C").reshape(block, k, part_units)
        own = g[:, :n].reshape(block, k, part_units)
        return jnp.concatenate([pick(c, own, far), pick(c, far, own)], axis=2).astype(F32)

    grad_gate_up = units_back(g_gu, 2)
    grad_down = units_back(g_down, 1).reshape(block, units).T

    return (
        from_rel(mixed, outer, b, c).reshape(tokens.shape),
        from_rel(dtok, outer, b, c).reshape(tokens.shape),
        from_rel(dctx, outer, b, c).reshape(context.shape),
        g_triple.astype(F32).reshape(block, 3, local),
        g_attn.astype(F32).T,
        g_cq.astype(F32),
        g_pair.astype(F32).reshape(-1, 2, local),
        g_cross.astype(F32).T,
        grad_gate_up,
        grad_down,
        g_norm[:, :3].T,
        g_norm[:, 3:6].T,
    )


def solution(mesh):
    dp, tensor = mesh.devices.shape
    inner = Mesh(mesh.devices.reshape(dp // 4, 2, 2, tensor), DP + (T,))
    rows_dp = P(DP, None, None)
    placed = (
        rows_dp,
        rows_dp,
        P(DP),
        rows_dp,
        P(DP, None, T),
        P(T, DP),
        P(DP, T),
        P(DP, None, T),
        P(T, DP),
        P(DP, None, T),
        P(T, DP),
        P(None, DP),
        P(None, DP),
    )
    return jax.shard_map(
        on_device,
        mesh=inner,
        in_specs=placed,
        out_specs=(
            rows_dp,
            rows_dp,
            rows_dp,
            P(DP, None, T),
            P(T, DP),
            P(DP, T),
            P(DP, None, T),
            P(T, DP),
            P(DP, None, T),
            P(T, DP),
            P(None, DP),
            P(None, DP),
        ),
        check_vma=False,
    )
```

time: 2930 us -> 1090 us (0.37)
  waiting for transfers between devices: 2410 us -> 509 us
  local copies, waits for them, and re-layouts: 82.5 us -> 182 us
  other arithmetic: 47 us -> 133 us
  blocking collectives: 78.5 us -> 0 us
  matrix products: 275 us -> 201 us
  starting transfers between devices: 2.45 us -> 39.3 us
    reduce_scatter x6 -> x7, waiting for transfers between devices: 1490 us -> 15.2 us  [scatter_z(): return lax.psum_scatter(rows, 'A', scatter_dimension=0, tiled=True)]
    all_gather x7 -> x4, waiting for transfers between devices: 539 us -> 37.7 us  [gather_z(): return lax.all_gather(shard, 'A', axis=0, tiled=True)]
    ppermute x0 -> x44, waiting for transfers between devices: none -> 456 us  [swap(): return lax.ppermute(value, axis, FLIP)]
    unnamed x25 -> x13, waiting for transfers between devices: 305 us -> 0.2 us
    psum x6 -> x0, waiting for transfers between devices: 78.7 us -> none  [the longest x3 56.6 us: head_sum(): return lax.psum(partial_rows, 'tensor')]
    all_gather x2 -> x0, blocking collectives: 78.5 us -> none  [the longest x1 42.6 us: on_device(): lax.all_gather(norm_shifts, 'dp', axis=1, tiled=True)]
    dot_general x66 -> x50, matrix products: 275 us -> 201 us  [the longest x38 163 us: dot(): lax.dot_general(left, right, (dims, ((), ())), preferred_element_type=F32)]
    convert_element_type x6 -> x25, other arithmetic: 2.38 us -> 45.5 us  [the longest x5 12.4 us: scatter_full(): return scatter_z(near.astype(BF16))]
  transfers between devices with their start and end apart: 22 -> 56, of which waited for: 20 -> 23; matrix products, arithmetic and copies ran while one was open for 9% -> 37% of each run, Pallas kernels for 0% -> 0%
where the time goes in v1:
time: 1090 us; the launch traced here: 1080 us
  waiting for transfers between devices  509 us (47%)
  matrix products  201 us (18%)
  local copies, waits for them, and re-layouts  182 us (17%)
  other arithmetic  133 us (12%)
  starting transfers between devices  39.3 us (4%)
  between operations  19.4 us (2%)
    ppermute x44, waiting for transfers between devices, swap(): return lax.ppermute(value, axis, FLIP)  456 us
    dot_general x38, matrix products, dot(): lax.dot_general(left, right, (dims, ((), ())), preferred_element_type=F32)  163 us
    unnamed x354, local copies, waits for them, and re-layouts  64.1 us
    ppermute x44, starting transfers between devices, swap(): return lax.ppermute(value, axis, FLIP)  38.1 us
    all_gather x4, waiting for transfers between devices, gather_z(): return lax.all_gather(shard, 'A', axis=0, tiled=True)  37.7 us
  transfers between devices with their start and end apart: 56, of which 23 were waited for; matrix products, arithmetic and copies ran while one was open for 37% of the time, Pallas kernels for 0%

profile of v1, /device:TPU:0, one launch (start us, length us, event | category | flops | bytes accessed | tf_op | source)
XLA Modules:
  0.0 1083.8 jit_solution(6457147799115434359)
XLA Ops:
  57.3 8.7 all-gather.5.cloned.1.call-done
  77.7 29.0 %all-gather.7.cloned.1.call-done = bf16[576,1536]{1,0:T(8,128)(2,1)} async-done(((bf16[144,1536]{1,0:T(8,128)(2,1)}), bf16[576,1536]{1,0:T(8,128)(2,1)}) %all-gather.7.cloned.1.call-update) | async-done | bytes 1769488 | tf_op jit(solution)/shard_map/all_gather | solution.py:68
  115.8 18.2 %collective-permute-done.4 = bf16[192,1536]{1,0:T(8,128)(2,1)} collective-permute-done((bf16[192,1536]{1,0:T(8,128)(2,1)}, bf16[192,1536]{1,0:T(8,128)(2,1)}, u32[]{:S(2)}, u32[]{:S(2)}) %collective-permute-start.4) | collective-permute-done | bytes 589856 | tf_op jit(solution)/shard_map/ppermute | solution.py:19
  142.5 36.8 %collective-permute-done.5 = bf16[192,1536]{1,0:T(8,128)(2,1)S(1)} collective-permute-done((bf16[192,1536]{1,0:T(8,128)(2,1)}, bf16[192,1536]{1,0:T(8,128)(2,1)S(1)}, u32[]{:S(2)}, u32[]{:S(2)}) %collective-permute-start.5) | collective-permute-done | bytes 589856 | tf_op jit(solution)/shard_map/ppermute | solution.py:19
  179.3 12.6 %collective-permute-done.6 = bf16[192,1536]{1,0:T(8,128)(2,1)S(1)} collective-permute-done((bf16[192,1536]{1,0:T(8,128)(2,1)}, bf16[192,1536]{1,0:T(8,128)(2,1)S(1)}, u32[]{:S(2)}, u32[]{:S(2)}) %collective-permute-start.6) | collective-permute-done | bytes 589856 | tf_op jit(solution)/shard_map/ppermute | solution.py:19
  215.9 28.8 %collective-permute-done.2 = bf16[384,3200]{1,0:T(8,128)(2,1)} collective-permute-done((bf16[384,3200]{1,0:T(8,128)(2,1)}, bf16[384,3200]{1,0:T(8,128)(2,1)}, u32[]{:S(2)}, u32[]{:S(2)}) %collective-permute-start.2) | collective-permute-done | bytes 2457632 | tf_op jit(solution)/shard_map/ppermute | solution.py:19
  248.0 6.3 slice_bitcast_fusion
  266.4 10.4 copy.221
  276.8 6.7 fusion.64
  284.6 13.5 %multiply_reduce_fusion.1 = (f32[2,12,256]{2,1,0:T(8,128)S(1)}, f32[2,12,256,256]{2,3,1,0:T(8,128)S(1)}) fusion(bf16[2,256,12,32]{1,3,2,0:T(8,128)(2,1)S(1)} %slice.799, bf16[2,256,12,16]{1,3,2,0:T(8,128)(2,1)S(1)} %get-tuple-element.156, bf16[2,256,12,16]{1,3,2,0:T(8,128)(2,1)S(1)} %get-tuple-element.157, bf16[2,256,12,32]{1,3,2,0:T(8,128)(2,1)S(1)} %slice.800, ...), kind=kOutput, calls=%fused_computation.16 | convolution fusion | flops 209184768 | bytes 7888896 | tf_op jit(solution)/shard_map/lqhd,lkhd->lhqk/dot_general | solution.py:156
  336.7 9.3 fusion.94
  353.1 68.9 %collective-permute-done.14 = bf16[384,6144]{1,0:T(8,128)(2,1)} collective-permute-done((bf16[384,6144]{1,0:T(8,128)(2,1)}, bf16[384,6144]{1,0:T(8,128)(2,1)}, u32[]{:S(2)}, u32[]{:S(2)}) %collective-permute-start.14) | collective-permute-done | bytes 4718624 | tf_op jit(solution)/shard_map/ppermute | solution.py:19
  430.7 11.0 %fusion.4 = f32[1024,1536]{1,0:T(8,128)} fusion(bf16[1536,3072]{1,0:T(8,128)(2,1)S(1)} %pad_maximum_fusion, bf16[256,1536]{1,0:T(8,128)(2,1)S(1)} %collective-permute-done.12, bf16[256,768]{1,0:T(8,128)(2,1)S(1)} %get-tuple-element.149, bf16[256,768]{1,0:T(8,128)(2,1)S(1)} %get-tuple-element.148, bf16[256,1536]{1,0:T(8,128)(2,1)S(1)} %get-tuple-element.136, ...), kind=kOutput, calls=%fused_computation.26 | convolution fusion | flops 4847566848 | bytes 14155776 | tf_op jit(solution)/shard_map/dot_general | solution.py:23
  441.7 18.0 %multiply_convert_fusion.2 = (bf16[1024,1536]{1,0:T(8,128)(2,1)}, bf16[1024,1536]{1,0:T(8,128)(2,1)}, bf16[1024,1536]{1,0:T(8,128)(2,1)}) fusion(f32[1024,1536]{1,0:T(8,128)} %fusion.94, f32[1024,1536]{1,0:T(8,128)} %fusion.4, bf16[1536,3072]{1,0:T(8,128)(2,1)} %copy-done.25, bf16[256,1536]{1,0:T(8,128)(2,1)S(1)} %collective-permute-done.12, ...), kind=kOutput, calls=%fused_computation.6 | convolution fusion | flops 4871159808 | bytes 29884416 | tf_op jit(solution)/shard_map/dot_general | solution.py:23
  459.8 16.4 %convolution_convert_fusion.3 = bf16[1024,1536]{1,0:T(8,128)(2,1)} fusion(bf16[1024,1536]{1,0:T(8,128)(2,1)} %get-tuple-element.99, bf16[1024,1536]{1,0:T(8,128)(2,1)} %get-tuple-element.98, bf16[384,3072]{1,0:T(8,128)(2,1)} %copy-done.24, bf16[384,3072]{1,0:T(8,128)(2,1)} %copy-done.22, bf16[384,3072]{1,0:T(8,128)(2,1)} %copy-done.23, ...), kind=kOutput, calls=%fused_computation.42 | convolution fusion | flops 9715580928 | bytes 18874368 | tf_op jit(solution)/shard_map/dot_general | solution.py:23
  483.4 6.8 pad_maximum_fusion.6
  500.6 12.8 %collective-permute-done.23 = bf16[256,1536]{1,0:T(8,128)(2,1)S(1)} collective-permute-done((bf16[256,1536]{1,0:T(8,128)(2,1)S(1)}, bf16[256,1536]{1,0:T(8,128)(2,1)S(1)}, u32[]{:S(2)}, u32[]{:S(2)}) %collective-permute-start.23) | collective-permute-done | bytes 786464 | tf_op jit(solution)/shard_map/ppermute | solution.py:19
  567.4 19.4 %collective-permute-done.34 = bf16[384,1536]{1,0:T(8,128)(2,1)S(1)} collective-permute-done((bf16[384,1536]{1,0:T(8,128)(2,1)S(1)}, bf16[384,1536]{1,0:T(8,128)(2,1)S(1)}, u32[]{:S(2)}, u32[]{:S(2)}) %collective-permute-start.34) | collective-permute-done | bytes 1179680 | tf_op jit(solution)/shard_map/ppermute | solution.py:19
  592.0 20.2 %collective-permute-done.32 = bf16[768,768]{1,0:T(8,128)(2,1)S(1)} collective-permute-done((bf16[768,768]{1,0:T(8,128)(2,1)S(1)}, bf16[768,768]{1,0:T(8,128)(2,1)S(1)}, u32[]{:S(2)}, u32[]{:S(2)}) %collective-permute-start.32) | collective-permute-done | bytes 1179680 | tf_op jit(solution)/shard_map/ppermute | solution.py:19
  614.0 19.8 %collective-permute-done.35 = bf16[192,1536]{1,0:T(8,128)(2,1)S(1)} collective-permute-done((bf16[192,1536]{1,0:T(8,128)(2,1)S(1)}, bf16[192,1536]{1,0:T(8,128)(2,1)S(1)}, u32[]{:S(2)}, u32[]{:S(2)}) %collective-permute-start.35) | collective-permute-done | bytes 589856 | tf_op jit(solution)/shard_map/ppermute | solution.py:19
  657.4 101.8 %collective-permute-done.37 = bf16[384,768]{1,0:T(8,128)(2,1)S(1)} collective-permute-done((bf16[384,768]{1,0:T(8,128)(2,1)S(1)}, bf16[384,768]{1,0:T(8,128)(2,1)S(1)}, u32[]{:S(2)}, u32[]{:S(2)}) %collective-permute-start.37) | collective-permute-done | bytes 589856 | tf_op jit(solution)/shard_map/ppermute | solution.py:19
  794.4 7.6 multiply_reduce_fusion
  817.3 7.3 convolution_convert_fusion.4
  833.3 8.3 add_convert_fusion.1
  844.2 5.6 add_convert_fusion
  864.3 6.0 convolution_convert_fusion
  871.0 10.9 %collective-permute-done.18 = bf16[256,1536]{1,0:T(8,128)(2,1)} collective-permute-done((bf16[256,1536]{1,0:T(8,128)(2,1)}, bf16[256,1536]{1,0:T(8,128)(2,1)}, u32[]{:S(2)}, u32[]{:S(2)}) %collective-permute-start.18) | collective-permute-done | bytes 786464 | tf_op jit(solution)/shard_map/ppermute | solution.py:19
  904.9 52.8 %collective-permute-done.28 = bf16[768,2304]{1,0:T(8,128)(2,1)} collective-permute-done((bf16[768,2304]{1,0:T(8,128)(2,1)}, bf16[768,2304]{1,0:T(8,128)(2,1)}, u32[]{:S(2)}, u32[]{:S(2)}) %collective-permute-start.28) | collective-permute-done | bytes 3538976 | tf_op jit(solution)/shard_map/ppermute | solution.py:19
  964.1 17.0 %collective-permute-done.30 = bf16[768,768]{1,0:T(8,128)(2,1)} collective-permute-done((bf16[768,768]{1,0:T(8,128)(2,1)}, bf16[768,768]{1,0:T(8,128)(2,1)}, u32[]{:S(2)}, u32[]{:S(2)}) %collective-permute-start.30) | collective-permute-done | bytes 1179680 | tf_op jit(solution)/shard_map/ppermute | solution.py:19
  994.1 18.0 %collective-permute-done.31 = bf16[384,768]{1,0:T(8,128)(2,1)S(1)} collective-permute-done((bf16[384,768]{1,0:T(8,128)(2,1)S(1)}, bf16[384,768]{1,0:T(8,128)(2,1)S(1)}, u32[]{:S(2)}, u32[]{:S(2)}) %collective-permute-start.31) | collective-permute-done | bytes 589856 | tf_op jit(solution)/shard_map/ppermute | solution.py:19
  1047.8 7.1 collective-permute-done.39
  1059.3 15.2 %reduce-scatter.11.cloned.1.call-done = bf16[96,2304]{1,0:T(8,128)(2,1)} async-done(((bf16[384,2304]{1,0:T(8,128)(2,1)}), bf16[96,2304]{1,0:T(8,128)(2,1)}) %reduce-scatter.11.cloned.1.call-update) | async-done | bytes 442384 | tf_op jit(solution)/shard_map/reduce_scatter | solution.py:72
  (686 shorter events, 433.3 us)
Async XLA Ops:
  7.2 58.8 %all-gather.5.cloned.1.call-start = ((), (), s32[]{:S(2)}) async-start(), calls=%async_computation.8 | async-start | bytes 3072000 | tf_op jit(solution)/shard_map/all_gather | solution.py:68
  11.0 95.7 %all-gather.7.cloned.1.call-start = ((), (), s32[]{:S(2)}) async-start(), calls=%async_computation.9 | async-start | bytes 2211840 | tf_op jit(solution)/shard_map/all_gather | solution.py:68
  12.9 199.1 %all-gather.11.cloned.1.call-start = ((), (), s32[]{:S(2)}) async-start(), calls=%async_computation.11 | async-start | bytes 2949120 | tf_op jit(solution)/shard_map/all_gather | solution.py:68
  20.6 91.0 %collective-permute-start.13 = (bf16[96,3072]{1,0:T(8,128)(2,1)}, bf16[96,3072]{1,0:T(8,128)(2,1)}, u32[]{:S(2)}, u32[]{:S(2)}) collective-permute-start(bf16[96,3072]{1,0:T(8,128)(2,1)} %bitcast.78), channel_id=1, source_target_pairs={{0,2},{2,0},{1,3},{3,1},{4,6},{6,4},{5,7},{7,5},{8,10},{10,8},{9,1... | collective-permute-start | bytes 1769480 | tf_op jit(solution)/shard_map/ppermute | solution.py:19
  45.4 272.4 %all-gather.9.cloned.1.call-start = ((), (), s32[]{:S(2)}) async-start(), calls=%async_computation.10 | async-start | bytes 5898240 | tf_op jit(solution)/shard_map/all_gather | solution.py:68
  49.8 64.0 %collective-permute-start.20 = (bf16[256,1536]{1,0:T(8,128)(2,1)}, bf16[256,1536]{1,0:T(8,128)(2,1)}, u32[]{:S(2)}, u32[]{:S(2)}) collective-permute-start(bf16[256,1536]{1,0:T(8,128)(2,1)} %get-tuple-element.133), channel_id=1, source_target_pairs={{0,2},{2,0},{1,3},{3,1},{4,6},{6,4},{5,7},{7,5},{8,10},{10,8},{9,1... | collective-permute-start | bytes 2359304 | tf_op jit(solution)/shard_map/ppermute | solution.py:19
  66.0 69.5 %collective-permute-start = (bf16[384,3200]{1,0:T(8,128)(2,1)}, bf16[384,3200]{1,0:T(8,128)(2,1)}, u32[]{:S(2)}, u32[]{:S(2)}) collective-permute-start(bf16[384,3200]{1,0:T(8,128)(2,1)} %all-gather.5.cloned.1.call-done), channel_id=1, source_target_pairs={{0,4},{4,0},{1,5},{5,1},{2,6},{6,2},{3,7},{7,3},{8,12},{12,8},{9,1... | collective-permute-start | bytes 7372808 | tf_op jit(solution)/shard_map/ppermute | solution.py:19
  110.1 101.8 %collective-permute-start.1 = (bf16[384,3200]{1,0:T(8,128)(2,1)}, bf16[384,3200]{1,0:T(8,128)(2,1)}, u32[]{:S(2)}, u32[]{:S(2)}) collective-permute-start(bf16[384,3200]{1,0:T(8,128)(2,1)} %all-gather.5.cloned.1.call-done), channel_id=1, source_target_pairs={{0,2},{2,0},{1,3},{3,1},{4,6},{6,4},{5,7},{7,5},{8,10},{10,8},{9,1... | collective-permute-start | bytes 7372808 | tf_op jit(solution)/shard_map/ppermute | solution.py:19
  113.8 870.4 %reduce-scatter.17.cloned.1.call-start = ((), (), s32[]{:S(2)}) async-start(), calls=%async_computation.15 | async-start | bytes 737280 | tf_op jit(solution)/shard_map/reduce_scatter | solution.py:72
  115.2 64.0 %collective-permute-start.5 = (bf16[192,1536]{1,0:T(8,128)(2,1)}, bf16[192,1536]{1,0:T(8,128)(2,1)S(1)}, u32[]{:S(2)}, u32[]{:S(2)}) collective-permute-start(bf16[192,1536]{1,0:T(8,128)(2,1)} %bitcast.18), channel_id=1, source_target_pairs={{0,2},{2,0},{1,3},{3,1},{4,6},{6,4},{5,7},{7,5},{8,10},{10,8},{9,1... | collective-permute-start | bytes 1769480 | tf_op jit(solution)/shard_map/ppermute | solution.py:19
  135.5 109.2 %collective-permute-start.2 = (bf16[384,3200]{1,0:T(8,128)(2,1)}, bf16[384,3200]{1,0:T(8,128)(2,1)}, u32[]{:S(2)}, u32[]{:S(2)}) collective-permute-start(bf16[384,3200]{1,0:T(8,128)(2,1)} %collective-permute-done), channel_id=1, source_target_pairs={{0,2},{2,0},{1,3},{3,1},{4,6},{6,4},{5,7},{7,5},{8,10},{10,8},{9,1... | collective-permute-start | bytes 7372808 | tf_op jit(solution)/shard_map/ppermute | solution.py:19
  139.4 68.4 %collective-permute-start.7 = (bf16[384,1536]{1,0:T(8,128)(2,1)}, bf16[384,1536]{1,0:T(8,128)(2,1)}, u32[]{:S(2)}, u32[]{:S(2)}) collective-permute-start(bf16[384,1536]{1,0:T(8,128)(2,1)} %bitcast.20), channel_id=1, source_target_pairs={{0,4},{4,0},{1,5},{5,1},{2,6},{6,2},{3,7},{7,3},{8,12},{12,8},{9,1... | collective-permute-start | bytes 3538952 | tf_op jit(solution)/shard_map/ppermute | solution.py:19
  179.2 156.3 %collective-permute-start.21 = (bf16[256,1536]{1,0:T(8,128)(2,1)}, bf16[256,1536]{1,0:T(8,128)(2,1)}, u32[]{:S(2)}, u32[]{:S(2)}) collective-permute-start(bf16[256,1536]{1,0:T(8,128)(2,1)} %pad_maximum_fusion.22), channel_id=1, source_target_pairs={{0,1},{1,0},{2,3},{3,2},{4,5},{5,4},{6,7},{7,6},{8,9},{9,8},{10,11... | collective-permute-start | bytes 2359304 | tf_op jit(solution)/shard_map/ppermute | solution.py:19
  191.9 117.3 %collective-permute-start.8 = (bf16[384,1536]{1,0:T(8,128)(2,1)}, bf16[384,1536]{1,0:T(8,128)(2,1)}, u32[]{:S(2)}, u32[]{:S(2)}) collective-permute-start(bf16[384,1536]{1,0:T(8,128)(2,1)} %bitcast.20), channel_id=1, source_target_pairs={{0,2},{2,0},{1,3},{3,1},{4,6},{6,4},{5,7},{7,5},{8,10},{10,8},{9,1... | collective-permute-start | bytes 3538952 | tf_op jit(solution)/shard_map/ppermute | solution.py:19
  207.7 101.5 %collective-permute-start.9 = (bf16[384,1536]{1,0:T(8,128)(2,1)}, bf16[384,1536]{1,0:T(8,128)(2,1)}, u32[]{:S(2)}, u32[]{:S(2)}) collective-permute-start(bf16[384,1536]{1,0:T(8,128)(2,1)} %collective-permute-done.7), channel_id=1, source_target_pairs={{0,2},{2,0},{1,3},{3,1},{4,6},{6,4},{5,7},{7,5},{8,10},{10,8},{9,1... | collective-permute-start | bytes 3538952 | tf_op jit(solution)/shard_map/ppermute | solution.py:19
  211.9 102.6 %collective-permute-start.16 = (bf16[384,3072]{1,0:T(8,128)(2,1)}, bf16[384,3072]{1,0:T(8,128)(2,1)}, u32[]{:S(2)}, u32[]{:S(2)}) collective-permute-start(bf16[384,3072]{1,0:T(8,128)(2,1)} %all-gather.11.cloned.1.call-done), channel_id=1, source_target_pairs={{0,4},{4,0},{1,5},{5,1},{2,6},{6,2},{3,7},{7,3},{8,12},{12,8},{9,1... | collective-permute-start | bytes 7077896 | tf_op jit(solution)/shard_map/ppermute | solution.py:19
  317.8 104.3 %collective-permute-start.14 = (bf16[384,6144]{1,0:T(8,128)(2,1)}, bf16[384,6144]{1,0:T(8,128)(2,1)}, u32[]{:S(2)}, u32[]{:S(2)}) collective-permute-start(bf16[384,6144]{1,0:T(8,128)(2,1)} %all-gather.9.cloned.1.call-done), channel_id=1, source_target_pairs={{0,4},{4,0},{1,5},{5,1},{2,6},{6,2},{3,7},{7,3},{8,12},{12,8},{9,1... | collective-permute-start | bytes 14155784 | tf_op jit(solution)/shard_map/ppermute | solution.py:19
  351.6 73.2 %collective-permute-start.11 = (bf16[256,1536]{1,0:T(8,128)(2,1)S(1)}, bf16[256,1536]{1,0:T(8,128)(2,1)S(1)}, u32[]{:S(2)}, u32[]{:S(2)}) collective-permute-start(bf16[256,1536]{1,0:T(8,128)(2,1)S(1)} %get-tuple-element.137), channel_id=1, source_target_pairs={{0,2},{2,0},{1,3},{3,1},{4,6},{6,4},{5,7},{7,5},{8,10},{10,8},{9,1... | collective-permute-start | bytes 2359304 | tf_op jit(solution)/shard_map/ppermute | solution.py:19
  566.8 194.8 %collective-permute-start.40 = (bf16[384,3072]{1,0:T(8,128)(2,1)}, bf16[384,3072]{1,0:T(8,128)(2,1)}, u32[]{:S(2)}, u32[]{:S(2)}) collective-permute-start(bf16[384,3072]{1,0:T(8,128)(2,1)} %pad_maximum_fusion.9), channel_id=1, source_target_pairs={{0,4},{4,0},{1,5},{5,1},{2,6},{6,2},{3,7},{7,3},{8,12},{12,8},{9,1... | collective-permute-start | bytes 7077896 | tf_op jit(solution)/shard_map/ppermute | solution.py:19
  589.9 58.8 %collective-permute-start.36 = (bf16[768,768]{1,0:T(8,128)(2,1)}, bf16[768,768]{1,0:T(8,128)(2,1)}, u32[]{:S(2)}, u32[]{:S(2)}) collective-permute-start(bf16[768,768]{1,0:T(8,128)(2,1)} %convolution_convert_fusion.12), channel_id=1, source_target_pairs={{0,2},{2,0},{1,3},{3,1},{4,6},{6,4},{5,7},{7,5},{8,10},{10,8},{9,1... | collective-permute-start | bytes 3538952 | tf_op jit(solution)/shard_map/ppermute | solution.py:19
  634.9 351.1 %reduce-scatter.15.cloned.1.call-start = ((), (), s32[]{:S(2)}) async-start(), calls=%async_computation.14 | async-start | bytes 737280 | tf_op jit(solution)/shard_map/reduce_scatter | solution.py:72
  640.2 193.1 %collective-permute-start.38 = (bf16[384,6144]{1,0:T(8,128)(2,1)}, bf16[384,6144]{1,0:T(8,128)(2,1)}, u32[]{:S(2)}, u32[]{:S(2)}) collective-permute-start(bf16[384,6144]{1,0:T(8,128)(2,1)} %pad_maximum_fusion.4), channel_id=1, source_target_pairs={{0,4},{4,0},{1,5},{5,1},{2,6},{6,2},{3,7},{7,3},{8,12},{12,8},{9,1... | collective-permute-start | bytes 14155784 | tf_op jit(solution)/shard_map/ppermute | solution.py:19
  648.7 339.0 %reduce-scatter.19.cloned.1.call-start = ((), (), s32[]{:S(2)}) async-start(), calls=%async_computation.16 | async-start | bytes 737280 | tf_op jit(solution)/shard_map/reduce_scatter | solution.py:72
  650.7 108.5 %collective-permute-start.37 = (bf16[384,768]{1,0:T(8,128)(2,1)S(1)}, bf16[384,768]{1,0:T(8,128)(2,1)S(1)}, u32[]{:S(2)}, u32[]{:S(2)}) collective-permute-start(bf16[384,768]{1,0:T(8,128)(2,1)S(1)} %add_convert_fusion.8), channel_id=1, source_target_pairs={{0,4},{4,0},{1,5},{5,1},{2,6},{6,2},{3,7},{7,3},{8,12},{12,8},{9,1... | collective-permute-start | bytes 1769480 | tf_op jit(solution)/shard_map/ppermute | solution.py:19
  655.8 114.7 %collective-permute-start.25 = (bf16[512,1536]{1,0:T(8,128)(2,1)}, bf16[512,1536]{1,0:T(8,128)(2,1)}, u32[]{:S(2)}, u32[]{:S(2)}) collective-permute-start(bf16[512,1536]{1,0:T(8,128)(2,1)} %convolution_convert_fusion.5), channel_id=1, source_target_pairs={{0,1},{1,0},{2,3},{3,2},{4,5},{5,4},{6,7},{7,6},{8,9},{9,8},{10,11... | collective-permute-start | bytes 4718600 | tf_op jit(solution)/shard_map/ppermute | solution.py:19
  761.4 266.0 %reduce-scatter.23.cloned.1.call-start = ((), (), s32[]{:S(2)}) async-start(), calls=%async_computation.18 | async-start | bytes 2949120 | tf_op jit(solution)/shard_map/reduce_scatter | solution.py:72
  770.4 269.2 %reduce-scatter.25.cloned.1.call-start = ((), (), s32[]{:S(2)}) async-start(), calls=%async_computation.19 | async-start | bytes 245760
  850.9 192.1 %reduce-scatter.21.cloned.1.call-start = ((), (), s32[]{:S(2)}) async-start(), calls=%async_computation.17 | async-start | bytes 5898240 | tf_op jit(solution)/shard_map/reduce_scatter | solution.py:72
  856.0 190.1 %reduce-scatter.13.cloned.1.call-start = ((), (), s32[]{:S(2)}) async-start(), calls=%async_computation.13 | async-start | bytes 737280 | tf_op jit(solution)/shard_map/reduce_scatter | solution.py:72
  870.3 87.4 %collective-permute-start.28 = (bf16[768,2304]{1,0:T(8,128)(2,1)}, bf16[768,2304]{1,0:T(8,128)(2,1)}, u32[]{:S(2)}, u32[]{:S(2)}) collective-permute-start(bf16[768,2304]{1,0:T(8,128)(2,1)} %convolution_convert_fusion), channel_id=1, source_target_pairs={{0,2},{2,0},{1,3},{3,1},{4,6},{6,4},{5,7},{7,5},{8,10},{10,8},{9,1... | collective-permute-start | bytes 10616840 | tf_op jit(solution)/shard_map/ppermute | solution.py:19
  897.4 83.7 %collective-permute-start.30 = (bf16[768,768]{1,0:T(8,128)(2,1)}, bf16[768,768]{1,0:T(8,128)(2,1)}, u32[]{:S(2)}, u32[]{:S(2)}) collective-permute-start(bf16[768,768]{1,0:T(8,128)(2,1)} %convolution_convert_fusion.14), channel_id=1, source_target_pairs={{0,2},{2,0},{1,3},{3,1},{4,6},{6,4},{5,7},{7,5},{8,10},{10,8},{9,1... | collective-permute-start | bytes 3538952 | tf_op jit(solution)/shard_map/ppermute | solution.py:19
  1014.2 60.3 %reduce-scatter.11.cloned.1.call-start = ((), (), s32[]{:S(2)}) async-start(), calls=%async_computation.12 | async-start | bytes 2211840 | tf_op jit(solution)/shard_map/reduce_scatter | solution.py:72
  (186 other events, 2124.5 us)
Sparse Core Ops, SparseCore 0:
  11.2 54.7 all-gather.4
  67.6 39.0 all-gather.6
  108.3 49.3 all-gather.10
  159.7 88.2 all-gather.8
  635.1 19.7 reduce-scatter.16
  657.0 20.4 reduce-scatter.14
  761.5 19.7 reduce-scatter.18
  783.6 46.3 reduce-scatter.22
  851.1 17.8 reduce-scatter.24
  871.2 83.4 reduce-scatter.20
  1014.3 20.9 reduce-scatter.12
  1037.6 36.8 reduce-scatter.10

commit v2 on v1

v2 whole, which is shorter than its diff:
```python
import functools

import jax
import jax.numpy as jnp
import numpy as np
from jax import lax
from jax.experimental import pallas as pl
from jax.experimental.pallas import tpu as pltpu
from jax.sharding import Mesh
from jax.sharding import PartitionSpec as P

HD = 64
ROT = 32
GROUP = 4
GW = GROUP * HD
UB = 256
EPSILON = 1e-05
SCALE = HD ** (-0.5)
F32 = jnp.float32
BF16 = jnp.bfloat16
DP = ("A", "B", "C")
T = "T"
FLIP = [(0, 1), (1, 0)]
AXIS = {"x": "C", "y": "B"}
VMEM_LIMIT = 58 * 1024 * 1024


class Lane:
    def __init__(self):
        self.last = None

    def run(self, move, value):
        if self.last is not None:
            value, _ = lax.optimization_barrier((value, self.last))
        self.last = move(value)
        return self.last


LANES = {}
TAIL = Lane()


def swap(value, axis):
    move = functools.partial(lax.ppermute, axis_name=axis, perm=FLIP)
    return LANES[axis].run(move, value) if axis in LANES else move(value)


def dot(left, right, dims):
    return lax.dot_general(left, right, (dims, ((), ())), preferred_element_type=F32)


def nn(left, right):
    return dot(left, right, ((1,), (0,)))


def nt(left, right):
    return dot(left, right, ((1,), (1,)))


def tn(left, right):
    return dot(left, right, ((0,), (0,)))


def pick(flag, when_zero, when_one):
    return jnp.where(flag == 0, when_zero, when_one)


def to_rel(values, outer, b, c):
    lead = values.shape[:-1]
    n = len(lead)
    v = values.reshape(lead + (outer, 2, 2, -1))
    v = jnp.transpose(v, tuple(range(n)) + (n + 2, n + 1, n, n + 3)).reshape(values.shape)
    return flip_blocks(v, b, c)


def flip_blocks(v, b, c):
    w = v.shape[-1]
    v = pick(c, v, jnp.concatenate([v[..., w // 2 :], v[..., : w // 2]], axis=-1))
    q = w // 4
    turned = [v[..., q : 2 * q], v[..., :q], v[..., 3 * q :], v[..., 2 * q : 3 * q]]
    return pick(b, v, jnp.concatenate(turned, axis=-1))


def from_rel(values, outer, b, c):
    lead = values.shape[:-1]
    n = len(lead)
    v = flip_blocks(values, b, c).reshape(lead + (2, 2, outer, -1))
    v = jnp.transpose(v, tuple(range(n)) + (n + 2, n + 1, n, n + 3))
    return v.reshape(values.shape)


def flip_half(values):
    half = values.shape[-1] // 2
    return jnp.concatenate([values[..., half:], values[..., :half]], axis=-1)


def gather_z(shard):
    return lax.all_gather(shard, "A", axis=0, tiled=True)


def scatter_z(rows):
    return lax.psum_scatter(rows, "A", scatter_dimension=0, tiled=True)


def hold(value, *others):
    return lax.optimization_barrier((value,) + others)[0]


def gather(shard, split):
    first = gather_z(shard)
    over_y, over_x = swap(first, "B"), swap(first, "C")
    fourth = []
    if split > 0:
        fourth.append((swap(over_y[:, :split], "C"), 0, split))
    if split < shard.shape[1]:
        fourth.append((swap(over_x[:, split:], "B"), split, shard.shape[1]))
    n = shard.shape[1]
    return {
        (0, 0): [(first, 0, n)],
        (0, 1): [(over_y, 0, n)],
        (1, 0): [(over_x, 0, n)],
        (1, 1): fourth,
    }


def columns(pieces, lo, width):
    found = []
    for p in PIECES:
        for a, begin, end in pieces[p]:
            if begin <= lo and lo + width <= end:
                found.append((a, (lo - begin) // width))
    return found


PIECES = ((0, 0), (0, 1), (1, 0), (1, 1))


class Scatter:
    def __init__(self, order):
        self.order = order

    def first(self, sent, kept):
        self.kept, self.got = kept, swap(sent, AXIS[self.order[0]])
        return self

    def second(self):
        n = self.kept.shape[1] // 2
        far = (self.kept[:, n:].astype(F32) + self.got[:, n:].astype(F32)).astype(BF16)
        moved = swap(far, AXIS[self.order[1]])
        near = self.kept[:, :n].astype(F32) + self.got[:, :n].astype(F32)
        self.kept = (near + moved.astype(F32)).astype(BF16)
        return self

    def third(self):
        return TAIL.run(scatter_z, self.kept).astype(F32)


def full(array):
    nd = array.ndim
    return pl.BlockSpec(array.shape, lambda *_: (0,) * nd)


def piece_specs(found, n):
    return [pl.BlockSpec((a.shape[0], n), functools.partial(lambda i, *_: (0, i), i)) for a, i in found]


def piece_args(found):
    return [a for a, _ in found]


def call(body, outs, ins, specs, out_specs, grid=(1,), scratch=(), flops=0, name=None):
    moved = sum(int(np.prod(o.shape)) * o.dtype.itemsize for o in outs)
    moved += sum(int(np.prod(i.shape)) * i.dtype.itemsize for i in ins)
    return pl.pallas_call(
        body,
        out_shape=outs,
        grid=grid,
        in_specs=specs,
        out_specs=out_specs,
        scratch_shapes=list(scratch),
        compiler_params=pltpu.CompilerParams(
            dimension_semantics=("arbitrary",) * len(grid), vmem_limit_bytes=VMEM_LIMIT
        ),
        cost_estimate=pl.CostEstimate(flops=1, transcendentals=0, bytes_accessed=1),
        name=name,
    )(*ins)


def shape(dims, dtype):
    return jax.ShapeDtypeStruct(dims, dtype)


def head_masks(value):
    lane = lax.broadcasted_iota(jnp.int32, (1, GW), 1) // HD
    return [jnp.where(lane == h, value, 0.0).astype(BF16) for h in range(GROUP)]


def probabilities(qm, k, bias):
    scores = nt(qm, k)
    if bias is not None:
        scores = scores + bias
    top = jnp.max(scores, axis=-1, keepdims=True)
    e = jnp.exp(scores - top)
    return e * (1.0 / jnp.sum(e, axis=-1, keepdims=True))


def attention(q, k, v, bias):
    out = None
    for m, s in zip(head_masks(1.0), head_masks(SCALE)):
        p = probabilities(q * s, k, bias).astype(BF16)
        o = nn(p, v * m)
        out = o if out is None else out + o
    return out


def attention_back(q, k, v, do, bias):
    dq = dk = dv = None
    for m, s in zip(head_masks(1.0), head_masks(SCALE)):
        qm = q * s
        p = probabilities(qm, k, bias)
        dom = do * m
        dp = nt(dom, v)
        centre = jnp.sum(p * dp, axis=-1, keepdims=True)
        ds = (p * (dp - centre)).astype(BF16)
        a, b, c = nn(ds, k * s), tn(ds, qm), tn(p.astype(BF16), dom)
        dq, dk, dv = (a, b, c) if dq is None else (dq + a, dk + b, dv + c)
    return (dq, dk, dv)


def turn(u, cos, sin_a, sin_b):
    return u * cos + pltpu.roll(u, GW - ROT // 2, 1) * sin_a + pltpu.roll(u, ROT // 2, 1) * sin_b


def rotary_tables(length):
    half_dim = ROT // 2
    freqs = 10000.0 ** (-(2.0 * jnp.arange(half_dim, dtype=F32) / ROT))
    angles = jnp.arange(length, dtype=F32)[:, None] * freqs[None, :]
    cos, sin = jnp.cos(angles), jnp.sin(angles)
    rest = jnp.zeros((length, HD - ROT), F32)
    none = jnp.zeros_like(sin)
    return tuple(
        jnp.tile(jnp.concatenate(parts, axis=1), (1, GROUP))
        for parts in ((cos, cos, rest + 1.0), (-sin, none, rest), (none, sin, rest))
    )


def norm_rows(pieces, at, outer_rows):
    found = columns(pieces, at, 128)

    def body(*refs):
        for i in range(4):
            refs[4][:, i * outer_rows : (i + 1) * outer_rows] = refs[i][...].astype(F32).T[:8, :]

    out = shape((8, 4 * outer_rows), F32)
    return call(body, [out], piece_args(found), piece_specs(found, 128), [full(out)], name="norm_rows")[0]


def restore(values, turned_b, turned_c, outer):
    rows, width = values.shape
    block = width // (4 * outer)
    h, q = width // 2, width // 4
    step = 128

    def body(b_ref, c_ref, v_ref, out_ref):
        v = v_ref[...]
        v = jnp.where(c_ref[0] == 0, v, jnp.concatenate([v[:, h:], v[:, :h]], axis=1))
        turned = [v[:, q : 2 * q], v[:, :q], v[:, 3 * q :], v[:, 2 * q : 3 * q]]
        v = jnp.where(b_ref[0] == 0, v, jnp.concatenate(turned, axis=1))
        out_ref[...] = jnp.concatenate(
            [
                v[:, (2 * c + b) * q + a * block : (2 * c + b) * q + (a + 1) * block]
                for a in range(outer)
                for b in range(2)
                for c in range(2)
            ],
            axis=1,
        )

    row = pl.BlockSpec((step, width), lambda i: (i, 0))
    flag = pl.BlockSpec(memory_space=pltpu.SMEM)
    return call(
        body,
        [shape((rows, width), values.dtype)],
        [turned_b.reshape(1), turned_c.reshape(1), values],
        [flag, flag, row],
        [row],
        grid=(rows // step,),
        name="restore",
    )[0]


def add_norm(base, mine, other, norms, index):
    rows, width = base.shape
    step = 256
    extra = [] if mine is None else [mine, other]

    def body(*refs):
        base_ref, norm_ref = refs[0], refs[1]
        h = base_ref[...].astype(F32)
        if extra:
            h = h + (refs[2][...].astype(F32) + refs[3][...].astype(F32))
        outs = refs[2 + len(extra) :]
        average = jnp.mean(h, axis=-1, keepdims=True)
        centred = h - average
        spread = jnp.mean(centred * centred, axis=-1, keepdims=True)
        normed = centred * lax.rsqrt(spread + EPSILON)
        gain = norm_ref[index : index + 1, :]
        shift = norm_ref[index + 3 : index + 4, :]
        outs[0][...] = (normed * gain + shift).astype(BF16)
        if extra:
            outs[1][...] = h

    row = pl.BlockSpec((step, width), lambda i: (i, 0))
    outs = [shape((rows, width), BF16)] + ([shape((rows, width), F32)] if extra else [])
    return call(
        body,
        outs,
        [base, norms] + extra,
        [row, full(norms)] + [row] * len(extra),
        [row] * len(outs),
        grid=(rows // step,),
        flops=rows * width * 12,
        name="add_norm",
    )


def norm_back(mine, other, h, above, norms, index):
    rows, width = h.shape
    step = 256

    def body(mine_ref, other_ref, h_ref, above_ref, norm_ref, out_ref, low_ref, sums_ref):
        dn = mine_ref[...].astype(F32) + other_ref[...].astype(F32)
        h = h_ref[...].astype(F32)
        average = jnp.mean(h, axis=-1, keepdims=True)
        centred = h - average
        spread = jnp.mean(centred * centred, axis=-1, keepdims=True)
        factor = lax.rsqrt(spread + EPSILON)
        normed = centred * factor
        scaled = dn * norm_ref[index : index + 1, :]
        first = jnp.mean(scaled, axis=-1, keepdims=True)
        second = jnp.mean(scaled * normed, axis=-1, keepdims=True)
        d = above_ref[...].astype(F32) + factor * (scaled - first - normed * second)
        out_ref[...] = d
        low_ref[...] = d.astype(BF16)

        @pl.when(pl.program_id(0) == 0)
        def _():
            sums_ref[...] = jnp.zeros_like(sums_ref)

        sums_ref[0:1, :] += jnp.sum(dn * normed, axis=0, keepdims=True)
        sums_ref[1:2, :] += jnp.sum(dn, axis=0, keepdims=True)

    row = pl.BlockSpec((step, width), lambda i: (i, 0))
    return call(
        body,
        [shape((rows, width), F32), shape((rows, width), BF16), shape((8, width), F32)],
        [mine, other, h, above, norms],
        [row, row, row, row, full(norms)],
        [row, row, pl.BlockSpec((8, width), lambda i: (0, 0))],
        grid=(rows // step,),
        flops=rows * width * 20,
        name="norm_back",
    )


def self_forward(n, pieces, tables, total, slots, last):
    rows, width = n.shape
    length = rows // slots
    q4 = width // 4
    cols = 4 * GW

    def body(*refs):
        n_ref, w_refs, tabs = refs[0], refs[1:5], refs[5:8]
        k = 8
        total_ref = None
        if total is not None:
            total_ref = refs[8]
            k = 9
        keep_ref, part_ref, w, raw = refs[k:]
        for i, r in enumerate(w_refs):
            w[i * q4 : (i + 1) * q4, :] = r[...]
        raw[...] = nn(n_ref[...], w[:, : 3 * GW])
        cos, sin_a, sin_b = (r[...] for r in tabs)
        for l in range(slots):
            at = slice(l * length, (l + 1) * length)
            q = turn(raw[at, :GW], cos, sin_a, sin_b).astype(BF16)
            key = turn(raw[at, GW : 2 * GW], cos, sin_a, sin_b).astype(BF16)
            v = raw[at, 2 * GW :].astype(BF16)
            keep_ref[at, :GW] = q
            keep_ref[at, GW : 2 * GW] = key
            keep_ref[at, 2 * GW : 3 * GW] = v
            keep_ref[at, 3 * GW :] = attention(q, key, v, None).astype(BF16)
        part = nt(keep_ref[:, 3 * GW :], w[:, 3 * GW :])
        if total_ref is not None:
            part = part + total_ref[...]
        part_ref[...] = part.astype(part_ref.dtype)

    ins = [n] + piece_args(pieces) + list(tables) + ([] if total is None else [total])
    specs = [full(n)] + piece_specs(pieces, cols) + [full(a) for a in tables]
    specs += [] if total is None else [full(total)]
    outs = [shape((rows, cols), BF16), shape((rows, width), BF16 if last else F32)]
    return call(
        body,
        outs,
        ins,
        specs,
        [full(o) for o in outs],
        scratch=[pltpu.VMEM((width, cols), BF16), pltpu.VMEM((rows, 3 * GW), F32)],
        flops=2 * rows * width * cols,
        name="self_forward",
    )


def load_cross(w_refs, w, wp, at, block, pair_block):
    both = block + pair_block
    outer = w_refs[0][0].shape[0] // both
    for i, parts in enumerate(w_refs):
        for o in range(outer):
            r = parts[0]
            w[(i * outer + o) * block : (i * outer + o + 1) * block, at] = r[o * both : o * both + block, :]
            wp[(i * outer + o) * pair_block : (i * outer + o + 1) * pair_block, at] = r[
                o * both + block : (o + 1) * both, :
            ]


def cross_operands(pieces, groups):
    found = [columns(pieces, j * 2 * GW, 2 * GW) for j in range(groups)]
    return [a for f in found for a in piece_args(f)], [q for f in found for q in piece_specs(f, 2 * GW)]


def cross_forward(n, ctx, pieces, slots, cond, groups, block, pair_block):
    rows, width = n.shape
    length, keys = rows // slots, ctx.shape[0] // slots
    cols = groups * 2 * GW

    def body(n_ref, ctx_ref, *refs):
        w_refs = refs[: 4 * groups]
        keep_ref, pair_ref, part_ref, w, wp, cq = refs[4 * groups :]
        lane = lax.broadcasted_iota(jnp.int32, (1, keys), 1)
        bias = jnp.where(lane < cond, 0.0, -1e30).astype(F32)
        part = None
        for j in range(groups):
            at_j = slice(2 * j * GW, 2 * (j + 1) * GW)
            load_cross([[r] for r in w_refs[4 * j : 4 * j + 4]], w, wp, at_j, block, pair_block)
            at_q = slice(2 * j * GW, (2 * j + 1) * GW)
            at_o = slice((2 * j + 1) * GW, (2 * j + 2) * GW)
            pair_ref[:, at_j] = nn(ctx_ref[...], wp[:, at_j]).astype(BF16)
            cq[...] = nn(n_ref[...], w[:, at_q]).astype(BF16)
            keep_ref[:, at_q] = cq[...]
            for l in range(slots):
                at = slice(l * length, (l + 1) * length)
                at_k = slice(l * keys, (l + 1) * keys)
                o = attention(cq[at, :], pair_ref[at_k, at_q], pair_ref[at_k, at_o], bias)
                keep_ref[at, at_o] = o.astype(BF16)
            more = nt(keep_ref[:, at_o], w[:, at_o])
            part = more if part is None else part + more
        part_ref[...] = part.astype(BF16)

    more_ins, more_specs = cross_operands(pieces, groups)
    ins = [n, ctx] + more_ins
    specs = [full(n), full(ctx)] + more_specs
    outs = [
        shape((rows, cols), BF16),
        shape((slots * keys, cols), BF16),
        shape((rows, width), BF16),
    ]
    return call(
        body,
        outs,
        ins,
        specs,
        [full(o) for o in outs],
        scratch=[
            pltpu.VMEM((width, cols), BF16),
            pltpu.VMEM((ctx.shape[1], cols), BF16),
            pltpu.VMEM((rows, GW), BF16),
        ],
        flops=2 * rows * width * cols + 2 * ctx.shape[0] * ctx.shape[1] * cols,
        name="cross_forward",
    )


def feed_forward(x, d, near_w, far_w, blocks):
    rows, width = x.shape
    q4 = width // 4
    cols = 6 * UB

    def body(x_ref, d_ref, a_ref, b_ref, keep_ref, send_ref, dn_ref, y_ref, w, dn, y):
        j = pl.program_id(0)
        for rx in range(2):
            for ry, r in enumerate((a_ref, b_ref)):
                at = (2 * rx + ry) * q4
                w[at : at + q4, :] = r[:, rx * 3 * UB : (rx + 1) * 3 * UB]
        gu = nn(x_ref[...], w[:, : 2 * UB])
        dh = nn(d_ref[...], w[:, 2 * UB :])
        gate, upper = gu[:, :UB], gu[:, UB:]
        sig = 1.0 / (1.0 + jnp.exp(-gate))
        silu = gate * sig
        hidden = (silu * upper).astype(BF16)
        dg = (dh * upper * (sig * (1.0 + gate * (1.0 - sig)))).astype(BF16)
        du = (dh * silu).astype(BF16)
        dgu = jnp.concatenate([dg, du], axis=1)
        for at, ref in ((0, keep_ref), (1, send_ref)):
            for rx in range(2):
                c0 = (2 * rx + at) * q4
                lo = rx * 3 * UB
                ref[:, lo : lo + 2 * UB] = tn(x_ref[:, c0 : c0 + q4], dgu).astype(BF16)
                ref[:, lo + 2 * UB : lo + 3 * UB] = tn(d_ref[:, c0 : c0 + q4], hidden).astype(BF16)
        more_dn = nt(dgu, w[:, : 2 * UB])
        more_y = nt(hidden, w[:, 2 * UB :])

        @pl.when(j == 0)
        def _():
            dn[...] = more_dn
            y[...] = more_y

        @pl.when(j > 0)
        def _():
            dn[...] += more_dn
            y[...] += more_y

        @pl.when(j == pl.num_programs(0) - 1)
        def _():
            dn_ref[...] = dn[...].astype(BF16)
            y_ref[...] = y[...].astype(BF16)

    block = pl.BlockSpec((q4, cols), lambda j: (0, j))
    from_w = [
        pl.BlockSpec((q4, cols), functools.partial(lambda i, j: (0, i + j), i * blocks))
        for _, i in (near_w, far_w)
    ]
    ins = [x, d, near_w[0], far_w[0]]
    outs = [shape((q4, blocks * cols), BF16)] * 2 + [shape((rows, width), BF16)] * 2
    return call(
        body,
        outs,
        ins,
        [full(x), full(d)] + from_w,
        [block, block] + [full(o) for o in outs[2:]],
        grid=(blocks,),
        scratch=[
            pltpu.VMEM((width, 3 * UB), BF16),
            pltpu.VMEM((rows, width), F32),
            pltpu.VMEM((rows, width), F32),
        ],
        flops=18 * rows * width * UB * blocks,
        name="feed_forward",
    )


def split_rows(left_ref, right, first, n, keep_ref, send_ref, lo=0, outer=1, at_row=0):
    q = left_ref.shape[1] // 4
    run = keep_ref.shape[0] // outer
    part = q // outer
    for rx, ry in PIECES:
        g = tn(left_ref[:, (2 * rx + ry) * q : (2 * rx + ry + 1) * q], right).astype(BF16)
        goes, other = (rx, ry) if first == "x" else (ry, rx)
        ref = send_ref if goes else keep_ref
        cols = slice(other * n + lo, other * n + lo + right.shape[1])
        for o in range(outer):
            ref[o * run + at_row : o * run + at_row + part, cols] = g[o * part : (o + 1) * part, :]


def cross_backward(dc, n, ctx, keep, pair_rows, pieces, slots, cond, groups, block, pair_block, first):
    rows, width = n.shape
    length, keys = rows // slots, ctx.shape[0] // slots
    cols = keep.shape[1]
    outer = width // 4 // block

    def body(dc_ref, n_ref, ctx_ref, keep_in, pair_in, *refs):
        w_refs = refs[: 4 * groups]
        g_keep, g_send, dn_ref, dctx_ref, w, wp, do, dcq, dpair = refs[4 * groups :]
        lane = lax.broadcasted_iota(jnp.int32, (1, keys), 1)
        bias = jnp.where(lane < cond, 0.0, -1e30).astype(F32)
        dn = None
        for j in range(groups):
            at_j = slice(2 * j * GW, 2 * (j + 1) * GW)
            load_cross([[r] for r in w_refs[4 * j : 4 * j + 4]], w, wp, at_j, block, pair_block)
            at_q = slice(2 * j * GW, (2 * j + 1) * GW)
            at_o = slice((2 * j + 1) * GW, (2 * j + 2) * GW)
            do[...] = nn(dc_ref[...], w[:, at_o]).astype(BF16)
            for l in range(slots):
                at = slice(l * length, (l + 1) * length)
                at_k = slice(l * keys, (l + 1) * keys)
                a, b, c = attention_back(
                    keep_in[at, at_q], pair_in[at_k, at_q], pair_in[at_k, at_o], do[at, :], bias
                )
                dcq[at, :] = a.astype(BF16)
                dpair[at_k, at_q] = b.astype(BF16)
                dpair[at_k, at_o] = c.astype(BF16)
            more = nt(dcq[...], w[:, at_q])
            dn = more if dn is None else dn + more
            split_rows(n_ref, dcq[...], first, cols, g_keep, g_send, 2 * j * GW, outer)
            split_rows(dc_ref, keep_in[:, at_o], first, cols, g_keep, g_send, (2 * j + 1) * GW, outer)
            split_rows(ctx_ref, dpair[:, at_j], first, cols, g_keep, g_send, 2 * j * GW, outer, block)
        dn_ref[...] = dn.astype(BF16)
        dctx_ref[...] = nt(dpair[...], wp[...]).astype(BF16)

    more_ins, more_specs = cross_operands(pieces, groups)
    ins = [dc, n, ctx, keep, pair_rows] + more_ins
    specs = [full(a) for a in ins[:5]] + more_specs
    grad_rows = outer * (block + pair_block)
    outs = [
        shape((grad_rows, 2 * cols), BF16),
        shape((grad_rows, 2 * cols), BF16),
        shape((rows, width), BF16),
        shape(ctx.shape, BF16),
    ]
    return call(
        body,
        outs,
        ins,
        specs,
        [full(o) for o in outs],
        scratch=[
            pltpu.VMEM((width, cols), BF16),
            pltpu.VMEM((ctx.shape[1], cols), BF16),
            pltpu.VMEM((rows, GW), BF16),
            pltpu.VMEM((rows, GW), BF16),
            pltpu.VMEM((slots * keys, cols), BF16),
        ],
        flops=4 * rows * width * cols + 4 * ctx.shape[0] * ctx.shape[1] * cols,
        name="cross_backward",
    )


def self_backward(da, n, keep, pieces, tables, total, slots, first, last):
    rows, width = n.shape
    length = rows // slots
    q4 = width // 4
    cols = 4 * GW

    def body(*refs):
        da_ref, n_ref, keep_in, w_refs, tabs = refs[0], refs[1], refs[2], refs[3:7], refs[7:10]
        k = 10
        total_ref = None
        if total is not None:
            total_ref = refs[10]
            k = 11
        g_keep, g_send, dn_ref, w, do, dt = refs[k:]
        for i, r in enumerate(w_refs):
            w[i * q4 : (i + 1) * q4, :] = r[...]
        do[...] = nn(da_ref[...], w[:, 3 * GW :]).astype(BF16)
        cos, sin_a, sin_b = (r[...] for r in tabs)
        for l in range(slots):
            at = slice(l * length, (l + 1) * length)
            dq, dk, dv = attention_back(
                keep_in[at, :GW], keep_in[at, GW : 2 * GW], keep_in[at, 2 * GW : 3 * GW], do[at, :], None
            )
            dt[at, :GW] = turn(dq, cos, -sin_a, -sin_b).astype(BF16)
            dt[at, GW : 2 * GW] = turn(dk, cos, -sin_a, -sin_b).astype(BF16)
            dt[at, 2 * GW :] = dv.astype(BF16)
        split_rows(n_ref, dt[...], first, cols, g_keep, g_send)
        split_rows(da_ref, keep_in[:, 3 * GW :], first, cols, g_keep, g_send, 3 * GW)
        dn = nt(dt[...], w[:, : 3 * GW])
        if total_ref is not None:
            dn = dn + total_ref[...]
        dn_ref[...] = dn.astype(dn_ref.dtype)

    ins = [da, n, keep] + piece_args(pieces) + list(tables) + ([] if total is None else [total])
    specs = [full(da), full(n), full(keep)] + piece_specs(pieces, cols)
    specs += [full(a) for a in tables] + ([] if total is None else [full(total)])
    outs = [
        shape((q4, 2 * cols), BF16),
        shape((q4, 2 * cols), BF16),
        shape((rows, width), BF16 if last else F32),
    ]
    return call(
        body,
        outs,
        ins,
        specs,
        [full(o) for o in outs],
        scratch=[
            pltpu.VMEM((width, cols), BF16),
            pltpu.VMEM((rows, GW), BF16),
            pltpu.VMEM((rows, 3 * GW), BF16),
        ],
        flops=4 * rows * width * cols,
        name="self_backward",
    )


ATTN_SPLIT = 2
CROSS_SPLIT = 1
FF_BLOCKS = (2, 2, 2)
FF_EARLY_Y = (True, False, False)
ATTN_SCATTER = ("xyz", "xyz", "yxz")
CROSS_SCATTER = "xyz"


def on_device(
    tokens,
    context,
    live_count,
    cotangent,
    triple_weight,
    attn_out_weight,
    cross_query_weight,
    cross_pair_weight,
    cross_out_weight,
    gate_up_weight,
    down_weight,
    norm_gains,
    norm_shifts,
):
    LANES.clear()
    TAIL.last = None
    LANES.update({name: Lane() for name in DP[1:]})
    b = lax.axis_index("B")
    c = lax.axis_index("C")
    t = lax.axis_index(T)
    outer = lax.axis_size("A")
    slots, length, width = tokens.shape
    rows = slots * length
    half = rows // 2
    cond = context.shape[1]
    keys = -(-cond // 16) * 16
    block = triple_weight.shape[0]
    pair_block = cross_pair_weight.shape[0]
    local = triple_weight.shape[2]
    groups = local // GW
    units = gate_up_weight.shape[2]
    part_blocks = units // 2 // UB
    q4 = width // 4

    def group(w, j):
        return w[..., j * GW : (j + 1) * GW]

    live = (live_count[0] > jnp.arange(slots)).astype(F32)
    live_rows = jnp.repeat(live, length)[:, None]

    def by_core(value):
        return (
            pick(t, value[:half], value[half:]),
            pick(t, value[half:], value[:half]),
        )

    def from_core(mine, other):
        return jnp.concatenate([pick(t, mine, other), pick(t, other, mine)], axis=0)

    def spread(value):
        mine, other = by_core(value)
        far = flip_half(swap(mine, "C"))
        return jnp.concatenate([mine, far, other, swap(far, T)], axis=0)

    def collect(parts):
        total = sum(p.astype(F32) for p in parts)
        got = total[:rows] + swap(total[rows:].astype(BF16), T).astype(F32)
        return got[:half] + swap(flip_half(got[half:].astype(BF16)), "C").astype(F32)

    attn_t, cross_t = attn_out_weight.T, cross_out_weight.T
    norm_in = jnp.concatenate([norm_gains, norm_shifts], axis=0).T
    attn_in = jnp.concatenate(
        [group(w, j) for j in range(groups) for w in [triple_weight[:, k] for k in range(3)] + [attn_t]]
        + [jnp.pad(norm_in, ((0, 0), (0, 128 - norm_in.shape[1])))],
        axis=1,
    )
    cross_in = jnp.concatenate(
        [
            jnp.concatenate(
                [group(w, j) for j in range(groups) for w in (cross_query_weight, cross_t)], axis=1
            ),
            jnp.concatenate(
                [group(cross_pair_weight[:, k], j) for j in range(groups) for k in range(2)], axis=1
            ),
        ],
        axis=0,
    )
    ff = jnp.concatenate([gate_up_weight, down_weight.T[:, None]], axis=1)
    ff = ff.reshape(block, 3, 2, part_blocks, UB).transpose(2, 0, 3, 1, 4)
    ff = ff.reshape(2, block, part_blocks, 3 * UB)
    ff_own = pick(c, ff[0], ff[1])
    ff_far = swap(pick(c, ff[1], ff[0]), "C")
    ff_in = jnp.stack([ff_own, ff_far], axis=2).reshape(block, part_blocks * 6 * UB)

    early = []
    at = 0
    for blocks, soon in zip(FF_BLOCKS, FF_EARLY_Y):
        shard = ff_in[:, at : at + blocks * 6 * UB]
        at += blocks * 6 * UB
        early.append((shard, swap(shard, "B") if soon else None))
    grad_top = to_rel(cotangent.reshape(rows, width), outer, b, c) * live_rows.astype(BF16)
    attn_w = gather(attn_in, ATTN_SPLIT * 4 * GW)
    cross_w = gather(cross_in, CROSS_SPLIT * 2 * GW)
    grad_all = spread(grad_top)
    norm_at = groups * 4 * GW
    norms = norm_rows(attn_w, norm_at, q4)
    ff_w = []
    for shard, moved in early:
        if moved is None:
            near = gather_z(shard)
            ff_w.append(((near, 0), (swap(near, "B"), 0)))
        else:
            whole = gather_z(jnp.concatenate([shard, moved], axis=1))
            ff_w.append(((whole, 0), (whole, 1)))

    start = to_rel(tokens.reshape(rows, width), outer, b, c)
    ctx = jnp.pad(to_rel(context, outer, b, c), ((0, 0), (0, keys - cond), (0, 0)))
    ctx = ctx.reshape(slots * keys, -1)
    tables = rotary_tables(length)

    (n1,) = add_norm(start, None, None, norms, 0)
    keep_one, part = [], None
    for j in range(groups):
        keep, part = self_forward(n1, columns(attn_w, j * 4 * GW, 4 * GW), tables, part, slots, j == groups - 1)
        keep_one.append(keep)
    part = hold(part, ff_w[0][0][0])
    n2, h1 = add_norm(start, part, swap(part, T), norms, 1)
    keep_two, pair_rows, part = cross_forward(n2, ctx, cross_w, slots, cond, groups, block, pair_block)
    part = hold(part, ff_w[1][0][0])
    n3, h2 = add_norm(h1, part, swap(part, T), norms, 2)
    n3_all = spread(n3)

    n3_all = hold(n3_all, *[w[0][0] for w in ff_w], ff_w[1][1][0])
    g_ff, dn3, y = [], [], []
    for i, blocks in enumerate(FF_BLOCKS):
        keep, send, dn_part, y_part = feed_forward(n3_all, grad_all, ff_w[i][0], ff_w[i][1], blocks)
        dn3.append(dn_part)
        y.append(y_part)
        g_ff.append((keep, lax.ppermute(send, "B", FLIP)))
    dn3 = collect(dn3).astype(BF16)
    dn3 = from_core(dn3, swap(dn3, T))

    def ff_sum(keep, got):
        return scatter_z((keep.astype(F32) + got.astype(F32)).astype(BF16))

    g_done = [ff_sum(hold(g_ff[0][0], dn3), g_ff[0][1])]

    dh2, dc, sums_three = norm_back(dn3, jnp.zeros_like(dn3), h2, grad_top, norms, 2)
    g_keep, g_send, dn2, dctx = cross_backward(
        dc, n2, ctx, keep_two, pair_rows, cross_w, slots, cond, groups, block, pair_block, CROSS_SCATTER[0]
    )
    g_cross = Scatter(CROSS_SCATTER).first(g_send, g_keep)
    dh1, da, sums_two = norm_back(dn2, swap(dn2, T), h1, dh2, norms, 1)
    g_done.append(ff_sum(hold(g_ff[1][0], da), g_ff[1][1]))
    g_attn, sends, dn1 = [], [], None
    for j in range(groups):
        g_keep, g_send, dn1 = self_backward(
            da,
            n1,
            keep_one[j],
            columns(attn_w, j * 4 * GW, 4 * GW),
            tables,
            dn1,
            slots,
            ATTN_SCATTER[j][0],
            j == groups - 1,
        )
        sends.append((g_send, g_keep))
    g_cross.kept = hold(g_cross.kept, dn1)
    g_cross.second()
    for j in range(groups):
        send, kept = sends[j]
        g_attn.append(Scatter(ATTN_SCATTER[j]).first(hold(send, dn1), kept))
    g_done.append(ff_sum(hold(g_ff[2][0], dn1), g_ff[2][1]))
    dn1 = hold(dn1, g_done[0])
    dtok, _, sums_one = norm_back(dn1, swap(dn1, T), start, dh1, norms, 0)
    dtok = restore(dtok, b, c, outer)

    sums = (sums_one, sums_two, sums_three)
    g_norm = jnp.concatenate([s[i : i + 1] for i in (0, 1) for s in sums], axis=0)
    g_norm = g_norm[:, : 2 * q4] + lax.ppermute(g_norm[:, 2 * q4 :], "C", FLIP)
    g_norm = g_norm[:, :q4] + lax.ppermute(g_norm[:, q4:], "B", FLIP)
    g_norm = TAIL.run(scatter_z, jnp.pad(g_norm.T, ((0, 0), (0, 128 - g_norm.shape[0]))))
    dctx = dctx.astype(F32) + swap(dctx, T).astype(F32)
    dctx = from_rel(dctx.reshape(slots, keys, -1)[:, :cond], outer, b, c)

    g_attn[0].second()
    g_attn[1].second()

    out_half = collect(y) + by_core(h2)[0]
    out_half = (out_half * pick(t, live_rows[:half], live_rows[half:])).astype(BF16)
    out_half = lax.optimization_barrier(out_half)
    mixed = restore(from_core(out_half, swap(out_half, T)), b, c, outer)

    g_attn[2].second()
    g_cross.kept = hold(g_cross.kept, *g_done)
    g_cross = g_cross.third()
    g_attn[0].kept = hold(g_attn[0].kept, dtok, dctx)
    g_attn_0 = g_attn[0].third()
    g_ff = jnp.concatenate(g_done, axis=1).reshape(block, part_blocks, 2, 3 * UB)
    own, far = g_ff[:, :, 0], lax.ppermute(g_ff[:, :, 1], "C", FLIP)
    g_ff = jnp.stack([pick(c, own, far), pick(c, far, own)], axis=1).astype(F32)
    g_ff = g_ff.reshape(block, 2, part_blocks, 3, UB).transpose(0, 3, 1, 2, 4)
    g_ff = g_ff.reshape(block, 3, units)
    g_gate_up, g_down = g_ff[:, :2], g_ff[:, 2].T
    g_attn[1].kept = hold(g_attn[1].kept, mixed, g_gate_up, g_down)
    g_attn = [g_attn_0] + [g.third() for g in g_attn[1:]]

    g_attn = jnp.stack([g.reshape(block, 4, GW) for g in g_attn], axis=2)
    g_attn = g_attn.reshape(block, 4, local)
    g_cross = g_cross.reshape(block + pair_block, groups, 2, GW)
    g_pair = g_cross[block:].transpose(0, 2, 1, 3)
    g_cross = g_cross[:block]

    return (
        mixed.reshape(tokens.shape),
        dtok.reshape(tokens.shape),
        dctx,
        g_attn[:, :3],
        g_attn[:, 3].T,
        g_cross[:, :, 0].reshape(block, local),
        g_pair.reshape(pair_block, 2, local),
        g_cross[:, :, 1].reshape(block, local).T,
        g_gate_up,
        g_down,
        g_norm[:, :3].T,
        g_norm[:, 3:6].T,
    )


def solution(mesh):
    dp, tensor = mesh.devices.shape
    inner = Mesh(mesh.devices.reshape(dp // 4, 2, 2, tensor), DP + (T,))
    rows_dp = P(DP, None, None)
    weights = (
        P(DP, None, T),
        P(T, DP),
        P(DP, T),
        P(DP, None, T),
        P(T, DP),
        P(DP, None, T),
        P(T, DP),
        P(None, DP),
        P(None, DP),
    )
    return jax.shard_map(
        on_device,
        mesh=inner,
        in_specs=(rows_dp, rows_dp, P(DP), rows_dp) + weights,
        out_specs=(rows_dp, rows_dp, rows_dp) + weights,
        check_vma=False,
    )
```

time: 1090 us -> 818 us (0.75)
  Pallas kernels: 0 us -> 234 us
  waiting for transfers between devices: 509 us -> 301 us
  matrix products: 201 us -> 0 us
  local copies, waits for them, and re-layouts: 182 us -> 122 us
  other arithmetic: 133 us -> 81.3 us
  starting transfers between devices: 39.3 us -> 52.4 us
    pallas_call x0 -> x20, Pallas kernels: none -> 234 us  [call(): pl.pallas_call(body, out_shape=outs, grid=grid, in_specs=specs, out_specs...]
    ppermute x44 -> x41, waiting for transfers between devices: 456 us -> 239 us  [the longest x24 159 us: run(): self.last = move(value)]
    dot_general x50 -> x0, matrix products: 201 us -> none  [the longest x38 163 us: dot(): lax.dot_general(left, right, (dims, ((), ())), preferred_element_type=F32)]
    convert_element_type x15 -> x0, local copies, waits for them, and re-layouts: 29.5 us -> none  [the longest x2 6.69 us: norm_forward(): return ((normed * gain_row + shift_row).astype(BF16), normed, factor)]
    concatenate x17 -> x7, other arithmetic: 37.7 us -> 8.67 us  [the longest x2 3.91 us: spread(): return jnp.concatenate([mine, far, other, swap(far, T)], axis=0)]
    unnamed x354 -> x134, local copies, waits for them, and re-layouts: 64.1 us -> 40.4 us
    reduce_sum x11 -> x0, other arithmetic: 17.8 us -> none  [the longest x3 10.1 us: norm_backward(): jnp.sum(grad_rows * normed, axis=0)]
    dot_general x2 -> x0, local copies, waits for them, and re-layouts: 16.7 us -> none  [dot(): lax.dot_general(left, right, (dims, ((), ())), preferred_element_type=F32)]
  transfers between devices with their start and end apart: 56 -> 54, of which waited for: 23 -> 28; matrix products, arithmetic and copies ran while one was open for 37% -> 22% of each run, Pallas kernels for 0% -> 25%
where the time goes in v2:
time: 818 us; the launch traced here: 809 us
  waiting for transfers between devices  301 us (37%)
  Pallas kernels  234 us (29%)
  local copies, waits for them, and re-layouts  122 us (15%)
  other arithmetic  81.3 us (10%)
  starting transfers between devices  52.4 us (6%)
  between operations  17.4 us (2%)
    pallas_call x20, Pallas kernels, call(): pl.pallas_call(body, out_shape=outs, grid=grid, in_specs=specs, out_specs...  234 us
    ppermute x24, waiting for transfers between devices, run(): self.last = move(value)  159 us
    ppermute x3, waiting for transfers between devices, on_device(): g_ff.append((keep, lax.ppermute(send, 'B', FLIP)))  42.3 us
    unnamed x134, local copies, waits for them, and re-layouts  40.4 us
    all_gather x5, waiting for transfers between devices, gather_z(): return lax.all_gather(shard, 'A', axis=0, tiled=True)  37.1 us
    ppermute x24, starting transfers between devices, run(): self.last = move(value)  34 us
    ppermute x1, waiting for transfers between devices, on_device(): g_norm = g_norm[:, :2 * q4] + lax.ppermute(g_norm[:, 2 * q4:], 'C', FLIP)  19.6 us
  transfers between devices with their start and end apart: 54, of which 28 were waited for; matrix products, arithmetic and copies ran while one was open for 22% of the time, Pallas kernels for 25%

profile of v2, /device:TPU:0, one launch (start us, length us, event | category | flops | bytes accessed | tf_op | source)
XLA Modules:
  0.0 809.0 jit_solution(5319083072454468865)
XLA Ops:
  26.4 14.4 %collective-permute-done = bf16[96,6,768]{2,0,1:T(8,128)(2,1)S(1)} collective-permute-done((bf16[96,6,768]{2,0,1:T(8,128)(2,1)}, bf16[96,6,768]{2,0,1:T(8,128)(2,1)S(1)}, u32[]{:S(2)}, u32[]{:S(2)}) %collective-permute-start) | collective-permute-done | bytes 884768 | tf_op jit(solution)/shard_map/ppermute | solution.py:35
  47.1 12.8 %collective-permute-done.1 = bf16[96,3072]{1,0:T(8,128)(2,1)S(1)} collective-permute-done((bf16[96,3072]{1,0:T(8,128)(2,1)S(1)}, bf16[96,3072]{1,0:T(8,128)(2,1)S(1)}, u32[]{:S(2)}, u32[]{:S(2)}) %collective-permute-start.1) | collective-permute-done | bytes 589856 | tf_op jit(solution)/shard_map/ppermute | solution.py:35
  61.2 5.8 all-gather.6.cloned.1.call-done.refs_0_.refs_1_.refs_3_
  69.9 11.7 %all-gather.14.cloned.1.call-start = ((), (), s32[]{:S(2)}) async-start(), calls=%async_computation.12 | async-start | bytes 2949120 | tf_op jit(solution)/shard_map/all_gather | solution.py:98
  81.6 40.5 %collective-permute-done.2.refs_1_.refs_2_.refs_4_ = bf16[384,3200]{1,0:T(8,128)(2,1)S(1)} collective-permute-done((bf16[384,3200]{1,0:T(8,128)(2,1)}, bf16[384,3200]{1,0:T(8,128)(2,1)S(1)}, u32[]{:S(2)}, u32[]{:S(2)}) %collective-permute-start.2) | collective-permute-done | bytes 2457632 | tf_op jit(solution)/shard_map/ppermute | solution.py:35
  185.5 8.2 %self_forward.3 = (bf16[512,1024]{1,0:T(8,128)(2,1)}, f32[512,1536]{1,0:T(8,128)}) custom-call(bf16[512,1536]{1,0:T(8,128)(2,1)} %add_norm.3.refs_0_.refs_1_, bf16[384,3200]{1,0:T(8,128)(2,1)} %all-gather.6.cloned.1.call-done.refs_0_.refs_1_.refs_3_, bf16[384,3200]{1,0:T(8,128)(2,1)} %copy-done, ...), custom_call_target="tpu_custom_call" | custom-call | flops 1 | bytes 1 | tf_op jit(solution)/shard_map/self_forward/pallas_call | solution.py:174
  193.7 9.3 %self_forward.4 = (bf16[512,1024]{1,0:T(8,128)(2,1)}, f32[512,1536]{1,0:T(8,128)}) custom-call(bf16[512,1536]{1,0:T(8,128)(2,1)} %add_norm.3.refs_0_.refs_1_, bf16[384,3200]{1,0:T(8,128)(2,1)} %all-gather.6.cloned.1.call-done.refs_0_.refs_1_.refs_3_, bf16[384,3200]{1,0:T(8,128)(2,1)} %copy-done, ...), custom_call_target="tpu_custom_call" | custom-call | flops 1 | bytes 1 | tf_op jit(solution)/shard_map/self_forward/pallas_call | solution.py:174
  203.0 9.1 %self_forward.5 = (bf16[512,1024]{1,0:T(8,128)(2,1)}, bf16[512,1536]{1,0:T(8,128)(2,1)}) custom-call(bf16[512,1536]{1,0:T(8,128)(2,1)} %add_norm.3.refs_0_.refs_1_, bf16[384,3200]{1,0:T(8,128)(2,1)} %all-gather.6.cloned.1.call-done.refs_0_.refs_1_.refs_3_, bf16[384,3200]{1,0:T(8,128)(2,1)} %copy-done, ...), custom_call_target="tpu_custom_call" | custom-call | flops 1 | bytes 1 | tf_op jit(solution)/shard_map/self_forward/pallas_call | solution.py:174
  220.1 28.9 %all-gather.12.cloned.1.call-done.a_ref = bf16[384,3072]{1,0:T(8,128)(2,1)} async-done(((bf16[96,3072]{1,0:T(8,128)(2,1)}), bf16[384,3072]{1,0:T(8,128)(2,1)}) %all-gather.12.cloned.1.call-update) | async-done | bytes 2359312 | tf_op jit(solution)/shard_map/all_gather | solution.py:98
  259.2 15.1 %cross_forward.1 = (bf16[512,1536]{1,0:T(8,128)(2,1)}, bf16[288,1536]{1,0:T(8,128)(2,1)}, bf16[512,1536]{1,0:T(8,128)(2,1)}) custom-call(bf16[512,1536]{1,0:T(8,128)(2,1)} %get-tuple-element.107.n_ref, bf16[288,768]{1,0:T(8,128)(2,1)} %bitcast.112, bf16[576,1536]{1,0:T(8,128)(2,1)} %all-gather.10.cloned.1.call-done.refs_0_.refs_4_.refs_8_, ...), custom_call_target="tpu_custom_call" | custom-call | flops 1 | bytes 1 | tf_op jit(solution)/shard_map/cross_forward/pallas_call | solution.py:174
  285.1 10.1 %collective-permute-done.12 = bf16[256,1536]{1,0:T(8,128)(2,1)S(1)} collective-permute-done((bf16[256,1536]{1,0:T(8,128)(2,1)S(1)}, bf16[256,1536]{1,0:T(8,128)(2,1)S(1)}, u32[]{:S(2)}, u32[]{:S(2)}) %collective-permute-start.12) | collective-permute-done | bytes 786464 | tf_op jit(solution)/shard_map/ppermute | solution.py:35
  305.1 10.3 %collective-permute-done.13 = bf16[256,1536]{1,0:T(8,128)(2,1)} collective-permute-done((bf16[256,1536]{1,0:T(8,128)(2,1)S(1)}, bf16[256,1536]{1,0:T(8,128)(2,1)}, u32[]{:S(2)}, u32[]{:S(2)}) %collective-permute-start.13) | collective-permute-done | bytes 786464 | tf_op jit(solution)/shard_map/ppermute | solution.py:35
  320.9 28.0 %feed_forward.3 = (bf16[384,3072]{1,0:T(8,128)(2,1)}, bf16[384,3072]{1,0:T(8,128)(2,1)}, bf16[1024,1536]{1,0:T(8,128)(2,1)}, bf16[1024,1536]{1,0:T(8,128)(2,1)}) custom-call(bf16[1024,1536]{1,0:T(8,128)(2,1)} %pad_maximum_fusion.x_ref, bf16[1024,1536]{1,0:T(8,128)(2,1)} %pad_maximum_fusion.1.d_ref, ...), custom_call_target="tpu_custom_call" | custom-call | flops 1 | bytes 1 | tf_op jit(solution)/shard_map/feed_forward/pallas_call | solution.py:174
  348.9 28.2 %feed_forward.4 = (bf16[384,3072]{1,0:T(8,128)(2,1)}, bf16[384,3072]{1,0:T(8,128)(2,1)}, bf16[1024,1536]{1,0:T(8,128)(2,1)}, bf16[1024,1536]{1,0:T(8,128)(2,1)}) custom-call(bf16[1024,1536]{1,0:T(8,128)(2,1)} %pad_maximum_fusion.x_ref, bf16[1024,1536]{1,0:T(8,128)(2,1)} %pad_maximum_fusion.1.d_ref, bf16[384,3072]{1,0:T(8,128)(2,1)} %all-gather.12.cloned.1.call-done.a_ref, ...), custom_call_target="tpu_custom_call" | custom-call | flops 1 | bytes 1 | tf_op jit(solution)/shard_map/feed_forward/pallas_call | solution.py:174
  377.1 28.6 %feed_forward.5 = (bf16[384,3072]{1,0:T(8,128)(2,1)}, bf16[384,3072]{1,0:T(8,128)(2,1)}, bf16[1024,1536]{1,0:T(8,128)(2,1)}, bf16[1024,1536]{1,0:T(8,128)(2,1)}) custom-call(bf16[1024,1536]{1,0:T(8,128)(2,1)} %pad_maximum_fusion.x_ref, bf16[1024,1536]{1,0:T(8,128)(2,1)} %pad_maximum_fusion.1.d_ref, bf16[384,3072]{1,0:T(8,128)(2,1)} %all-gather.14.cloned.1.call-done.a_ref, ...), custom_call_target="tpu_custom_call" | custom-call | flops 1 | bytes 1 | tf_op jit(solution)/shard_map/feed_forward/pallas_call | solution.py:174
  416.2 17.7 %collective-permute-done.20 = bf16[256,1536]{1,0:T(8,128)(2,1)S(1)} collective-permute-done((bf16[256,1536]{1,0:T(8,128)(2,1)S(1)}, bf16[256,1536]{1,0:T(8,128)(2,1)S(1)}, u32[]{:S(2)}, u32[]{:S(2)}) %collective-permute-start.20) | collective-permute-done | bytes 786464 | tf_op jit(solution)/shard_map/ppermute | solution.py:35
  437.8 31.2 %collective-permute-done.28 = bf16[384,3072]{1,0:T(8,128)(2,1)S(1)} collective-permute-done((bf16[384,3072]{1,0:T(8,128)(2,1)S(1)}, bf16[384,3072]{1,0:T(8,128)(2,1)S(1)}, u32[]{:S(2)}, u32[]{:S(2)}) %collective-permute-start.28) | collective-permute-done | bytes 2359328 | tf_op jit(solution)/shard_map/ppermute | solution.py:821
  473.4 6.4 norm_back.3
  479.8 25.5 %cross_backward.1 = (bf16[576,3072]{1,0:T(8,128)(2,1)}, bf16[576,3072]{1,0:T(8,128)(2,1)}, bf16[512,1536]{1,0:T(8,128)(2,1)}, bf16[288,768]{1,0:T(8,128)(2,1)}) custom-call(bf16[512,1536]{1,0:T(8,128)(2,1)} %get-tuple-element.128.dc_ref, bf16[512,1536]{1,0:T(8,128)(2,1)} %get-tuple-element.107.n_ref, bf16[288,768]{1,0:T(8,128)(2,1)} %bitcast.113, ...), custom_call_target="tpu_custom_call" | custom-call | flops 1 | bytes 1 | tf_op jit(solution)/shard_map/cross_backward/pallas_call | solution.py:174
  510.1 6.6 norm_back.4
  516.7 7.7 collective-permute-done.34
  538.1 12.4 %self_backward.3 = (bf16[384,2048]{1,0:T(8,128)(2,1)}, bf16[384,2048]{1,0:T(8,128)(2,1)}, f32[512,1536]{1,0:T(8,128)}) custom-call(bf16[512,1536]{1,0:T(8,128)(2,1)} %get-tuple-element.133.refs_0_, bf16[512,1536]{1,0:T(8,128)(2,1)} %add_norm.3.refs_0_.refs_1_, bf16[512,1024]{1,0:T(8,128)(2,1)} %get-tuple-element.135.refs_2_, ...), custom_call_target="tpu_custom_call" | custom-call | flops 1 | bytes 1 | tf_op jit(solution)/shard_map/self_backward/pallas_call | solution.py:174
  550.5 13.7 %self_backward.4 = (bf16[384,2048]{1,0:T(8,128)(2,1)}, bf16[384,2048]{1,0:T(8,128)(2,1)}, f32[512,1536]{1,0:T(8,128)}) custom-call(bf16[512,1536]{1,0:T(8,128)(2,1)} %get-tuple-element.133.refs_0_, bf16[512,1536]{1,0:T(8,128)(2,1)} %add_norm.3.refs_0_.refs_1_, bf16[512,1024]{1,0:T(8,128)(2,1)} %get-tuple-element.134.refs_2_, ...), custom_call_target="tpu_custom_call" | custom-call | flops 1 | bytes 1 | tf_op jit(solution)/shard_map/self_backward/pallas_call | solution.py:174
  564.2 13.1 %self_backward.5 = (bf16[384,2048]{1,0:T(8,128)(2,1)}, bf16[384,2048]{1,0:T(8,128)(2,1)}, bf16[512,1536]{1,0:T(8,128)(2,1)}) custom-call(bf16[512,1536]{1,0:T(8,128)(2,1)} %get-tuple-element.133.refs_0_, bf16[512,1536]{1,0:T(8,128)(2,1)} %add_norm.3.refs_0_.refs_1_, bf16[512,1024]{1,0:T(8,128)(2,1)} %get-tuple-element.138.refs_2_, ...), custom_call_target="tpu_custom_call" | custom-call | flops 1 | bytes 1 | tf_op jit(solution)/shard_map/self_backward/pallas_call | solution.py:174
  593.9 12.2 %collective-permute-done.23 = bf16[576,3072]{1,0:T(8,128)(2,1)} collective-permute-done((bf16[576,3072]{1,0:T(8,128)(2,1)}, bf16[576,3072]{1,0:T(8,128)(2,1)}, u32[]{:S(2)}, u32[]{:S(2)}) %collective-permute-start.23) | collective-permute-done | bytes 3538976 | tf_op jit(solution)/shard_map/ppermute | solution.py:35
  615.6 6.3 norm_back.5
  626.5 19.6 %collective-permute-done.36 = f32[6,768]{1,0:T(8,128)S(1)} collective-permute-done((f32[6,768]{1,0:T(8,128)S(1)}, f32[6,768]{1,0:T(8,128)S(1)}, u32[]{:S(2)}, u32[]{:S(2)}) %collective-permute-start.36) | collective-permute-done | bytes 18464 | tf_op jit(solution)/shard_map/ppermute | solution.py:863
  656.7 12.3 %reduce-scatter.25.cloned.1.call-done = f32[96,128]{1,0:T(8,128)} async-done(((f32[384,128]{1,0:T(8,128)}), f32[96,128]{1,0:T(8,128)}) %reduce-scatter.25.cloned.1.call-update) | async-done | bytes 49168
  694.4 7.4 collective-permute-done.39
  733.6 11.6 %collective-permute-done.38 = bf16[384,1024]{1,0:T(8,128)(2,1)} collective-permute-done((bf16[384,1024]{1,0:T(8,128)(2,1)S(1)}, bf16[384,1024]{1,0:T(8,128)(2,1)}, u32[]{:S(2)}, u32[]{:S(2)}) %collective-permute-start.38) | collective-permute-done | bytes 786464 | tf_op jit(solution)/shard_map/ppermute | solution.py:35
  751.1 17.7 %collective-permute-done.40 = bf16[384,1024]{1,0:T(8,128)(2,1)S(1)} collective-permute-done((bf16[384,1024]{1,0:T(8,128)(2,1)S(1)}, bf16[384,1024]{1,0:T(8,128)(2,1)S(1)}, u32[]{:S(2)}, u32[]{:S(2)}) %collective-permute-start.40) | collective-permute-done | bytes 786464 | tf_op jit(solution)/shard_map/ppermute | solution.py:35
  784.7 12.2 %reduce-scatter.23.cloned.1.call-done = bf16[96,1024]{1,0:T(8,128)(2,1)} async-done(((bf16[384,1024]{1,0:T(8,128)(2,1)}), bf16[96,1024]{1,0:T(8,128)(2,1)}) %reduce-scatter.23.cloned.1.call-update) | async-done | bytes 196624 | tf_op jit(solution)/shard_map/reduce_scatter | solution.py:102
  (387 shorter events, 296.8 us)
Async XLA Ops:
  7.2 59.7 %all-gather.6.cloned.1.call-start = ((), (), s32[]{:S(2)}) async-start(), calls=%async_computation.8 | async-start | bytes 3072000 | tf_op jit(solution)/shard_map/all_gather | solution.py:98
  12.0 140.8 %all-gather.10.cloned.1.call-start = ((), (), s32[]{:S(2)}) async-start(), calls=%async_computation.10 | async-start | bytes 2211840 | tf_op jit(solution)/shard_map/all_gather | solution.py:98
  24.5 187.5 %all-gather.8.cloned.1.call-start = ((), (), s32[]{:S(2)}) async-start(), calls=%async_computation.9 | async-start | bytes 5898240 | tf_op jit(solution)/shard_map/all_gather | solution.py:98
  61.1 188.0 %all-gather.12.cloned.1.call-start = ((), (), s32[]{:S(2)}) async-start(), calls=%async_computation.11 | async-start | bytes 2949120 | tf_op jit(solution)/shard_map/all_gather | solution.py:98
  66.9 55.3 %collective-permute-start.2 = (bf16[384,3200]{1,0:T(8,128)(2,1)}, bf16[384,3200]{1,0:T(8,128)(2,1)S(1)}, u32[]{:S(2)}, u32[]{:S(2)}) collective-permute-start(bf16[384,3200]{1,0:T(8,128)(2,1)} %all-gather.6.cloned.1.call-done.refs_0_.refs_1_.refs_3_), channel_id=1, source_target_pairs={{0,4},{4,0},{1,5},{5,1},{2,6},{6,2},{3,7},{7,3},{8,12},{12,8},{9,1... | collective-permute-start | bytes 7372808 | tf_op jit(solution)/shard_map/ppermute | solution.py:35
  68.4 55.3 %collective-permute-start.3 = (bf16[384,3200]{1,0:T(8,128)(2,1)}, bf16[384,3200]{1,0:T(8,128)(2,1)}, u32[]{:S(2)}, u32[]{:S(2)}) collective-permute-start(bf16[384,3200]{1,0:T(8,128)(2,1)} %all-gather.6.cloned.1.call-done.refs_0_.refs_1_.refs_3_), channel_id=1, source_target_pairs={{0,2},{2,0},{1,3},{3,1},{4,6},{6,4},{5,7},{7,5},{8,10},{10,8},{9,1... | collective-permute-start | bytes 7372808 | tf_op jit(solution)/shard_map/ppermute | solution.py:35
  69.9 229.9 %all-gather.14.cloned.1.call-start = ((), (), s32[]{:S(2)}) async-start(), calls=%async_computation.12 | async-start | bytes 2949120 | tf_op jit(solution)/shard_map/all_gather | solution.py:98
  123.7 35.6 %collective-permute-start.5 = (bf16[384,2048]{1,0:T(8,128)(2,1)}, bf16[384,2048]{1,0:T(8,128)(2,1)}, u32[]{:S(2)}, u32[]{:S(2)}) collective-permute-start(bf16[384,2048]{1,0:T(8,128)(2,1)} %slice.562), channel_id=1, source_target_pairs={{0,2},{2,0},{1,3},{3,1},{4,6},{6,4},{5,7},{7,5},{8,10},{10,8},{9,1... | collective-permute-start | bytes 4718600 | tf_op jit(solution)/shard_map/ppermute | solution.py:35
  152.7 63.2 %collective-permute-start.7 = (bf16[576,1536]{1,0:T(8,128)(2,1)}, bf16[576,1536]{1,0:T(8,128)(2,1)S(1)}, u32[]{:S(2)}, u32[]{:S(2)}) collective-permute-start(bf16[576,1536]{1,0:T(8,128)(2,1)} %all-gather.10.cloned.1.call-done.refs_0_.refs_4_.refs_8_), channel_id=1, source_target_pairs={{0,4},{4,0},{1,5},{5,1},{2,6},{6,2},{3,7},{7,3},{8,12},{12,8},{9,1... | collective-permute-start | bytes 5308424 | tf_op jit(solution)/shard_map/ppermute | solution.py:35
  159.3 55.4 %collective-permute-start.8 = (bf16[576,1536]{1,0:T(8,128)(2,1)}, bf16[576,1536]{1,0:T(8,128)(2,1)S(1)}, u32[]{:S(2)}, u32[]{:S(2)}) collective-permute-start(bf16[576,1536]{1,0:T(8,128)(2,1)} %all-gather.10.cloned.1.call-done.refs_0_.refs_4_.refs_8_), channel_id=1, source_target_pairs={{0,2},{2,0},{1,3},{3,1},{4,6},{6,4},{5,7},{7,5},{8,10},{10,8},{9,1... | collective-permute-start | bytes 5308424 | tf_op jit(solution)/shard_map/ppermute | solution.py:35
  212.1 41.4 %collective-permute-start.6 = (bf16[512,1536]{1,0:T(8,128)(2,1)}, bf16[512,1536]{1,0:T(8,128)(2,1)}, u32[]{:S(2)}, u32[]{:S(2)}) collective-permute-start(bf16[512,1536]{1,0:T(8,128)(2,1)} %get-tuple-element.105.refs_2_), channel_id=1, source_target_pairs={{0,1},{1,0},{2,3},{3,2},{4,5},{5,4},{6,7},{7,6},{8,9},{9,8},{10,11... | collective-permute-start | bytes 4718600 | tf_op jit(solution)/shard_map/ppermute | solution.py:45
  214.6 378.0 %reduce-scatter.11.cloned.1.call-start = ((), (), s32[]{:S(2)}) async-start(), calls=%async_computation.13 | async-start | bytes 2949120 | tf_op jit(solution)/shard_map/reduce_scatter | solution.py:102
  215.9 33.2 %collective-permute-start.10 = (bf16[576,1024]{1,0:T(8,128)(2,1)}, bf16[576,1024]{1,0:T(8,128)(2,1)}, u32[]{:S(2)}, u32[]{:S(2)}) collective-permute-start(bf16[576,1024]{1,0:T(8,128)(2,1)} %slice.579), channel_id=1, source_target_pairs={{0,4},{4,0},{1,5},{5,1},{2,6},{6,2},{3,7},{7,3},{8,12},{12,8},{9,1... | collective-permute-start | bytes 3538952 | tf_op jit(solution)/shard_map/ppermute | solution.py:35
  219.7 38.7 %collective-permute-start.9 = (bf16[576,512]{1,0:T(8,128)(2,1)}, bf16[576,512]{1,0:T(8,128)(2,1)S(1)}, u32[]{:S(2)}, u32[]{:S(2)}) collective-permute-start(bf16[576,512]{1,0:T(8,128)(2,1)} %slice.578), channel_id=1, source_target_pairs={{0,2},{2,0},{1,3},{3,1},{4,6},{6,4},{5,7},{7,5},{8,10},{10,8},{9,1... | collective-permute-start | bytes 1769480 | tf_op jit(solution)/shard_map/ppermute | solution.py:35
  249.1 53.3 %collective-permute-start.15 = (bf16[384,3072]{1,0:T(8,128)(2,1)}, bf16[384,3072]{1,0:T(8,128)(2,1)}, u32[]{:S(2)}, u32[]{:S(2)}) collective-permute-start(bf16[384,3072]{1,0:T(8,128)(2,1)} %all-gather.12.cloned.1.call-done.a_ref), channel_id=1, source_target_pairs={{0,4},{4,0},{1,5},{5,1},{2,6},{6,2},{3,7},{7,3},{8,12},{12,8},{9,1... | collective-permute-start | bytes 7077896 | tf_op jit(solution)/shard_map/ppermute | solution.py:35
  302.3 74.7 %collective-permute-start.17 = (bf16[384,3072]{1,0:T(8,128)(2,1)}, bf16[384,3072]{1,0:T(8,128)(2,1)}, u32[]{:S(2)}, u32[]{:S(2)}) collective-permute-start(bf16[384,3072]{1,0:T(8,128)(2,1)} %all-gather.14.cloned.1.call-done.a_ref), channel_id=1, source_target_pairs={{0,4},{4,0},{1,5},{5,1},{2,6},{6,2},{3,7},{7,3},{8,12},{12,8},{9,1... | collective-permute-start | bytes 7077896 | tf_op jit(solution)/shard_map/ppermute | solution.py:35
  415.7 53.4 %collective-permute-start.28 = (bf16[384,3072]{1,0:T(8,128)(2,1)S(1)}, bf16[384,3072]{1,0:T(8,128)(2,1)S(1)}, u32[]{:S(2)}, u32[]{:S(2)}) collective-permute-start(bf16[384,3072]{1,0:T(8,128)(2,1)S(1)} %copy-done.46), channel_id=1, source_target_pairs={{0,4},{4,0},{1,5},{5,1},{2,6},{6,2},{3,7},{7,3},{8,12},{12,8},{9,1... | collective-permute-start | bytes 7077896 | tf_op jit(solution)/shard_map/ppermute | solution.py:821
  471.4 185.3 %reduce-scatter.13.cloned.1.call-start = ((), (), s32[]{:S(2)}) async-start(), calls=%async_computation.14 | async-start | bytes 2949120 | tf_op jit(solution)/shard_map/reduce_scatter | solution.py:102
  471.5 52.9 %collective-permute-start.34 = (bf16[384,3072]{1,0:T(8,128)(2,1)}, bf16[384,3072]{1,0:T(8,128)(2,1)}, u32[]{:S(2)}, u32[]{:S(2)}) collective-permute-start(bf16[384,3072]{1,0:T(8,128)(2,1)} %get-tuple-element.167), channel_id=1, source_target_pairs={{0,4},{4,0},{1,5},{5,1},{2,6},{6,2},{3,7},{7,3},{8,12},{12,8},{9,1... | collective-permute-start | bytes 7077896 | tf_op jit(solution)/shard_map/ppermute | solution.py:821
  528.6 128.1 %reduce-scatter.15.cloned.1.call-start = ((), (), s32[]{:S(2)}) async-start(), calls=%async_computation.15 | async-start | bytes 2949120 | tf_op jit(solution)/shard_map/reduce_scatter | solution.py:102
  528.6 52.0 %collective-permute-start.35 = (bf16[384,3072]{1,0:T(8,128)(2,1)}, bf16[384,3072]{1,0:T(8,128)(2,1)}, u32[]{:S(2)}, u32[]{:S(2)}) collective-permute-start(bf16[384,3072]{1,0:T(8,128)(2,1)} %get-tuple-element.170), channel_id=1, source_target_pairs={{0,4},{4,0},{1,5},{5,1},{2,6},{6,2},{3,7},{7,3},{8,12},{12,8},{9,1... | collective-permute-start | bytes 7077896 | tf_op jit(solution)/shard_map/ppermute | solution.py:821
  529.2 76.9 %collective-permute-start.23 = (bf16[576,3072]{1,0:T(8,128)(2,1)}, bf16[576,3072]{1,0:T(8,128)(2,1)}, u32[]{:S(2)}, u32[]{:S(2)}) collective-permute-start(bf16[576,3072]{1,0:T(8,128)(2,1)} %get-tuple-element.145), channel_id=1, source_target_pairs={{0,2},{2,0},{1,3},{3,1},{4,6},{6,4},{5,7},{7,5},{8,10},{10,8},{9,1... | collective-permute-start | bytes 10616840 | tf_op jit(solution)/shard_map/ppermute | solution.py:35
  538.0 48.5 %collective-permute-start.18 = (bf16[512,1536]{1,0:T(8,128)(2,1)S(1)}, bf16[512,1536]{1,0:T(8,128)(2,1)}, u32[]{:S(2)}, u32[]{:S(2)}) collective-permute-start(bf16[512,1536]{1,0:T(8,128)(2,1)S(1)} %slice.717), channel_id=1, source_target_pairs={{0,1},{1,0},{2,3},{3,2},{4,5},{5,4},{6,7},{7,6},{8,9},{9,8},{10,11... | collective-permute-start | bytes 4718600 | tf_op jit(solution)/shard_map/ppermute | solution.py:45
  584.6 84.4 %reduce-scatter.25.cloned.1.call-start = ((), (), s32[]{:S(2)}) async-start(), calls=%async_computation.20 | async-start | bytes 245760
  609.3 40.6 %collective-permute-start.31 = (bf16[576,1536]{1,0:T(8,128)(2,1)}, bf16[576,1536]{1,0:T(8,128)(2,1)}, u32[]{:S(2)}, u32[]{:S(2)}) collective-permute-start(bf16[576,1536]{1,0:T(8,128)(2,1)} %add_convert_fusion.4), channel_id=1, source_target_pairs={{0,4},{4,0},{1,5},{5,1},{2,6},{6,2},{3,7},{7,3},{8,12},{12,8},{9,1... | collective-permute-start | bytes 5308424 | tf_op jit(solution)/shard_map/ppermute | solution.py:35
  612.1 36.2 %collective-permute-start.24 = (bf16[384,2048]{1,0:T(8,128)(2,1)}, bf16[384,2048]{1,0:T(8,128)(2,1)}, u32[]{:S(2)}, u32[]{:S(2)}) collective-permute-start(bf16[384,2048]{1,0:T(8,128)(2,1)} %get-tuple-element.146), channel_id=1, source_target_pairs={{0,2},{2,0},{1,3},{3,1},{4,6},{6,4},{5,7},{7,5},{8,10},{10,8},{9,1... | collective-permute-start | bytes 4718600 | tf_op jit(solution)/shard_map/ppermute | solution.py:35
  648.3 41.7 %collective-permute-start.25 = (bf16[384,2048]{1,0:T(8,128)(2,1)}, bf16[384,2048]{1,0:T(8,128)(2,1)}, u32[]{:S(2)}, u32[]{:S(2)}) collective-permute-start(bf16[384,2048]{1,0:T(8,128)(2,1)} %get-tuple-element.147), channel_id=1, source_target_pairs={{0,2},{2,0},{1,3},{3,1},{4,6},{6,4},{5,7},{7,5},{8,10},{10,8},{9,1... | collective-permute-start | bytes 4718600 | tf_op jit(solution)/shard_map/ppermute | solution.py:35
  649.9 43.0 %collective-permute-start.32 = (bf16[384,2048]{1,0:T(8,128)(2,1)}, bf16[384,2048]{1,0:T(8,128)(2,1)}, u32[]{:S(2)}, u32[]{:S(2)}) collective-permute-start(bf16[384,2048]{1,0:T(8,128)(2,1)} %get-tuple-element.162), channel_id=1, source_target_pairs={{0,4},{4,0},{1,5},{5,1},{2,6},{6,2},{3,7},{7,3},{8,12},{12,8},{9,1... | collective-permute-start | bytes 4718600 | tf_op jit(solution)/shard_map/ppermute | solution.py:35
  652.2 71.3 %reduce-scatter.17.cloned.1.call-start = ((), (), s32[]{:S(2)}) async-start(), calls=%async_computation.16 | async-start | bytes 2211840 | tf_op jit(solution)/shard_map/reduce_scatter | solution.py:102
  670.6 77.4 %reduce-scatter.19.cloned.1.call-start = ((), (), s32[]{:S(2)}) async-start(), calls=%async_computation.17 | async-start | bytes 983040 | tf_op jit(solution)/shard_map/reduce_scatter | solution.py:102
  723.5 47.8 %reduce-scatter.21.cloned.1.call-start = ((), (), s32[]{:S(2)}) async-start(), calls=%async_computation.18 | async-start | bytes 983040 | tf_op jit(solution)/shard_map/reduce_scatter | solution.py:102
  748.0 48.9 %reduce-scatter.23.cloned.1.call-start = ((), (), s32[]{:S(2)}) async-start(), calls=%async_computation.19 | async-start | bytes 983040 | tf_op jit(solution)/shard_map/reduce_scatter | solution.py:102
  (70 other events, 654.2 us)
Sparse Core Ops, SparseCore 0:
  12.1 54.7 all-gather.5
  69.1 39.0 all-gather.9
  110.4 88.2 all-gather.7
  200.1 48.9 all-gather.11
  250.5 49.2 all-gather.13
  471.6 46.1 reduce-scatter.10
  528.7 46.1 reduce-scatter.12
  584.7 46.1 reduce-scatter.14
  652.3 16.6 reduce-scatter.24
  671.3 36.6 reduce-scatter.16
  723.7 22.3 reduce-scatter.18
  748.7 22.5 reduce-scatter.20
  774.2 22.5 reduce-scatter.22

commit v3 on v2

--- a/solution.py
+++ b/solution.py
@@ -136,18 +136,21 @@
 
 
 class Scatter:
-    def __init__(self, order):
-        self.order = order
-
-    def first(self, sent, kept):
-        self.kept, self.got = kept, swap(sent, AXIS[self.order[0]])
+    def __init__(self, order, grads):
+        self.order, self.grads = order, grads
+
+    def first_far(self):
+        self.far = (self.grads[2], swap(self.grads[3], AXIS[self.order[0]]))
         return self
 
+    def first_near(self):
+        self.near = (self.grads[0], swap(self.grads[1], AXIS[self.order[0]]))
+        return self
+
     def second(self):
-        n = self.kept.shape[1] // 2
-        far = (self.kept[:, n:].astype(F32) + self.got[:, n:].astype(F32)).astype(BF16)
+        far = (self.far[0].astype(F32) + self.far[1].astype(F32)).astype(BF16)
         moved = swap(far, AXIS[self.order[1]])
-        near = self.kept[:, :n].astype(F32) + self.got[:, :n].astype(F32)
+        near = self.near[0].astype(F32) + self.near[1].astype(F32)
         self.kept = (near + moved.astype(F32)).astype(BF16)
         return self
 
@@ -363,22 +366,48 @@
     )
 
 
-def self_forward(n, pieces, tables, total, slots, last):
+def grouped_specs(pieces, n):
+    out = []
+    for p in PIECES:
+        for a, begin, end in pieces[p]:
+            lo, count = begin // n, (end - begin) // n
+            pick_block = functools.partial(
+                lambda lo, count, j: (0, jnp.clip(j - lo, 0, count - 1)), lo, count
+            )
+            out.append((a, pl.BlockSpec((a.shape[0], n), pick_block), lo, lo + count))
+    return out
+
+
+def load_grouped(found, refs, w, rows):
+    j = pl.program_id(0)
+    at = -rows
+    for (_, _, lo, hi), r in zip(found, refs):
+        if lo == 0:
+            at += rows
+        target = slice(at, at + rows)
+
+        @pl.when((j >= lo) & (j < hi))
+        def _(r=r, target=target):
+            w[target, :] = r[...]
+
+
+def constant(array):
+    nd = array.ndim
+    return pl.BlockSpec(array.shape, lambda *_: (0,) * nd, pipeline_mode=pl.Buffered(1))
+
+
+def self_forward(n, pieces, tables, slots, groups):
     rows, width = n.shape
     length = rows // slots
     q4 = width // 4
     cols = 4 * GW
+    found = grouped_specs(pieces, cols)
 
     def body(*refs):
-        n_ref, w_refs, tabs = refs[0], refs[1:5], refs[5:8]
-        k = 8
-        total_ref = None
-        if total is not None:
-            total_ref = refs[8]
-            k = 9
-        keep_ref, part_ref, w, raw = refs[k:]
-        for i, r in enumerate(w_refs):
-            w[i * q4 : (i + 1) * q4, :] = r[...]
+        n_ref, w_refs, tabs = refs[0], refs[1 : 1 + len(found)], refs[1 + len(found) : 4 + len(found)]
+        keep_ref, part_ref, w, raw, total = refs[4 + len(found) :]
+        j = pl.program_id(0)
+        load_grouped(found, w_refs, w, q4)
         raw[...] = nn(n_ref[...], w[:, : 3 * GW])
         cos, sin_a, sin_b = (r[...] for r in tabs)
         for l in range(slots):
@@ -391,22 +420,34 @@
             keep_ref[at, 2 * GW : 3 * GW] = v
             keep_ref[at, 3 * GW :] = attention(q, key, v, None).astype(BF16)
         part = nt(keep_ref[:, 3 * GW :], w[:, 3 * GW :])
-        if total_ref is not None:
-            part = part + total_ref[...]
-        part_ref[...] = part.astype(part_ref.dtype)
-
-    ins = [n] + piece_args(pieces) + list(tables) + ([] if total is None else [total])
-    specs = [full(n)] + piece_specs(pieces, cols) + [full(a) for a in tables]
-    specs += [] if total is None else [full(total)]
-    outs = [shape((rows, cols), BF16), shape((rows, width), BF16 if last else F32)]
+
+        @pl.when(j == 0)
+        def _():
+            total[...] = part
+
+        @pl.when(j > 0)
+        def _():
+            total[...] += part
+
+        @pl.when(j == pl.num_programs(0) - 1)
+        def _():
+            part_ref[...] = total[...].astype(BF16)
+
+    ins = [n] + [f[0] for f in found] + list(tables)
+    specs = [constant(n)] + [f[1] for f in found] + [constant(a) for a in tables]
+    outs = [shape((rows, groups * cols), BF16), shape((rows, width), BF16)]
     return call(
         body,
         outs,
         ins,
         specs,
-        [full(o) for o in outs],
-        scratch=[pltpu.VMEM((width, cols), BF16), pltpu.VMEM((rows, 3 * GW), F32)],
-        flops=2 * rows * width * cols,
+        [pl.BlockSpec((rows, cols), lambda j: (0, j)), full(outs[1])],
+        grid=(groups,),
+        scratch=[
+            pltpu.VMEM((width, cols), BF16),
+            pltpu.VMEM((rows, 3 * GW), F32),
+            pltpu.VMEM((rows, width), F32),
+        ],
         name="self_forward",
     )
 
@@ -480,12 +521,16 @@
     )
 
 
-def feed_forward(x, d, near_w, far_w, blocks):
+def feed_forward(x, d, near_w, far_w, blocks, joint):
     rows, width = x.shape
     q4 = width // 4
     cols = 6 * UB
 
-    def body(x_ref, d_ref, a_ref, b_ref, keep_ref, send_ref, dn_ref, y_ref, w, dn, y):
+    def body(*refs):
+        if not joint:
+            x_ref, d_ref, a_ref, b_ref, keep_ref, send_ref, dn_ref, y_ref, w, dn, y = refs
+        else:
+            x_ref, d_ref, a_ref, b_ref, keep_ref, dn_ref, y_ref, w, dn, y = refs
         j = pl.program_id(0)
         for rx in range(2):
             for ry, r in enumerate((a_ref, b_ref)):
@@ -500,12 +545,17 @@
         dg = (dh * upper * (sig * (1.0 + gate * (1.0 - sig)))).astype(BF16)
         du = (dh * silu).astype(BF16)
         dgu = jnp.concatenate([dg, du], axis=1)
-        for at, ref in ((0, keep_ref), (1, send_ref)):
-            for rx in range(2):
-                c0 = (2 * rx + at) * q4
-                lo = rx * 3 * UB
-                ref[:, lo : lo + 2 * UB] = tn(x_ref[:, c0 : c0 + q4], dgu).astype(BF16)
-                ref[:, lo + 2 * UB : lo + 3 * UB] = tn(d_ref[:, c0 : c0 + q4], hidden).astype(BF16)
+        for rx in range(2):
+            for ref, right, lo, n in ((x_ref, dgu, 0, 2 * UB), (d_ref, hidden, 2 * UB, UB)):
+                c0 = 2 * rx * q4
+                at = slice(rx * 3 * UB + lo, rx * 3 * UB + lo + n)
+                near = tn(ref[:, c0 : c0 + q4], right)
+                far = tn(ref[:, c0 + q4 : c0 + 2 * q4], right)
+                keep_ref[:, at] = near.astype(BF16)
+                if joint:
+                    keep_ref[:, cols + at.start : cols + at.stop] = far.astype(BF16)
+                else:
+                    send_ref[:, at] = far.astype(BF16)
         more_dn = nt(dgu, w[:, : 2 * UB])
         more_y = nt(hidden, w[:, 2 * UB :])
 
@@ -530,13 +580,20 @@
         for _, i in (near_w, far_w)
     ]
     ins = [x, d, near_w[0], far_w[0]]
-    outs = [shape((q4, blocks * cols), BF16)] * 2 + [shape((rows, width), BF16)] * 2
+    specs = [constant(x), constant(d)] + from_w
+    if joint:
+        outs = [shape((q4, 2 * blocks * cols), BF16)]
+        out_specs = [pl.BlockSpec((q4, 2 * cols), lambda j: (0, j))]
+    else:
+        outs = [shape((q4, blocks * cols), BF16)] * 2
+        out_specs = [block, block]
+    sums = [shape((rows, width), BF16)] * 2
     return call(
         body,
-        outs,
+        outs + sums,
         ins,
-        [full(x), full(d)] + from_w,
-        [block, block] + [full(o) for o in outs[2:]],
+        specs,
+        out_specs + [full(o) for o in sums],
         grid=(blocks,),
         scratch=[
             pltpu.VMEM((width, 3 * UB), BF16),
@@ -548,17 +605,17 @@
     )
 
 
-def split_rows(left_ref, right, first, n, keep_ref, send_ref, lo=0, outer=1, at_row=0):
+def split_rows(left_ref, right, first, grads, cols, outer=1, at_row=0):
     q = left_ref.shape[1] // 4
-    run = keep_ref.shape[0] // outer
+    run = grads[0].shape[0] // outer
     part = q // outer
     for rx, ry in PIECES:
         g = tn(left_ref[:, (2 * rx + ry) * q : (2 * rx + ry + 1) * q], right).astype(BF16)
         goes, other = (rx, ry) if first == "x" else (ry, rx)
-        ref = send_ref if goes else keep_ref
-        cols = slice(other * n + lo, other * n + lo + right.shape[1])
         for o in range(outer):
-            ref[o * run + at_row : o * run + at_row + part, cols] = g[o * part : (o + 1) * part, :]
+            grads[2 * other + goes][o * run + at_row : o * run + at_row + part, cols] = g[
+                o * part : (o + 1) * part, :
+            ]
 
 
 def cross_backward(dc, n, ctx, keep, pair_rows, pieces, slots, cond, groups, block, pair_block, first):
@@ -569,7 +626,7 @@
 
     def body(dc_ref, n_ref, ctx_ref, keep_in, pair_in, *refs):
         w_refs = refs[: 4 * groups]
-        g_keep, g_send, dn_ref, dctx_ref, w, wp, do, dcq, dpair = refs[4 * groups :]
+        grads, (dn_ref, dctx_ref, w, wp, do, dcq, dpair) = refs[4 * groups : 4 * groups + 4], refs[4 * groups + 4 :]
         lane = lax.broadcasted_iota(jnp.int32, (1, keys), 1)
         bias = jnp.where(lane < cond, 0.0, -1e30).astype(F32)
         dn = None
@@ -590,9 +647,9 @@
                 dpair[at_k, at_o] = c.astype(BF16)
             more = nt(dcq[...], w[:, at_q])
             dn = more if dn is None else dn + more
-            split_rows(n_ref, dcq[...], first, cols, g_keep, g_send, 2 * j * GW, outer)
-            split_rows(dc_ref, keep_in[:, at_o], first, cols, g_keep, g_send, (2 * j + 1) * GW, outer)
-            split_rows(ctx_ref, dpair[:, at_j], first, cols, g_keep, g_send, 2 * j * GW, outer, block)
+            split_rows(n_ref, dcq[...], first, grads, at_q, outer)
+            split_rows(dc_ref, keep_in[:, at_o], first, grads, at_o, outer)
+            split_rows(ctx_ref, dpair[:, at_j], first, grads, at_j, outer, block)
         dn_ref[...] = dn.astype(BF16)
         dctx_ref[...] = nt(dpair[...], wp[...]).astype(BF16)
 
@@ -600,12 +657,7 @@
     ins = [dc, n, ctx, keep, pair_rows] + more_ins
     specs = [full(a) for a in ins[:5]] + more_specs
     grad_rows = outer * (block + pair_block)
-    outs = [
-        shape((grad_rows, 2 * cols), BF16),
-        shape((grad_rows, 2 * cols), BF16),
-        shape((rows, width), BF16),
-        shape(ctx.shape, BF16),
-    ]
+    outs = [shape((grad_rows, cols), BF16)] * 4 + [shape((rows, width), BF16), shape(ctx.shape, BF16)]
     return call(
         body,
         outs,
@@ -624,22 +676,20 @@
     )
 
 
-def self_backward(da, n, keep, pieces, tables, total, slots, first, last):
+def self_backward(da, n, keep, pieces, tables, slots, groups, firsts):
     rows, width = n.shape
     length = rows // slots
     q4 = width // 4
     cols = 4 * GW
+    found = grouped_specs(pieces, cols)
 
     def body(*refs):
-        da_ref, n_ref, keep_in, w_refs, tabs = refs[0], refs[1], refs[2], refs[3:7], refs[7:10]
-        k = 10
-        total_ref = None
-        if total is not None:
-            total_ref = refs[10]
-            k = 11
-        g_keep, g_send, dn_ref, w, do, dt = refs[k:]
-        for i, r in enumerate(w_refs):
-            w[i * q4 : (i + 1) * q4, :] = r[...]
+        da_ref, n_ref, keep_in = refs[:3]
+        w_refs, tabs = refs[3 : 3 + len(found)], refs[3 + len(found) : 6 + len(found)]
+        grads = [refs[6 + len(found) : 10 + len(found)], refs[10 + len(found) : 14 + len(found)]]
+        dn_ref, w, do, dt, total = refs[14 + len(found) :]
+        j = pl.program_id(0)
+        load_grouped(found, w_refs, w, q4)
         do[...] = nn(da_ref[...], w[:, 3 * GW :]).astype(BF16)
         cos, sin_a, sin_b = (r[...] for r in tabs)
         for l in range(slots):
@@ -650,33 +700,41 @@
             dt[at, :GW] = turn(dq, cos, -sin_a, -sin_b).astype(BF16)
             dt[at, GW : 2 * GW] = turn(dk, cos, -sin_a, -sin_b).astype(BF16)
             dt[at, 2 * GW :] = dv.astype(BF16)
-        split_rows(n_ref, dt[...], first, cols, g_keep, g_send)
-        split_rows(da_ref, keep_in[:, 3 * GW :], first, cols, g_keep, g_send, 3 * GW)
+        split_rows(n_ref, dt[:, : 2 * GW], firsts[0], grads[0], slice(0, 2 * GW))
+        split_rows(n_ref, dt[:, 2 * GW :], firsts[1], grads[1], slice(0, GW))
+        split_rows(da_ref, keep_in[:, 3 * GW :], firsts[1], grads[1], slice(GW, 2 * GW))
         dn = nt(dt[...], w[:, : 3 * GW])
-        if total_ref is not None:
-            dn = dn + total_ref[...]
-        dn_ref[...] = dn.astype(dn_ref.dtype)
-
-    ins = [da, n, keep] + piece_args(pieces) + list(tables) + ([] if total is None else [total])
-    specs = [full(da), full(n), full(keep)] + piece_specs(pieces, cols)
-    specs += [full(a) for a in tables] + ([] if total is None else [full(total)])
-    outs = [
-        shape((q4, 2 * cols), BF16),
-        shape((q4, 2 * cols), BF16),
-        shape((rows, width), BF16 if last else F32),
-    ]
+
+        @pl.when(j == 0)
+        def _():
+            total[...] = dn
+
+        @pl.when(j > 0)
+        def _():
+            total[...] += dn
+
+        @pl.when(j == pl.num_programs(0) - 1)
+        def _():
+            dn_ref[...] = total[...].astype(BF16)
+
+    ins = [da, n, keep] + [f[0] for f in found] + list(tables)
+    step = pl.BlockSpec((rows, cols), lambda j: (0, j))
+    specs = [constant(da), constant(n), step] + [f[1] for f in found] + [constant(a) for a in tables]
+    outs = [shape((q4, groups * cols // 2), BF16)] * 8 + [shape((rows, width), BF16)]
+    grad = pl.BlockSpec((q4, cols // 2), lambda j: (0, j))
     return call(
         body,
         outs,
         ins,
         specs,
-        [full(o) for o in outs],
+        [grad] * 8 + [full(outs[8])],
+        grid=(groups,),
         scratch=[
             pltpu.VMEM((width, cols), BF16),
             pltpu.VMEM((rows, GW), BF16),
             pltpu.VMEM((rows, 3 * GW), BF16),
+            pltpu.VMEM((rows, width), F32),
         ],
-        flops=4 * rows * width * cols,
         name="self_backward",
     )
 
@@ -685,7 +743,8 @@
 CROSS_SPLIT = 1
 FF_BLOCKS = (2, 2, 2)
 FF_EARLY_Y = (True, False, False)
-ATTN_SCATTER = ("xyz", "xyz", "yxz")
+FF_JOINT = (True, True, False)
+ATTN_SCATTER = ("yxz", "xyz")
 CROSS_SCATTER = "xyz"
 
 
@@ -739,9 +798,11 @@
     def from_core(mine, other):
         return jnp.concatenate([pick(t, mine, other), pick(t, other, mine)], axis=0)
 
-    def spread(value):
+    def spread(value, *others):
         mine, other = by_core(value)
         far = flip_half(swap(mine, "C"))
+        if others:
+            far = hold(far, *others)
         return jnp.concatenate([mine, far, other, swap(far, T)], axis=0)
 
     def collect(parts):
@@ -801,60 +862,59 @@
     tables = rotary_tables(length)
 
     (n1,) = add_norm(start, None, None, norms, 0)
-    keep_one, part = [], None
-    for j in range(groups):
-        keep, part = self_forward(n1, columns(attn_w, j * 4 * GW, 4 * GW), tables, part, slots, j == groups - 1)
-        keep_one.append(keep)
-    part = hold(part, ff_w[0][0][0])
+    keep_one, part = self_forward(n1, attn_w, tables, slots, groups)
     n2, h1 = add_norm(start, part, swap(part, T), norms, 1)
     keep_two, pair_rows, part = cross_forward(n2, ctx, cross_w, slots, cond, groups, block, pair_block)
-    part = hold(part, ff_w[1][0][0])
+    part = hold(part, ff_w[0][0][0], ff_w[1][0][0])
     n3, h2 = add_norm(h1, part, swap(part, T), norms, 2)
-    n3_all = spread(n3)
-
-    n3_all = hold(n3_all, *[w[0][0] for w in ff_w], ff_w[1][1][0])
+    n3_all = spread(n3, ff_w[1][1][0])
+
+    n3_all = hold(n3_all, *[w[0][0] for w in ff_w])
     g_ff, dn3, y = [], [], []
     for i, blocks in enumerate(FF_BLOCKS):
-        keep, send, dn_part, y_part = feed_forward(n3_all, grad_all, ff_w[i][0], ff_w[i][1], blocks)
+        *grads, dn_part, y_part = feed_forward(
+            n3_all, grad_all, ff_w[i][0], ff_w[i][1], blocks, FF_JOINT[i]
+        )
         dn3.append(dn_part)
         y.append(y_part)
-        g_ff.append((keep, lax.ppermute(send, "B", FLIP)))
+        if FF_JOINT[i]:
+            g_ff.append(scatter_z(grads[0]).reshape(block, blocks, 2, 6 * UB))
+        else:
+            g_ff.append((grads[0], lax.ppermute(grads[1], "B", FLIP)))
     dn3 = collect(dn3).astype(BF16)
+
+    out_half = collect(y) + by_core(h2)[0]
+    out_half = (out_half * pick(t, live_rows[:half], live_rows[half:])).astype(BF16)
+    out_half = lax.optimization_barrier(out_half)
     dn3 = from_core(dn3, swap(dn3, T))
 
     def ff_sum(keep, got):
         return scatter_z((keep.astype(F32) + got.astype(F32)).astype(BF16))
 
-    g_done = [ff_sum(hold(g_ff[0][0], dn3), g_ff[0][1])]
-
     dh2, dc, sums_three = norm_back(dn3, jnp.zeros_like(dn3), h2, grad_top, norms, 2)
-    g_keep, g_send, dn2, dctx = cross_backward(
+    dc = hold(dc, out_half)
+    *g_cross, dn2, dctx = cross_backward(
         dc, n2, ctx, keep_two, pair_rows, cross_w, slots, cond, groups, block, pair_block, CROSS_SCATTER[0]
     )
-    g_cross = Scatter(CROSS_SCATTER).first(g_send, g_keep)
+    g_cross = Scatter(CROSS_SCATTER, g_cross).first_far().first_near()
     dh1, da, sums_two = norm_back(dn2, swap(dn2, T), h1, dh2, norms, 1)
-    g_done.append(ff_sum(hold(g_ff[1][0], da), g_ff[1][1]))
-    g_attn, sends, dn1 = [], [], None
-    for j in range(groups):
-        g_keep, g_send, dn1 = self_backward(
-            da,
-            n1,
-            keep_one[j],
-            columns(attn_w, j * 4 * GW, 4 * GW),
-            tables,
-            dn1,
-            slots,
-            ATTN_SCATTER[j][0],
-            j == groups - 1,
-        )
-        sends.append((g_send, g_keep))
-    g_cross.kept = hold(g_cross.kept, dn1)
+    da = hold(da, g_ff[2][1])
+    mixed = restore(from_core(out_half, swap(hold(out_half, da), T)), b, c, outer)
+    *g_attn, dn1 = self_backward(
+        da, n1, keep_one, attn_w, tables, slots, groups, [order[0] for order in ATTN_SCATTER]
+    )
+    g_done = []
+    for g in g_ff[:2]:
+        far = lax.ppermute(hold(g[:, :, 1], dc), "B", FLIP)
+        g_done.append((g[:, :, 0].astype(F32) + far.astype(F32)).astype(BF16).reshape(block, -1))
+    g_done.append(ff_sum(hold(g_ff[2][0], da), g_ff[2][1]))
+    dn1 = hold(dn1, g_cross.far[1], g_done[0])
+    g_attn = [Scatter(order, g) for order, g in zip(ATTN_SCATTER, (g_attn[:4], g_attn[4:]))]
+    for g in g_attn:
+        g.first_far()
     g_cross.second()
-    for j in range(groups):
-        send, kept = sends[j]
-        g_attn.append(Scatter(ATTN_SCATTER[j]).first(hold(send, dn1), kept))
-    g_done.append(ff_sum(hold(g_ff[2][0], dn1), g_ff[2][1]))
-    dn1 = hold(dn1, g_done[0])
+    for g in g_attn:
+        g.first_near()
     dtok, _, sums_one = norm_back(dn1, swap(dn1, T), start, dh1, norms, 0)
     dtok = restore(dtok, b, c, outer)
 
@@ -862,34 +922,30 @@
     g_norm = jnp.concatenate([s[i : i + 1] for i in (0, 1) for s in sums], axis=0)
     g_norm = g_norm[:, : 2 * q4] + lax.ppermute(g_norm[:, 2 * q4 :], "C", FLIP)
     g_norm = g_norm[:, :q4] + lax.ppermute(g_norm[:, q4:], "B", FLIP)
-    g_norm = TAIL.run(scatter_z, jnp.pad(g_norm.T, ((0, 0), (0, 128 - g_norm.shape[0]))))
+    g_norm = jnp.pad(g_norm.T.astype(BF16), ((0, 0), (0, 128 - g_norm.shape[0])))
+    g_norm = g_norm.reshape(outer, block, 128)
+    g_norm = jnp.pad(g_norm, ((0, 0), (0, pair_block), (0, 0))).reshape(-1, 128)
     dctx = dctx.astype(F32) + swap(dctx, T).astype(F32)
     dctx = from_rel(dctx.reshape(slots, keys, -1)[:, :cond], outer, b, c)
 
-    g_attn[0].second()
-    g_attn[1].second()
-
-    out_half = collect(y) + by_core(h2)[0]
-    out_half = (out_half * pick(t, live_rows[:half], live_rows[half:])).astype(BF16)
-    out_half = lax.optimization_barrier(out_half)
-    mixed = restore(from_core(out_half, swap(out_half, T)), b, c, outer)
-
-    g_attn[2].second()
+    for g in g_attn:
+        g.second()
+
     g_cross.kept = hold(g_cross.kept, *g_done)
+    g_cross.kept = jnp.concatenate([g_cross.kept, g_norm], axis=1)
     g_cross = g_cross.third()
-    g_attn[0].kept = hold(g_attn[0].kept, dtok, dctx)
-    g_attn_0 = g_attn[0].third()
+    g_norm = g_cross[:block, 2 * local :]
+    g_cross = g_cross[:, : 2 * local]
     g_ff = jnp.concatenate(g_done, axis=1).reshape(block, part_blocks, 2, 3 * UB)
     own, far = g_ff[:, :, 0], lax.ppermute(g_ff[:, :, 1], "C", FLIP)
     g_ff = jnp.stack([pick(c, own, far), pick(c, far, own)], axis=1).astype(F32)
     g_ff = g_ff.reshape(block, 2, part_blocks, 3, UB).transpose(0, 3, 1, 2, 4)
     g_ff = g_ff.reshape(block, 3, units)
     g_gate_up, g_down = g_ff[:, :2], g_ff[:, 2].T
-    g_attn[1].kept = hold(g_attn[1].kept, mixed, g_gate_up, g_down)
-    g_attn = [g_attn_0] + [g.third() for g in g_attn[1:]]
-
-    g_attn = jnp.stack([g.reshape(block, 4, GW) for g in g_attn], axis=2)
-    g_attn = g_attn.reshape(block, 4, local)
+    g_attn = hold(jnp.concatenate([g.kept for g in g_attn], axis=1), mixed, dtok, dctx)
+    g_attn = TAIL.run(scatter_z, g_attn).astype(F32)
+
+    g_attn = g_attn.reshape(block, 2, groups, 2, GW).transpose(0, 1, 3, 2, 4).reshape(block, 4, local)
     g_cross = g_cross.reshape(block + pair_block, groups, 2, GW)
     g_pair = g_cross[block:].transpose(0, 2, 1, 3)
     g_cross = g_cross[:block]

time: 818 us -> 773 us (0.945)
  other arithmetic: 81.3 us -> 63.1 us
  Pallas kernels: 234 us -> 217 us
  starting transfers between devices: 52.4 us -> 38.6 us
    ppermute x24 -> x25, waiting for transfers between devices: 159 us -> 240 us  [run(): self.last = move(value)]
    all_gather x5, waiting for transfers between devices: 37.1 us -> 4.16 us  [gather_z(): return lax.all_gather(shard, 'A', axis=0, tiled=True)]
    ppermute x3, waiting for transfers between devices: 42.3 us -> 12.6 us  [the longest x2 12.6 us: on_device(): far = lax.ppermute(hold(g[:, :, 1], dc), 'B', FLIP)]
    pallas_call x20 -> x16, Pallas kernels: 234 us -> 217 us  [call(): pl.pallas_call(body, out_shape=outs, grid=grid, in_specs=specs, out_specs...]
    ppermute x1, waiting for transfers between devices: 0.01 us -> 16.6 us  [on_device(): g_norm = g_norm[:, :q4] + lax.ppermute(g_norm[:, q4:], 'B', FLIP)]
    ppermute x1, waiting for transfers between devices: 19.6 us -> 4.14 us  [on_device(): g_norm = g_norm[:, :2 * q4] + lax.ppermute(g_norm[:, 2 * q4:], 'C', FLIP)]
    unnamed x14 -> x10, waiting for transfers between devices: 12.5 us -> 0.84 us
    all_gather x5, starting transfers between devices: 11.9 us -> 0.38 us  [gather_z(): return lax.all_gather(shard, 'A', axis=0, tiled=True)]
  transfers between devices with their start and end apart: 54 -> 52, of which waited for: 28 -> 26; matrix products, arithmetic and copies ran while one was open for 22% -> 21% of each run, Pallas kernels for 25% -> 28%
where the time goes in v3:
time: 773 us; the launch traced here: 764 us
  waiting for transfers between devices  306 us (40%)
  Pallas kernels  217 us (28%)
  local copies, waits for them, and re-layouts  122 us (16%)
  other arithmetic  63.1 us (8%)
  starting transfers between devices  38.6 us (5%)
  between operations  17.7 us (2%)
    ppermute x25, waiting for transfers between devices, run(): self.last = move(value)  240 us
    pallas_call x16, Pallas kernels, call(): pl.pallas_call(body, out_shape=outs, grid=grid, in_specs=specs, out_specs...  217 us
    unnamed x146, local copies, waits for them, and re-layouts  38.1 us
    ppermute x25, starting transfers between devices, run(): self.last = move(value)  31.7 us
    ppermute x1, waiting for transfers between devices, on_device(): own, far = (g_ff[:, :, 0], lax.ppermute(g_ff[:, :, 1], 'C', FLIP))  17.6 us
    ppermute x1, waiting for transfers between devices, on_device(): g_norm = g_norm[:, :q4] + lax.ppermute(g_norm[:, q4:], 'B', FLIP)  16.6 us
  transfers between devices with their start and end apart: 52, of which 26 were waited for; matrix products, arithmetic and copies ran while one was open for 21% of the time, Pallas kernels for 28%

profile of v3, /device:TPU:0, one launch (start us, length us, event | category | flops | bytes accessed | tf_op | source)
XLA Modules:
  0.0 764.4 jit_solution(2240092647703384218)
XLA Ops:
  23.3 18.0 %collective-permute-done = bf16[96,6,768]{2,0,1:T(8,128)(2,1)S(1)} collective-permute-done((bf16[96,6,768]{2,0,1:T(8,128)(2,1)}, bf16[96,6,768]{2,0,1:T(8,128)(2,1)S(1)}, u32[]{:S(2)}, u32[]{:S(2)}) %collective-permute-start) | collective-permute-done | bytes 884768 | tf_op jit(solution)/shard_map/ppermute | solution.py:35
  47.8 12.8 %collective-permute-done.1 = bf16[96,3072]{1,0:T(8,128)(2,1)S(1)} collective-permute-done((bf16[96,3072]{1,0:T(8,128)(2,1)S(1)}, bf16[96,3072]{1,0:T(8,128)(2,1)S(1)}, u32[]{:S(2)}, u32[]{:S(2)}) %collective-permute-start.1) | collective-permute-done | bytes 589856 | tf_op jit(solution)/shard_map/ppermute | solution.py:35
  69.1 52.3 %collective-permute-done.2.refs_1_.refs_2_.refs_4_ = bf16[384,3200]{1,0:T(8,128)(2,1)S(1)} collective-permute-done((bf16[384,3200]{1,0:T(8,128)(2,1)}, bf16[384,3200]{1,0:T(8,128)(2,1)S(1)}, u32[]{:S(2)}, u32[]{:S(2)}) %collective-permute-start.2) | collective-permute-done | bytes 2457632 | tf_op jit(solution)/shard_map/ppermute | solution.py:35
  134.1 12.6 %collective-permute-done.4.refs_3_.refs_5_.refs_7_ = bf16[384,1152]{1,0:T(8,128)(2,1)} collective-permute-done((bf16[384,1152]{1,0:T(8,128)(2,1)}, bf16[384,1152]{1,0:T(8,128)(2,1)}, u32[]{:S(2)}, u32[]{:S(2)}) %collective-permute-start.4) | collective-permute-done | bytes 884768 | tf_op jit(solution)/shard_map/ppermute | solution.py:35
  148.2 10.9 %collective-permute-done.5.refs_4_.refs_6_ = bf16[384,2048]{1,0:T(8,128)(2,1)} collective-permute-done((bf16[384,2048]{1,0:T(8,128)(2,1)}, bf16[384,2048]{1,0:T(8,128)(2,1)}, u32[]{:S(2)}, u32[]{:S(2)}) %collective-permute-start.5) | collective-permute-done | bytes 1572896 | tf_op jit(solution)/shard_map/ppermute | solution.py:35
  172.1 4.9 copy.161
  200.6 18.3 %self_forward.1 = (bf16[512,3072]{1,0:T(8,128)(2,1)}, bf16[512,1536]{1,0:T(8,128)(2,1)}) custom-call(bf16[512,1536]{1,0:T(8,128)(2,1)} %add_norm.3.refs_0_.refs_1_, bf16[384,3200]{1,0:T(8,128)(2,1)} %all-gather.6.cloned.1.call-done.refs_0_.refs_1_.refs_3_, bf16[384,3200]{1,0:T(8,128)(2,1)} %copy-done.2, bf16[384,3200]{1,0:T(8,128)(2,1)} %copy-done.3, ...), custom_call_target="tpu_custom_call" | custom-call | flops 1 | bytes 1 | tf_op jit(solution)/shard_map/self_forward/pallas_call | solution.py:177
  226.1 24.0 %collective-permute-done.10.refs_7_.refs_11_ = bf16[576,1024]{1,0:T(8,128)(2,1)} collective-permute-done((bf16[576,1024]{1,0:T(8,128)(2,1)}, bf16[576,1024]{1,0:T(8,128)(2,1)}, u32[]{:S(2)}, u32[]{:S(2)}) %collective-permute-start.10) | collective-permute-done | bytes 1179680 | tf_op jit(solution)/shard_map/ppermute | solution.py:35
  254.5 4.9 add_norm.4
  260.2 15.1 %cross_forward.1 = (bf16[512,1536]{1,0:T(8,128)(2,1)}, bf16[288,1536]{1,0:T(8,128)(2,1)}, bf16[512,1536]{1,0:T(8,128)(2,1)}) custom-call(bf16[512,1536]{1,0:T(8,128)(2,1)} %get-tuple-element.96.n_ref, bf16[288,768]{1,0:T(8,128)(2,1)} %bitcast.140, bf16[576,1536]{1,0:T(8,128)(2,1)} %all-gather.8.cloned.1.call-done.refs_0_.refs_4_.refs_8_, ...), custom_call_target="tpu_custom_call" | custom-call | flops 1 | bytes 1 | tf_op jit(solution)/shard_map/cross_forward/pallas_call | solution.py:177
  286.0 11.0 %collective-permute-done.12 = bf16[256,1536]{1,0:T(8,128)(2,1)S(1)} collective-permute-done((bf16[256,1536]{1,0:T(8,128)(2,1)S(1)}, bf16[256,1536]{1,0:T(8,128)(2,1)S(1)}, u32[]{:S(2)}, u32[]{:S(2)}) %collective-permute-start.12) | collective-permute-done | bytes 786464 | tf_op jit(solution)/shard_map/ppermute | solution.py:35
  306.0 11.3 %collective-permute-done.13 = bf16[256,1536]{1,0:T(8,128)(2,1)} collective-permute-done((bf16[256,1536]{1,0:T(8,128)(2,1)S(1)}, bf16[256,1536]{1,0:T(8,128)(2,1)}, u32[]{:S(2)}, u32[]{:S(2)}) %collective-permute-start.13) | collective-permute-done | bytes 786464 | tf_op jit(solution)/shard_map/ppermute | solution.py:35
  322.8 28.2 %feed_forward.3 = (bf16[384,6144]{1,0:T(8,128)(2,1)}, bf16[1024,1536]{1,0:T(8,128)(2,1)}, bf16[1024,1536]{1,0:T(8,128)(2,1)}) custom-call(bf16[1024,1536]{1,0:T(8,128)(2,1)} %pad_maximum_fusion.refs_0_, bf16[1024,1536]{1,0:T(8,128)(2,1)} %pad_maximum_fusion.1.refs_1_, bf16[384,6144]{1,0:T(8,128)(2,1)} %all-gather.10.cloned.1.call-done.refs_2_.refs_3_, ...), custom_call_target="tpu_custom_call" | custom-call | flops 1 | bytes 1 | tf_op jit(solution)/shard_map/feed_forward/pallas_call | solution.py:177
  351.1 28.3 %feed_forward.4 = (bf16[384,6144]{1,0:T(8,128)(2,1)}, bf16[1024,1536]{1,0:T(8,128)(2,1)}, bf16[1024,1536]{1,0:T(8,128)(2,1)}) custom-call(bf16[1024,1536]{1,0:T(8,128)(2,1)} %pad_maximum_fusion.refs_0_, bf16[1024,1536]{1,0:T(8,128)(2,1)} %pad_maximum_fusion.1.refs_1_, bf16[384,3072]{1,0:T(8,128)(2,1)} %all-gather.12.cloned.1.call-done.refs_2_, ...), custom_call_target="tpu_custom_call" | custom-call | flops 1 | bytes 1 | tf_op jit(solution)/shard_map/feed_forward/pallas_call | solution.py:177
  379.4 28.6 %feed_forward.5 = (bf16[384,3072]{1,0:T(8,128)(2,1)}, bf16[384,3072]{1,0:T(8,128)(2,1)}, bf16[1024,1536]{1,0:T(8,128)(2,1)}, bf16[1024,1536]{1,0:T(8,128)(2,1)}) custom-call(bf16[1024,1536]{1,0:T(8,128)(2,1)} %pad_maximum_fusion.refs_0_, bf16[1024,1536]{1,0:T(8,128)(2,1)} %pad_maximum_fusion.1.refs_1_, ...), custom_call_target="tpu_custom_call" | custom-call | flops 1 | bytes 1 | tf_op jit(solution)/shard_map/feed_forward/pallas_call | solution.py:177
  424.2 17.0 %collective-permute-done.20 = bf16[256,1536]{1,0:T(8,128)(2,1)} collective-permute-done((bf16[256,1536]{1,0:T(8,128)(2,1)}, bf16[256,1536]{1,0:T(8,128)(2,1)}, u32[]{:S(2)}, u32[]{:S(2)}) %collective-permute-start.20) | collective-permute-done | bytes 786464 | tf_op jit(solution)/shard_map/ppermute | solution.py:35
  442.6 4.7 fusion.14
  450.8 6.5 norm_back.3
  457.3 10.1 %collective-permute-done.21 = bf16[256,1536]{1,0:T(8,128)(2,1)S(1)} collective-permute-done((bf16[256,1536]{1,0:T(8,128)(2,1)S(1)}, bf16[256,1536]{1,0:T(8,128)(2,1)S(1)}, u32[]{:S(2)}, u32[]{:S(2)}) %collective-permute-start.21) | collective-permute-done | bytes 786464 | tf_op jit(solution)/shard_map/ppermute | solution.py:35
  470.3 25.2 %cross_backward.1 = (bf16[576,1536]{1,0:T(8,128)(2,1)}, bf16[576,1536]{1,0:T(8,128)(2,1)}, bf16[576,1536]{1,0:T(8,128)(2,1)}, bf16[576,1536]{1,0:T(8,128)(2,1)},...) custom-call(bf16[512,1536]{1,0:T(8,128)(2,1)} %get-tuple-element.120.dc_ref, ...), custom_call_target="tpu_custom_call" | custom-call | flops 1 | bytes 1 | tf_op jit(solution)/shard_map/cross_backward/pallas_call | solution.py:177
  500.2 6.7 norm_back.4
  516.6 30.2 %self_backward.1 = (bf16[384,1536]{1,0:T(8,128)(2,1)}, bf16[384,1536]{1,0:T(8,128)(2,1)}, bf16[384,1536]{1,0:T(8,128)(2,1)}, bf16[384,1536]{1,0:T(8,128)(2,1)}, ...) custom-call(bf16[512,1536]{1,0:T(8,128)(2,1)} %get-tuple-element.127, ...), custom_call_target="tpu_custom_call" | custom-call | flops 1 | bytes 1 | tf_op jit(solution)/shard_map/self_backward/pallas_call | solution.py:177
  556.0 18.5 %collective-permute-done.30 = bf16[384,1536]{1,0:T(8,128)(2,1)S(1)} collective-permute-done((bf16[384,1536]{1,0:T(8,128)(2,1)}, bf16[384,1536]{1,0:T(8,128)(2,1)S(1)}, u32[]{:S(2)}, u32[]{:S(2)}) %collective-permute-start.30) | collective-permute-done | bytes 1179680 | tf_op jit(solution)/shard_map/ppermute | solution.py:35
  581.8 11.2 %collective-permute-done.33 = bf16[576,1536]{1,0:T(8,128)(2,1)} collective-permute-done((bf16[576,1536]{1,0:T(8,128)(2,1)}, bf16[576,1536]{1,0:T(8,128)(2,1)}, u32[]{:S(2)}, u32[]{:S(2)}) %collective-permute-start.33) | collective-permute-done | bytes 1769504 | tf_op jit(solution)/shard_map/ppermute | solution.py:35
  593.6 6.4 norm_back.5
  603.5 10.6 %collective-permute-done.31 = bf16[576,1536]{1,0:T(8,128)(2,1)} collective-permute-done((bf16[576,1536]{1,0:T(8,128)(2,1)}, bf16[576,1536]{1,0:T(8,128)(2,1)}, u32[]{:S(2)}, u32[]{:S(2)}) %collective-permute-start.31) | collective-permute-done | bytes 1769504 | tf_op jit(solution)/shard_map/ppermute | solution.py:35
  623.8 16.6 %collective-permute-done.39 = f32[6,384]{1,0:T(8,128)S(1)} collective-permute-done((f32[6,384]{1,0:T(8,128)S(1)}, f32[6,384]{1,0:T(8,128)S(1)}, u32[]{:S(2)}, u32[]{:S(2)}) %collective-permute-start.39) | collective-permute-done | bytes 9248 | tf_op jit(solution)/shard_map/ppermute | solution.py:924
  659.8 5.0 restore.3
  664.8 11.4 %collective-permute-done.37 = bf16[384,1536]{1,0:T(8,128)(2,1)} collective-permute-done((bf16[384,1536]{1,0:T(8,128)(2,1)}, bf16[384,1536]{1,0:T(8,128)(2,1)}, u32[]{:S(2)}, u32[]{:S(2)}) %collective-permute-start.37) | collective-permute-done | bytes 1179680 | tf_op jit(solution)/shard_map/ppermute | solution.py:35
  682.8 5.1 reduce-scatter.10.cloned.1.call-done
  692.1 12.6 %collective-permute-done.40 = bf16[96,2,1536]{2,0,1:T(8,128)(2,1)S(1)} collective-permute-done((bf16[96,2,1536]{2,0,1:T(8,128)(2,1)S(1)}, bf16[96,2,1536]{2,0,1:T(8,128)(2,1)S(1)}, u32[]{:S(2)}, u32[]{:S(2)}) %collective-permute-start.40) | collective-permute-done | bytes 589856 | tf_op jit(solution)/shard_map/ppermute | solution.py:908
  711.3 17.6 %collective-permute-done.41 = bf16[96,6,768]{2,0,1:T(8,128)(2,1)} collective-permute-done((bf16[96,6,768]{2,0,1:T(8,128)(2,1)S(1)}, bf16[96,6,768]{2,0,1:T(8,128)(2,1)}, u32[]{:S(2)}, u32[]{:S(2)}) %collective-permute-start.41) | collective-permute-done | bytes 884768 | tf_op jit(solution)/shard_map/ppermute | solution.py:940
  (388 shorter events, 250.0 us)
Async XLA Ops:
  7.2 58.9 %all-gather.6.cloned.1.call-start = ((), (), s32[]{:S(2)}) async-start(), calls=%async_computation.5 | async-start | bytes 3072000 | tf_op jit(solution)/shard_map/all_gather | solution.py:98
  11.2 122.9 %all-gather.8.cloned.1.call-start = ((), (), s32[]{:S(2)}) async-start(), calls=%async_computation.6 | async-start | bytes 2211840 | tf_op jit(solution)/shard_map/all_gather | solution.py:98
  12.5 213.6 %all-gather.12.cloned.1.call-start = ((), (), s32[]{:S(2)}) async-start(), calls=%async_computation.8 | async-start | bytes 2949120 | tf_op jit(solution)/shard_map/all_gather | solution.py:98
  45.9 229.4 %all-gather.10.cloned.1.call-start = ((), (), s32[]{:S(2)}) async-start(), calls=%async_computation.7 | async-start | bytes 5898240 | tf_op jit(solution)/shard_map/all_gather | solution.py:98
  61.8 236.9 %all-gather.14.cloned.1.call-start = ((), (), s32[]{:S(2)}) async-start(), calls=%async_computation.9 | async-start | bytes 2949120 | tf_op jit(solution)/shard_map/all_gather | solution.py:98
  66.1 55.3 %collective-permute-start.2 = (bf16[384,3200]{1,0:T(8,128)(2,1)}, bf16[384,3200]{1,0:T(8,128)(2,1)S(1)}, u32[]{:S(2)}, u32[]{:S(2)}) collective-permute-start(bf16[384,3200]{1,0:T(8,128)(2,1)} %all-gather.6.cloned.1.call-done.refs_0_.refs_1_.refs_3_), channel_id=1, source_target_pairs={{0,4},{4,0},{1,5},{5,1},{2,6},{6,2},{3,7},{7,3},{8,12},{12,8},{9,1... | collective-permute-start | bytes 7372808 | tf_op jit(solution)/shard_map/ppermute | solution.py:35
  67.6 55.8 %collective-permute-start.3 = (bf16[384,3200]{1,0:T(8,128)(2,1)}, bf16[384,3200]{1,0:T(8,128)(2,1)S(1)}, u32[]{:S(2)}, u32[]{:S(2)}) collective-permute-start(bf16[384,3200]{1,0:T(8,128)(2,1)} %all-gather.6.cloned.1.call-done.refs_0_.refs_1_.refs_3_), channel_id=1, source_target_pairs={{0,2},{2,0},{1,3},{3,1},{4,6},{6,4},{5,7},{7,5},{8,10},{10,8},{9,1... | collective-permute-start | bytes 7372808 | tf_op jit(solution)/shard_map/ppermute | solution.py:35
  123.4 35.6 %collective-permute-start.5 = (bf16[384,2048]{1,0:T(8,128)(2,1)}, bf16[384,2048]{1,0:T(8,128)(2,1)}, u32[]{:S(2)}, u32[]{:S(2)}) collective-permute-start(bf16[384,2048]{1,0:T(8,128)(2,1)} %slice.520), channel_id=1, source_target_pairs={{0,2},{2,0},{1,3},{3,1},{4,6},{6,4},{5,7},{7,5},{8,10},{10,8},{9,1... | collective-permute-start | bytes 4718600 | tf_op jit(solution)/shard_map/ppermute | solution.py:35
  146.7 74.8 %collective-permute-start.7 = (bf16[576,1536]{1,0:T(8,128)(2,1)}, bf16[576,1536]{1,0:T(8,128)(2,1)S(1)}, u32[]{:S(2)}, u32[]{:S(2)}) collective-permute-start(bf16[576,1536]{1,0:T(8,128)(2,1)} %all-gather.8.cloned.1.call-done.refs_0_.refs_4_.refs_8_), channel_id=1, source_target_pairs={{0,4},{4,0},{1,5},{5,1},{2,6},{6,2},{3,7},{7,3},{8,12},{12,8},{9,1... | collective-permute-start | bytes 5308424 | tf_op jit(solution)/shard_map/ppermute | solution.py:35
  159.0 61.2 %collective-permute-start.8 = (bf16[576,1536]{1,0:T(8,128)(2,1)}, bf16[576,1536]{1,0:T(8,128)(2,1)S(1)}, u32[]{:S(2)}, u32[]{:S(2)}) collective-permute-start(bf16[576,1536]{1,0:T(8,128)(2,1)} %all-gather.8.cloned.1.call-done.refs_0_.refs_4_.refs_8_), channel_id=1, source_target_pairs={{0,2},{2,0},{1,3},{3,1},{4,6},{6,4},{5,7},{7,5},{8,10},{10,8},{9,1... | collective-permute-start | bytes 5308424 | tf_op jit(solution)/shard_map/ppermute | solution.py:35
  218.9 35.6 %collective-permute-start.6 = (bf16[512,1536]{1,0:T(8,128)(2,1)}, bf16[512,1536]{1,0:T(8,128)(2,1)}, u32[]{:S(2)}, u32[]{:S(2)}) collective-permute-start(bf16[512,1536]{1,0:T(8,128)(2,1)} %get-tuple-element.94.refs_2_), channel_id=1, source_target_pairs={{0,1},{1,0},{2,3},{3,2},{4,5},{5,4},{6,7},{7,6},{8,9},{9,8},{10,11... | collective-permute-start | bytes 4718600 | tf_op jit(solution)/shard_map/ppermute | solution.py:45
  220.2 292.3 %reduce-scatter.6.cloned.1.call-start = ((), (), s32[]{:S(2)}) async-start(), calls=%async_computation.10 | async-start | bytes 5898240 | tf_op jit(solution)/shard_map/reduce_scatter | solution.py:102
  221.5 28.7 %collective-permute-start.10 = (bf16[576,1024]{1,0:T(8,128)(2,1)}, bf16[576,1024]{1,0:T(8,128)(2,1)}, u32[]{:S(2)}, u32[]{:S(2)}) collective-permute-start(bf16[576,1024]{1,0:T(8,128)(2,1)} %slice.537), channel_id=1, source_target_pairs={{0,4},{4,0},{1,5},{5,1},{2,6},{6,2},{3,7},{7,3},{8,12},{12,8},{9,1... | collective-permute-start | bytes 3538952 | tf_op jit(solution)/shard_map/ppermute | solution.py:35
  225.2 34.1 %collective-permute-start.9 = (bf16[576,512]{1,0:T(8,128)(2,1)}, bf16[576,512]{1,0:T(8,128)(2,1)S(1)}, u32[]{:S(2)}, u32[]{:S(2)}) collective-permute-start(bf16[576,512]{1,0:T(8,128)(2,1)} %slice.536), channel_id=1, source_target_pairs={{0,2},{2,0},{1,3},{3,1},{4,6},{6,4},{5,7},{7,5},{8,10},{10,8},{9,1... | collective-permute-start | bytes 1769480 | tf_op jit(solution)/shard_map/ppermute | solution.py:35
  250.1 53.2 %collective-permute-start.14 = (bf16[384,3072]{1,0:T(8,128)(2,1)}, bf16[384,3072]{1,0:T(8,128)(2,1)}, u32[]{:S(2)}, u32[]{:S(2)}) collective-permute-start(bf16[384,3072]{1,0:T(8,128)(2,1)} %all-gather.12.cloned.1.call-done.refs_2_), channel_id=1, source_target_pairs={{0,4},{4,0},{1,5},{5,1},{2,6},{6,2},{3,7},{7,3},{8,12},{12,8},{9,1... | collective-permute-start | bytes 7077896 | tf_op jit(solution)/shard_map/ppermute | solution.py:35
  303.3 76.1 %collective-permute-start.17 = (bf16[384,3072]{1,0:T(8,128)(2,1)}, bf16[384,3072]{1,0:T(8,128)(2,1)}, u32[]{:S(2)}, u32[]{:S(2)}) collective-permute-start(bf16[384,3072]{1,0:T(8,128)(2,1)} %all-gather.14.cloned.1.call-done.refs_2_), channel_id=1, source_target_pairs={{0,4},{4,0},{1,5},{5,1},{2,6},{6,2},{3,7},{7,3},{8,12},{12,8},{9,1... | collective-permute-start | bytes 7077896 | tf_op jit(solution)/shard_map/ppermute | solution.py:35
  351.0 272.8 %reduce-scatter.8.cloned.1.call-start = ((), (), s32[]{:S(2)}) async-start(), calls=%async_computation.11 | async-start | bytes 2949120 | tf_op jit(solution)/shard_map/reduce_scatter | solution.py:102
  423.8 83.1 %collective-permute-start.24 = (bf16[384,3072]{1,0:T(8,128)(2,1)}, bf16[384,3072]{1,0:T(8,128)(2,1)}, u32[]{:S(2)}, u32[]{:S(2)}) collective-permute-start(bf16[384,3072]{1,0:T(8,128)(2,1)} %get-tuple-element.126), channel_id=1, source_target_pairs={{0,4},{4,0},{1,5},{5,1},{2,6},{6,2},{3,7},{7,3},{8,12},{12,8},{9,1... | collective-permute-start | bytes 7077896 | tf_op jit(solution)/shard_map/ppermute | solution.py:883
  510.9 146.9 %reduce-scatter.14.cloned.1.call-start = ((), (), s32[]{:S(2)}) async-start(), calls=%async_computation.14 | async-start | bytes 5898240 | tf_op jit(solution)/shard_map/reduce_scatter | solution.py:102
  511.7 176.2 %reduce-scatter.10.cloned.1.call-start = ((), (), s32[]{:S(2)}) async-start(), calls=%async_computation.12 | async-start | bytes 2396160 | tf_op jit(solution)/shard_map/reduce_scatter | solution.py:102
  511.7 40.9 %collective-permute-start.26 = (bf16[576,1536]{1,0:T(8,128)(2,1)}, bf16[576,1536]{1,0:T(8,128)(2,1)S(1)}, u32[]{:S(2)}, u32[]{:S(2)}) collective-permute-start(bf16[576,1536]{1,0:T(8,128)(2,1)} %get-tuple-element.132), channel_id=1, source_target_pairs={{0,2},{2,0},{1,3},{3,1},{4,6},{6,4},{5,7},{7,5},{8,10},{10,8},{9,1... | collective-permute-start | bytes 5308424 | tf_op jit(solution)/shard_map/ppermute | solution.py:35
  516.2 37.1 %collective-permute-start.27 = (bf16[96,2,1536]{2,0,1:T(8,128)(2,1)S(1)}, bf16[96,2,1536]{2,0,1:T(8,128)(2,1)S(1)}, u32[]{:S(2)}, u32[]{:S(2)}) collective-permute-start(bf16[96,2,1536]{2,0,1:T(8,128)(2,1)S(1)} %bitcast.154), channel_id=1, source_target_pairs={{0,4},{4,0},{1,5},{5,1},{2,6},{6,2},{3,7},{7,3},{8,12},{12,8},{9,1... | collective-permute-start | bytes 1769480 | tf_op jit(solution)/shard_map/ppermute | solution.py:908
  546.8 27.7 %collective-permute-start.30 = (bf16[384,1536]{1,0:T(8,128)(2,1)}, bf16[384,1536]{1,0:T(8,128)(2,1)S(1)}, u32[]{:S(2)}, u32[]{:S(2)}) collective-permute-start(bf16[384,1536]{1,0:T(8,128)(2,1)} %get-tuple-element.143), channel_id=1, source_target_pairs={{0,4},{4,0},{1,5},{5,1},{2,6},{6,2},{3,7},{7,3},{8,12},{12,8},{9,1... | collective-permute-start | bytes 3538952 | tf_op jit(solution)/shard_map/ppermute | solution.py:35
  552.7 40.2 %collective-permute-start.33 = (bf16[576,1536]{1,0:T(8,128)(2,1)}, bf16[576,1536]{1,0:T(8,128)(2,1)}, u32[]{:S(2)}, u32[]{:S(2)}) collective-permute-start(bf16[576,1536]{1,0:T(8,128)(2,1)} %get-tuple-element.150), channel_id=1, source_target_pairs={{0,2},{2,0},{1,3},{3,1},{4,6},{6,4},{5,7},{7,5},{8,10},{10,8},{9,1... | collective-permute-start | bytes 5308424 | tf_op jit(solution)/shard_map/ppermute | solution.py:35
  554.4 39.2 %collective-permute-start.28 = (bf16[512,1536]{1,0:T(8,128)(2,1)}, bf16[512,1536]{1,0:T(8,128)(2,1)}, u32[]{:S(2)}, u32[]{:S(2)}) collective-permute-start(bf16[512,1536]{1,0:T(8,128)(2,1)} %get-tuple-element.135.mine_ref), channel_id=1, source_target_pairs={{0,1},{1,0},{2,3},{3,2},{4,5},{5,4},{6,7},{7,6},{8,9},{9,8},{10,11... | collective-permute-start | bytes 4718600 | tf_op jit(solution)/shard_map/ppermute | solution.py:45
  574.6 39.6 %collective-permute-start.31 = (bf16[576,1536]{1,0:T(8,128)(2,1)}, bf16[576,1536]{1,0:T(8,128)(2,1)}, u32[]{:S(2)}, u32[]{:S(2)}) collective-permute-start(bf16[576,1536]{1,0:T(8,128)(2,1)} %add_convert_fusion.2), channel_id=1, source_target_pairs={{0,4},{4,0},{1,5},{5,1},{2,6},{6,2},{3,7},{7,3},{8,12},{12,8},{9,1... | collective-permute-start | bytes 5308424 | tf_op jit(solution)/shard_map/ppermute | solution.py:35
  592.9 30.4 %collective-permute-start.34 = (bf16[384,1536]{1,0:T(8,128)(2,1)}, bf16[384,1536]{1,0:T(8,128)(2,1)}, u32[]{:S(2)}, u32[]{:S(2)}) collective-permute-start(bf16[384,1536]{1,0:T(8,128)(2,1)} %get-tuple-element.151), channel_id=1, source_target_pairs={{0,2},{2,0},{1,3},{3,1},{4,6},{6,4},{5,7},{7,5},{8,10},{10,8},{9,1... | collective-permute-start | bytes 3538952 | tf_op jit(solution)/shard_map/ppermute | solution.py:35
  614.2 33.7 %collective-permute-start.32 = (bf16[384,1536]{1,0:T(8,128)(2,1)}, bf16[384,1536]{1,0:T(8,128)(2,1)}, u32[]{:S(2)}, u32[]{:S(2)}) collective-permute-start(bf16[384,1536]{1,0:T(8,128)(2,1)} %get-tuple-element.145), channel_id=1, source_target_pairs={{0,4},{4,0},{1,5},{5,1},{2,6},{6,2},{3,7},{7,3},{8,12},{12,8},{9,1... | collective-permute-start | bytes 3538952 | tf_op jit(solution)/shard_map/ppermute | solution.py:35
  623.4 27.5 %collective-permute-start.35 = (bf16[384,1536]{1,0:T(8,128)(2,1)}, bf16[384,1536]{1,0:T(8,128)(2,1)}, u32[]{:S(2)}, u32[]{:S(2)}) collective-permute-start(bf16[384,1536]{1,0:T(8,128)(2,1)} %get-tuple-element.152), channel_id=1, source_target_pairs={{0,2},{2,0},{1,3},{3,1},{4,6},{6,4},{5,7},{7,5},{8,10},{10,8},{9,1... | collective-permute-start | bytes 3538952 | tf_op jit(solution)/shard_map/ppermute | solution.py:35
  642.1 110.0 %reduce-scatter.12.cloned.1.call-start = ((), (), s32[]{:S(2)}) async-start(), calls=%async_computation.13 | async-start | bytes 2949120 | tf_op jit(solution)/shard_map/reduce_scatter | solution.py:102
  647.9 28.3 %collective-permute-start.37 = (bf16[384,1536]{1,0:T(8,128)(2,1)}, bf16[384,1536]{1,0:T(8,128)(2,1)}, u32[]{:S(2)}, u32[]{:S(2)}) collective-permute-start(bf16[384,1536]{1,0:T(8,128)(2,1)} %add_convert_fusion.4), channel_id=1, source_target_pairs={{0,4},{4,0},{1,5},{5,1},{2,6},{6,2},{3,7},{7,3},{8,12},{12,8},{9,1... | collective-permute-start | bytes 3538952 | tf_op jit(solution)/shard_map/ppermute | solution.py:35
  650.9 28.0 %collective-permute-start.36 = (bf16[384,1536]{1,0:T(8,128)(2,1)}, bf16[384,1536]{1,0:T(8,128)(2,1)}, u32[]{:S(2)}, u32[]{:S(2)}) collective-permute-start(bf16[384,1536]{1,0:T(8,128)(2,1)} %add_convert_fusion.6), channel_id=1, source_target_pairs={{0,2},{2,0},{1,3},{3,1},{4,6},{6,4},{5,7},{7,5},{8,10},{10,8},{9,1... | collective-permute-start | bytes 3538952 | tf_op jit(solution)/shard_map/ppermute | solution.py:35
  (71 other events, 578.5 us)
Sparse Core Ops, SparseCore 0:
  11.3 54.7 all-gather.5
  68.3 39.0 all-gather.7
  109.0 49.3 all-gather.11
  159.8 88.2 all-gather.9
  249.5 48.9 all-gather.13
  351.2 82.6 reduce-scatter.5
  511.1 45.3 reduce-scatter.7
  558.8 84.7 reduce-scatter.13
  646.5 41.3 reduce-scatter.9
  690.0 47.2 reduce-scatter.11

commit v4 on v3

--- a/solution.py
+++ b/solution.py
@@ -106,14 +106,15 @@
     return lax.optimization_barrier((value,) + others)[0]
 
 
-def gather(shard, split):
+def gather(shard, split, ready=()):
     first = gather_z(shard)
     over_y, over_x = swap(first, "B"), swap(first, "C")
     fourth = []
+    from_y, from_x = (hold(over_y, *ready), hold(over_x, *ready)) if ready else (over_y, over_x)
     if split > 0:
-        fourth.append((swap(over_y[:, :split], "C"), 0, split))
+        fourth.append((swap(from_y[:, :split], "C"), 0, split))
     if split < shard.shape[1]:
-        fourth.append((swap(over_x[:, split:], "B"), split, shard.shape[1]))
+        fourth.append((swap(from_x[:, split:], "B"), split, shard.shape[1]))
     n = shard.shape[1]
     return {
         (0, 0): [(first, 0, n)],
@@ -842,8 +843,12 @@
         at += blocks * 6 * UB
         early.append((shard, swap(shard, "B") if soon else None))
     grad_top = to_rel(cotangent.reshape(rows, width), outer, b, c) * live_rows.astype(BF16)
-    attn_w = gather(attn_in, ATTN_SPLIT * 4 * GW)
-    cross_w = gather(cross_in, CROSS_SPLIT * 2 * GW)
+    start = to_rel(tokens.reshape(rows, width), outer, b, c)
+    ctx = jnp.pad(to_rel(context, outer, b, c), ((0, 0), (0, keys - cond), (0, 0)))
+    ctx = ctx.reshape(slots * keys, -1)
+    tables = rotary_tables(length)
+    attn_w = gather(attn_in, ATTN_SPLIT * 4 * GW, (start, ctx) + tables)
+    cross_w = gather(cross_in, CROSS_SPLIT * 2 * GW, (grad_top,))
     grad_all = spread(grad_top)
     norm_at = groups * 4 * GW
     norms = norm_rows(attn_w, norm_at, q4)
@@ -856,10 +861,6 @@
             whole = gather_z(jnp.concatenate([shard, moved], axis=1))
             ff_w.append(((whole, 0), (whole, 1)))
 
-    start = to_rel(tokens.reshape(rows, width), outer, b, c)
-    ctx = jnp.pad(to_rel(context, outer, b, c), ((0, 0), (0, keys - cond), (0, 0)))
-    ctx = ctx.reshape(slots * keys, -1)
-    tables = rotary_tables(length)
 
     (n1,) = add_norm(start, None, None, norms, 0)
     keep_one, part = self_forward(n1, attn_w, tables, slots, groups)

time: 773 us -> 759 us (0.982)
  waiting for transfers between devices: 306 us -> 291 us
    ppermute x25, waiting for transfers between devices: 240 us -> 211 us  [run(): self.last = move(value)]
    all_gather x5, waiting for transfers between devices: 4.16 us -> 15.7 us  [gather_z(): return lax.all_gather(shard, 'A', axis=0, tiled=True)]
    unnamed x146 -> x132, local copies, waits for them, and re-layouts: 38.1 us -> 36.6 us
  transfers between devices with their start and end apart: 52 -> 52, of which waited for: 26 -> 26; matrix products, arithmetic and copies ran while one was open for 21% -> 23% of each run, Pallas kernels for 28% -> 29%
where the time goes in v4:
time: 759 us; the launch traced here: 751 us
  waiting for transfers between devices  291 us (38%)
  Pallas kernels  217 us (29%)
  local copies, waits for them, and re-layouts  124 us (16%)
  other arithmetic  63.2 us (8%)
  starting transfers between devices  37.9 us (5%)
  between operations  17.6 us (2%)
    pallas_call x16, Pallas kernels, call(): pl.pallas_call(body, out_shape=outs, grid=grid, in_specs=specs, out_specs...  217 us
    ppermute x25, waiting for transfers between devices, run(): self.last = move(value)  211 us
    unnamed x132, local copies, waits for them, and re-layouts  36.6 us
    ppermute x25, starting transfers between devices, run(): self.last = move(value)  30.3 us
    ppermute x1, waiting for transfers between devices, on_device(): own, far = (g_ff[:, :, 0], lax.ppermute(g_ff[:, :, 1], 'C', FLIP))  17.7 us
    ppermute x1, waiting for transfers between devices, on_device(): g_norm = g_norm[:, :q4] + lax.ppermute(g_norm[:, q4:], 'B', FLIP)  16.5 us
    all_gather x5, waiting for transfers between devices, gather_z(): return lax.all_gather(shard, 'A', axis=0, tiled=True)  15.7 us
  transfers between devices with their start and end apart: 52, of which 26 were waited for; matrix products, arithmetic and copies ran while one was open for 23% of the time, Pallas kernels for 29%

profile of v4, /device:TPU:0, one launch (start us, length us, event | category | flops | bytes accessed | tf_op | source)
XLA Modules:
  0.0 750.7 jit_solution(14539720118412246205)
XLA Ops:
  23.3 18.0 %collective-permute-done = bf16[96,6,768]{2,0,1:T(8,128)(2,1)S(1)} collective-permute-done((bf16[96,6,768]{2,0,1:T(8,128)(2,1)}, bf16[96,6,768]{2,0,1:T(8,128)(2,1)S(1)}, u32[]{:S(2)}, u32[]{:S(2)}) %collective-permute-start) | collective-permute-done | bytes 884768 | tf_op jit(solution)/shard_map/ppermute | solution.py:35
  47.7 12.8 %collective-permute-done.1 = bf16[96,3072]{1,0:T(8,128)(2,1)S(1)} collective-permute-done((bf16[96,3072]{1,0:T(8,128)(2,1)S(1)}, bf16[96,3072]{1,0:T(8,128)(2,1)S(1)}, u32[]{:S(2)}, u32[]{:S(2)}) %collective-permute-start.1) | collective-permute-done | bytes 589856 | tf_op jit(solution)/shard_map/ppermute | solution.py:35
  72.6 4.9 copy.142
  91.6 29.8 %collective-permute-done.2.refs_1_.refs_2_.refs_4_ = bf16[384,3200]{1,0:T(8,128)(2,1)S(1)} collective-permute-done((bf16[384,3200]{1,0:T(8,128)(2,1)}, bf16[384,3200]{1,0:T(8,128)(2,1)S(1)}, u32[]{:S(2)}, u32[]{:S(2)}) %collective-permute-start.2) | collective-permute-done | bytes 2457632 | tf_op jit(solution)/shard_map/ppermute | solution.py:35
  130.0 18.2 %collective-permute-done.4.refs_3_.refs_5_.refs_7_ = bf16[384,1152]{1,0:T(8,128)(2,1)} collective-permute-done((bf16[384,1152]{1,0:T(8,128)(2,1)S(1)}, bf16[384,1152]{1,0:T(8,128)(2,1)}, u32[]{:S(2)}, u32[]{:S(2)}) %collective-permute-start.4) | collective-permute-done | bytes 884768 | tf_op jit(solution)/shard_map/ppermute | solution.py:35
  149.7 11.0 %collective-permute-done.5.refs_4_.refs_6_ = bf16[384,2048]{1,0:T(8,128)(2,1)} collective-permute-done((bf16[384,2048]{1,0:T(8,128)(2,1)}, bf16[384,2048]{1,0:T(8,128)(2,1)}, u32[]{:S(2)}, u32[]{:S(2)}) %collective-permute-start.5) | collective-permute-done | bytes 1572896 | tf_op jit(solution)/shard_map/ppermute | solution.py:35
  165.8 5.0 copy.161
  191.3 18.4 %self_forward.1 = (bf16[512,3072]{1,0:T(8,128)(2,1)}, bf16[512,1536]{1,0:T(8,128)(2,1)}) custom-call(bf16[512,1536]{1,0:T(8,128)(2,1)} %add_norm.3.refs_0_.refs_1_, bf16[384,3200]{1,0:T(8,128)(2,1)} %all-gather.6.cloned.1.call-done.refs_0_.refs_1_.refs_3_, bf16[384,3200]{1,0:T(8,128)(2,1)} %copy-done.2, ...), custom_call_target="tpu_custom_call" | custom-call | flops 1 | bytes 1 | tf_op jit(solution)/shard_map/self_forward/pallas_call | solution.py:178
  217.0 25.5 %collective-permute-done.10.refs_7_.refs_11_ = bf16[576,1024]{1,0:T(8,128)(2,1)} collective-permute-done((bf16[576,1024]{1,0:T(8,128)(2,1)}, bf16[576,1024]{1,0:T(8,128)(2,1)}, u32[]{:S(2)}, u32[]{:S(2)}) %collective-permute-start.10) | collective-permute-done | bytes 1179680 | tf_op jit(solution)/shard_map/ppermute | solution.py:35
  248.4 15.2 %cross_forward.1 = (bf16[512,1536]{1,0:T(8,128)(2,1)}, bf16[288,1536]{1,0:T(8,128)(2,1)}, bf16[512,1536]{1,0:T(8,128)(2,1)}) custom-call(bf16[512,1536]{1,0:T(8,128)(2,1)} %get-tuple-element.102.n_ref, bf16[288,768]{1,0:T(8,128)(2,1)} %bitcast.140, bf16[576,1536]{1,0:T(8,128)(2,1)} %all-gather.8.cloned.1.call-done.refs_0_.refs_4_.refs_8_, ...), custom_call_target="tpu_custom_call" | custom-call | flops 1 | bytes 1 | tf_op jit(solution)/shard_map/cross_forward/pallas_call | solution.py:178
  273.4 10.4 %collective-permute-done.12 = bf16[256,1536]{1,0:T(8,128)(2,1)S(1)} collective-permute-done((bf16[256,1536]{1,0:T(8,128)(2,1)S(1)}, bf16[256,1536]{1,0:T(8,128)(2,1)S(1)}, u32[]{:S(2)}, u32[]{:S(2)}) %collective-permute-start.12) | collective-permute-done | bytes 786464 | tf_op jit(solution)/shard_map/ppermute | solution.py:35
  285.2 13.5 %all-gather.14.cloned.1.call-done.refs_2_ = bf16[384,3072]{1,0:T(8,128)(2,1)} async-done(((bf16[96,3072]{1,0:T(8,128)(2,1)}), bf16[384,3072]{1,0:T(8,128)(2,1)}) %all-gather.14.cloned.1.call-update) | async-done | bytes 2359312 | tf_op jit(solution)/shard_map/all_gather | solution.py:98
  309.4 28.2 %feed_forward.3 = (bf16[384,6144]{1,0:T(8,128)(2,1)}, bf16[1024,1536]{1,0:T(8,128)(2,1)}, bf16[1024,1536]{1,0:T(8,128)(2,1)}) custom-call(bf16[1024,1536]{1,0:T(8,128)(2,1)} %pad_maximum_fusion.refs_0_, bf16[1024,1536]{1,0:T(8,128)(2,1)} %pad_maximum_fusion.1.refs_1_, bf16[384,6144]{1,0:T(8,128)(2,1)} %all-gather.10.cloned.1.call-done.refs_2_.refs_3_, ...), custom_call_target="tpu_custom_call" | custom-call | flops 1 | bytes 1 | tf_op jit(solution)/shard_map/feed_forward/pallas_call | solution.py:178
  337.7 28.5 %feed_forward.4 = (bf16[384,6144]{1,0:T(8,128)(2,1)}, bf16[1024,1536]{1,0:T(8,128)(2,1)}, bf16[1024,1536]{1,0:T(8,128)(2,1)}) custom-call(bf16[1024,1536]{1,0:T(8,128)(2,1)} %pad_maximum_fusion.refs_0_, bf16[1024,1536]{1,0:T(8,128)(2,1)} %pad_maximum_fusion.1.refs_1_, bf16[384,3072]{1,0:T(8,128)(2,1)} %all-gather.12.cloned.1.call-done.refs_2_, ...), custom_call_target="tpu_custom_call" | custom-call | flops 1 | bytes 1 | tf_op jit(solution)/shard_map/feed_forward/pallas_call | solution.py:178
  366.2 28.6 %feed_forward.5 = (bf16[384,3072]{1,0:T(8,128)(2,1)}, bf16[384,3072]{1,0:T(8,128)(2,1)}, bf16[1024,1536]{1,0:T(8,128)(2,1)}, bf16[1024,1536]{1,0:T(8,128)(2,1)}) custom-call(bf16[1024,1536]{1,0:T(8,128)(2,1)} %pad_maximum_fusion.refs_0_, bf16[1024,1536]{1,0:T(8,128)(2,1)} %pad_maximum_fusion.1.refs_1_, ...), custom_call_target="tpu_custom_call" | custom-call | flops 1 | bytes 1 | tf_op jit(solution)/shard_map/feed_forward/pallas_call | solution.py:178
  410.8 17.1 %collective-permute-done.20 = bf16[256,1536]{1,0:T(8,128)(2,1)} collective-permute-done((bf16[256,1536]{1,0:T(8,128)(2,1)}, bf16[256,1536]{1,0:T(8,128)(2,1)}, u32[]{:S(2)}, u32[]{:S(2)}) %collective-permute-start.20) | collective-permute-done | bytes 786464 | tf_op jit(solution)/shard_map/ppermute | solution.py:35
  429.3 4.7 fusion.14
  437.1 6.5 norm_back.3
  443.6 10.4 %collective-permute-done.21 = bf16[256,1536]{1,0:T(8,128)(2,1)S(1)} collective-permute-done((bf16[256,1536]{1,0:T(8,128)(2,1)S(1)}, bf16[256,1536]{1,0:T(8,128)(2,1)S(1)}, u32[]{:S(2)}, u32[]{:S(2)}) %collective-permute-start.21) | collective-permute-done | bytes 786464 | tf_op jit(solution)/shard_map/ppermute | solution.py:35
  456.9 25.2 %cross_backward.1 = (bf16[576,1536]{1,0:T(8,128)(2,1)}, bf16[576,1536]{1,0:T(8,128)(2,1)}, bf16[576,1536]{1,0:T(8,128)(2,1)}, bf16[576,1536]{1,0:T(8,128)(2,1)},...) custom-call(bf16[512,1536]{1,0:T(8,128)(2,1)} %get-tuple-element.128.dc_ref, ...), custom_call_target="tpu_custom_call" | custom-call | flops 1 | bytes 1 | tf_op jit(solution)/shard_map/cross_backward/pallas_call | solution.py:178
  486.8 6.6 norm_back.4
  503.1 30.2 %self_backward.1 = (bf16[384,1536]{1,0:T(8,128)(2,1)}, bf16[384,1536]{1,0:T(8,128)(2,1)}, bf16[384,1536]{1,0:T(8,128)(2,1)}, bf16[384,1536]{1,0:T(8,128)(2,1)}, ...) custom-call(bf16[512,1536]{1,0:T(8,128)(2,1)} %get-tuple-element.135, ...), custom_call_target="tpu_custom_call" | custom-call | flops 1 | bytes 1 | tf_op jit(solution)/shard_map/self_backward/pallas_call | solution.py:178
  542.3 18.7 %collective-permute-done.30 = bf16[384,1536]{1,0:T(8,128)(2,1)S(1)} collective-permute-done((bf16[384,1536]{1,0:T(8,128)(2,1)}, bf16[384,1536]{1,0:T(8,128)(2,1)S(1)}, u32[]{:S(2)}, u32[]{:S(2)}) %collective-permute-start.30) | collective-permute-done | bytes 1179680 | tf_op jit(solution)/shard_map/ppermute | solution.py:35
  568.1 11.4 %collective-permute-done.33 = bf16[576,1536]{1,0:T(8,128)(2,1)} collective-permute-done((bf16[576,1536]{1,0:T(8,128)(2,1)}, bf16[576,1536]{1,0:T(8,128)(2,1)}, u32[]{:S(2)}, u32[]{:S(2)}) %collective-permute-start.33) | collective-permute-done | bytes 1769504 | tf_op jit(solution)/shard_map/ppermute | solution.py:35
  579.8 6.3 norm_back.5
  590.0 10.6 %collective-permute-done.31 = bf16[576,1536]{1,0:T(8,128)(2,1)} collective-permute-done((bf16[576,1536]{1,0:T(8,128)(2,1)}, bf16[576,1536]{1,0:T(8,128)(2,1)}, u32[]{:S(2)}, u32[]{:S(2)}) %collective-permute-start.31) | collective-permute-done | bytes 1769504 | tf_op jit(solution)/shard_map/ppermute | solution.py:35
  610.2 16.5 %collective-permute-done.39 = f32[6,384]{1,0:T(8,128)S(1)} collective-permute-done((f32[6,384]{1,0:T(8,128)S(1)}, f32[6,384]{1,0:T(8,128)S(1)}, u32[]{:S(2)}, u32[]{:S(2)}) %collective-permute-start.39) | collective-permute-done | bytes 9248 | tf_op jit(solution)/shard_map/ppermute | solution.py:925
  646.4 5.0 restore.3
  651.4 11.2 %collective-permute-done.37 = bf16[384,1536]{1,0:T(8,128)(2,1)} collective-permute-done((bf16[384,1536]{1,0:T(8,128)(2,1)}, bf16[384,1536]{1,0:T(8,128)(2,1)}, u32[]{:S(2)}, u32[]{:S(2)}) %collective-permute-start.37) | collective-permute-done | bytes 1179680 | tf_op jit(solution)/shard_map/ppermute | solution.py:35
  669.1 5.1 reduce-scatter.10.cloned.1.call-done
  678.4 12.6 %collective-permute-done.40 = bf16[96,2,1536]{2,0,1:T(8,128)(2,1)S(1)} collective-permute-done((bf16[96,2,1536]{2,0,1:T(8,128)(2,1)S(1)}, bf16[96,2,1536]{2,0,1:T(8,128)(2,1)S(1)}, u32[]{:S(2)}, u32[]{:S(2)}) %collective-permute-start.40) | collective-permute-done | bytes 589856 | tf_op jit(solution)/shard_map/ppermute | solution.py:909
  697.5 17.7 %collective-permute-done.41 = bf16[96,6,768]{2,0,1:T(8,128)(2,1)} collective-permute-done((bf16[96,6,768]{2,0,1:T(8,128)(2,1)S(1)}, bf16[96,6,768]{2,0,1:T(8,128)(2,1)}, u32[]{:S(2)}, u32[]{:S(2)}) %collective-permute-start.41) | collective-permute-done | bytes 884768 | tf_op jit(solution)/shard_map/ppermute | solution.py:941
  (374 shorter events, 249.2 us)
Async XLA Ops:
  7.2 58.9 %all-gather.6.cloned.1.call-start = ((), (), s32[]{:S(2)}) async-start(), calls=%async_computation.5 | async-start | bytes 3072000 | tf_op jit(solution)/shard_map/all_gather | solution.py:98
  11.2 118.8 %all-gather.8.cloned.1.call-start = ((), (), s32[]{:S(2)}) async-start(), calls=%async_computation.6 | async-start | bytes 2211840 | tf_op jit(solution)/shard_map/all_gather | solution.py:98
  12.5 204.5 %all-gather.12.cloned.1.call-start = ((), (), s32[]{:S(2)}) async-start(), calls=%async_computation.8 | async-start | bytes 2949120 | tf_op jit(solution)/shard_map/all_gather | solution.py:98
  45.8 217.8 %all-gather.10.cloned.1.call-start = ((), (), s32[]{:S(2)}) async-start(), calls=%async_computation.7 | async-start | bytes 5898240 | tf_op jit(solution)/shard_map/all_gather | solution.py:98
  61.7 237.0 %all-gather.14.cloned.1.call-start = ((), (), s32[]{:S(2)}) async-start(), calls=%async_computation.9 | async-start | bytes 2949120 | tf_op jit(solution)/shard_map/all_gather | solution.py:98
  66.1 55.3 %collective-permute-start.2 = (bf16[384,3200]{1,0:T(8,128)(2,1)}, bf16[384,3200]{1,0:T(8,128)(2,1)S(1)}, u32[]{:S(2)}, u32[]{:S(2)}) collective-permute-start(bf16[384,3200]{1,0:T(8,128)(2,1)} %all-gather.6.cloned.1.call-done.refs_0_.refs_1_.refs_3_), channel_id=1, source_target_pairs={{0,4},{4,0},{1,5},{5,1},{2,6},{6,2},{3,7},{7,3},{8,12},{12,8},{9,1... | collective-permute-start | bytes 7372808 | tf_op jit(solution)/shard_map/ppermute | solution.py:35
  67.6 57.5 %collective-permute-start.3 = (bf16[384,3200]{1,0:T(8,128)(2,1)}, bf16[384,3200]{1,0:T(8,128)(2,1)}, u32[]{:S(2)}, u32[]{:S(2)}) collective-permute-start(bf16[384,3200]{1,0:T(8,128)(2,1)} %all-gather.6.cloned.1.call-done.refs_0_.refs_1_.refs_3_), channel_id=1, source_target_pairs={{0,2},{2,0},{1,3},{3,1},{4,6},{6,4},{5,7},{7,5},{8,10},{10,8},{9,1... | collective-permute-start | bytes 7372808 | tf_op jit(solution)/shard_map/ppermute | solution.py:35
  125.1 35.6 %collective-permute-start.5 = (bf16[384,2048]{1,0:T(8,128)(2,1)}, bf16[384,2048]{1,0:T(8,128)(2,1)}, u32[]{:S(2)}, u32[]{:S(2)}) collective-permute-start(bf16[384,2048]{1,0:T(8,128)(2,1)} %slice.414), channel_id=1, source_target_pairs={{0,2},{2,0},{1,3},{3,1},{4,6},{6,4},{5,7},{7,5},{8,10},{10,8},{9,1... | collective-permute-start | bytes 4718600 | tf_op jit(solution)/shard_map/ppermute | solution.py:35
  148.2 65.6 %collective-permute-start.7 = (bf16[576,1536]{1,0:T(8,128)(2,1)}, bf16[576,1536]{1,0:T(8,128)(2,1)S(1)}, u32[]{:S(2)}, u32[]{:S(2)}) collective-permute-start(bf16[576,1536]{1,0:T(8,128)(2,1)} %all-gather.8.cloned.1.call-done.refs_0_.refs_4_.refs_8_), channel_id=1, source_target_pairs={{0,4},{4,0},{1,5},{5,1},{2,6},{6,2},{3,7},{7,3},{8,12},{12,8},{9,1... | collective-permute-start | bytes 5308424 | tf_op jit(solution)/shard_map/ppermute | solution.py:35
  160.7 51.8 %collective-permute-start.8 = (bf16[576,1536]{1,0:T(8,128)(2,1)}, bf16[576,1536]{1,0:T(8,128)(2,1)S(1)}, u32[]{:S(2)}, u32[]{:S(2)}) collective-permute-start(bf16[576,1536]{1,0:T(8,128)(2,1)} %all-gather.8.cloned.1.call-done.refs_0_.refs_4_.refs_8_), channel_id=1, source_target_pairs={{0,2},{2,0},{1,3},{3,1},{4,6},{6,4},{5,7},{7,5},{8,10},{10,8},{9,1... | collective-permute-start | bytes 5308424 | tf_op jit(solution)/shard_map/ppermute | solution.py:35
  209.6 34.3 %collective-permute-start.6 = (bf16[512,1536]{1,0:T(8,128)(2,1)}, bf16[512,1536]{1,0:T(8,128)(2,1)}, u32[]{:S(2)}, u32[]{:S(2)}) collective-permute-start(bf16[512,1536]{1,0:T(8,128)(2,1)} %get-tuple-element.100.refs_2_), channel_id=1, source_target_pairs={{0,1},{1,0},{2,3},{3,2},{4,5},{5,4},{6,7},{7,6},{8,9},{9,8},{10,11... | collective-permute-start | bytes 4718600 | tf_op jit(solution)/shard_map/ppermute | solution.py:45
  213.8 28.7 %collective-permute-start.10 = (bf16[576,1024]{1,0:T(8,128)(2,1)}, bf16[576,1024]{1,0:T(8,128)(2,1)}, u32[]{:S(2)}, u32[]{:S(2)}) collective-permute-start(bf16[576,1024]{1,0:T(8,128)(2,1)} %slice.436), channel_id=1, source_target_pairs={{0,4},{4,0},{1,5},{5,1},{2,6},{6,2},{3,7},{7,3},{8,12},{12,8},{9,1... | collective-permute-start | bytes 3538952 | tf_op jit(solution)/shard_map/ppermute | solution.py:35
  215.3 283.4 %reduce-scatter.6.cloned.1.call-start = ((), (), s32[]{:S(2)}) async-start(), calls=%async_computation.10 | async-start | bytes 5898240 | tf_op jit(solution)/shard_map/reduce_scatter | solution.py:102
  216.4 32.0 %collective-permute-start.9 = (bf16[576,512]{1,0:T(8,128)(2,1)}, bf16[576,512]{1,0:T(8,128)(2,1)}, u32[]{:S(2)}, u32[]{:S(2)}) collective-permute-start(bf16[576,512]{1,0:T(8,128)(2,1)} %slice.435), channel_id=1, source_target_pairs={{0,2},{2,0},{1,3},{3,1},{4,6},{6,4},{5,7},{7,5},{8,10},{10,8},{9,1... | collective-permute-start | bytes 1769480 | tf_op jit(solution)/shard_map/ppermute | solution.py:35
  242.5 56.2 %collective-permute-start.14 = (bf16[384,3072]{1,0:T(8,128)(2,1)}, bf16[384,3072]{1,0:T(8,128)(2,1)}, u32[]{:S(2)}, u32[]{:S(2)}) collective-permute-start(bf16[384,3072]{1,0:T(8,128)(2,1)} %all-gather.12.cloned.1.call-done.refs_2_), channel_id=1, source_target_pairs={{0,4},{4,0},{1,5},{5,1},{2,6},{6,2},{3,7},{7,3},{8,12},{12,8},{9,1... | collective-permute-start | bytes 7077896 | tf_op jit(solution)/shard_map/ppermute | solution.py:35
  298.7 67.5 %collective-permute-start.17 = (bf16[384,3072]{1,0:T(8,128)(2,1)}, bf16[384,3072]{1,0:T(8,128)(2,1)}, u32[]{:S(2)}, u32[]{:S(2)}) collective-permute-start(bf16[384,3072]{1,0:T(8,128)(2,1)} %all-gather.14.cloned.1.call-done.refs_2_), channel_id=1, source_target_pairs={{0,4},{4,0},{1,5},{5,1},{2,6},{6,2},{3,7},{7,3},{8,12},{12,8},{9,1... | collective-permute-start | bytes 7077896 | tf_op jit(solution)/shard_map/ppermute | solution.py:35
  337.6 272.6 %reduce-scatter.8.cloned.1.call-start = ((), (), s32[]{:S(2)}) async-start(), calls=%async_computation.11 | async-start | bytes 2949120 | tf_op jit(solution)/shard_map/reduce_scatter | solution.py:102
  410.1 83.3 %collective-permute-start.24 = (bf16[384,3072]{1,0:T(8,128)(2,1)}, bf16[384,3072]{1,0:T(8,128)(2,1)}, u32[]{:S(2)}, u32[]{:S(2)}) collective-permute-start(bf16[384,3072]{1,0:T(8,128)(2,1)} %get-tuple-element.134), channel_id=1, source_target_pairs={{0,4},{4,0},{1,5},{5,1},{2,6},{6,2},{3,7},{7,3},{8,12},{12,8},{9,1... | collective-permute-start | bytes 7077896 | tf_op jit(solution)/shard_map/ppermute | solution.py:884
  497.5 146.9 %reduce-scatter.14.cloned.1.call-start = ((), (), s32[]{:S(2)}) async-start(), calls=%async_computation.14 | async-start | bytes 5898240 | tf_op jit(solution)/shard_map/reduce_scatter | solution.py:102
  498.2 175.9 %reduce-scatter.10.cloned.1.call-start = ((), (), s32[]{:S(2)}) async-start(), calls=%async_computation.12 | async-start | bytes 2396160 | tf_op jit(solution)/shard_map/reduce_scatter | solution.py:102
  498.3 40.9 %collective-permute-start.26 = (bf16[576,1536]{1,0:T(8,128)(2,1)}, bf16[576,1536]{1,0:T(8,128)(2,1)S(1)}, u32[]{:S(2)}, u32[]{:S(2)}) collective-permute-start(bf16[576,1536]{1,0:T(8,128)(2,1)} %get-tuple-element.140), channel_id=1, source_target_pairs={{0,2},{2,0},{1,3},{3,1},{4,6},{6,4},{5,7},{7,5},{8,10},{10,8},{9,1... | collective-permute-start | bytes 5308424 | tf_op jit(solution)/shard_map/ppermute | solution.py:35
  502.5 37.1 %collective-permute-start.27 = (bf16[96,2,1536]{2,0,1:T(8,128)(2,1)S(1)}, bf16[96,2,1536]{2,0,1:T(8,128)(2,1)S(1)}, u32[]{:S(2)}, u32[]{:S(2)}) collective-permute-start(bf16[96,2,1536]{2,0,1:T(8,128)(2,1)S(1)} %bitcast.154), channel_id=1, source_target_pairs={{0,4},{4,0},{1,5},{5,1},{2,6},{6,2},{3,7},{7,3},{8,12},{12,8},{9,1... | collective-permute-start | bytes 1769480 | tf_op jit(solution)/shard_map/ppermute | solution.py:909
  533.3 27.7 %collective-permute-start.30 = (bf16[384,1536]{1,0:T(8,128)(2,1)}, bf16[384,1536]{1,0:T(8,128)(2,1)S(1)}, u32[]{:S(2)}, u32[]{:S(2)}) collective-permute-start(bf16[384,1536]{1,0:T(8,128)(2,1)} %get-tuple-element.151), channel_id=1, source_target_pairs={{0,4},{4,0},{1,5},{5,1},{2,6},{6,2},{3,7},{7,3},{8,12},{12,8},{9,1... | collective-permute-start | bytes 3538952 | tf_op jit(solution)/shard_map/ppermute | solution.py:35
  539.2 40.2 %collective-permute-start.33 = (bf16[576,1536]{1,0:T(8,128)(2,1)}, bf16[576,1536]{1,0:T(8,128)(2,1)}, u32[]{:S(2)}, u32[]{:S(2)}) collective-permute-start(bf16[576,1536]{1,0:T(8,128)(2,1)} %get-tuple-element.158), channel_id=1, source_target_pairs={{0,2},{2,0},{1,3},{3,1},{4,6},{6,4},{5,7},{7,5},{8,10},{10,8},{9,1... | collective-permute-start | bytes 5308424 | tf_op jit(solution)/shard_map/ppermute | solution.py:35
  540.6 39.2 %collective-permute-start.28 = (bf16[512,1536]{1,0:T(8,128)(2,1)}, bf16[512,1536]{1,0:T(8,128)(2,1)}, u32[]{:S(2)}, u32[]{:S(2)}) collective-permute-start(bf16[512,1536]{1,0:T(8,128)(2,1)} %get-tuple-element.143.mine_ref), channel_id=1, source_target_pairs={{0,1},{1,0},{2,3},{3,2},{4,5},{5,4},{6,7},{7,6},{8,9},{9,8},{10,11... | collective-permute-start | bytes 4718600 | tf_op jit(solution)/shard_map/ppermute | solution.py:45
  561.0 39.6 %collective-permute-start.31 = (bf16[576,1536]{1,0:T(8,128)(2,1)}, bf16[576,1536]{1,0:T(8,128)(2,1)}, u32[]{:S(2)}, u32[]{:S(2)}) collective-permute-start(bf16[576,1536]{1,0:T(8,128)(2,1)} %add_convert_fusion.2), channel_id=1, source_target_pairs={{0,4},{4,0},{1,5},{5,1},{2,6},{6,2},{3,7},{7,3},{8,12},{12,8},{9,1... | collective-permute-start | bytes 5308424 | tf_op jit(solution)/shard_map/ppermute | solution.py:35
  579.5 30.2 %collective-permute-start.34 = (bf16[384,1536]{1,0:T(8,128)(2,1)}, bf16[384,1536]{1,0:T(8,128)(2,1)}, u32[]{:S(2)}, u32[]{:S(2)}) collective-permute-start(bf16[384,1536]{1,0:T(8,128)(2,1)} %get-tuple-element.159), channel_id=1, source_target_pairs={{0,2},{2,0},{1,3},{3,1},{4,6},{6,4},{5,7},{7,5},{8,10},{10,8},{9,1... | collective-permute-start | bytes 3538952 | tf_op jit(solution)/shard_map/ppermute | solution.py:35
  600.6 33.6 %collective-permute-start.32 = (bf16[384,1536]{1,0:T(8,128)(2,1)}, bf16[384,1536]{1,0:T(8,128)(2,1)}, u32[]{:S(2)}, u32[]{:S(2)}) collective-permute-start(bf16[384,1536]{1,0:T(8,128)(2,1)} %get-tuple-element.153), channel_id=1, source_target_pairs={{0,4},{4,0},{1,5},{5,1},{2,6},{6,2},{3,7},{7,3},{8,12},{12,8},{9,1... | collective-permute-start | bytes 3538952 | tf_op jit(solution)/shard_map/ppermute | solution.py:35
  609.7 27.4 %collective-permute-start.35 = (bf16[384,1536]{1,0:T(8,128)(2,1)}, bf16[384,1536]{1,0:T(8,128)(2,1)}, u32[]{:S(2)}, u32[]{:S(2)}) collective-permute-start(bf16[384,1536]{1,0:T(8,128)(2,1)} %get-tuple-element.160), channel_id=1, source_target_pairs={{0,2},{2,0},{1,3},{3,1},{4,6},{6,4},{5,7},{7,5},{8,10},{10,8},{9,1... | collective-permute-start | bytes 3538952 | tf_op jit(solution)/shard_map/ppermute | solution.py:35
  628.5 109.9 %reduce-scatter.12.cloned.1.call-start = ((), (), s32[]{:S(2)}) async-start(), calls=%async_computation.13 | async-start | bytes 2949120 | tf_op jit(solution)/shard_map/reduce_scatter | solution.py:102
  634.2 28.3 %collective-permute-start.37 = (bf16[384,1536]{1,0:T(8,128)(2,1)}, bf16[384,1536]{1,0:T(8,128)(2,1)}, u32[]{:S(2)}, u32[]{:S(2)}) collective-permute-start(bf16[384,1536]{1,0:T(8,128)(2,1)} %add_convert_fusion.4), channel_id=1, source_target_pairs={{0,4},{4,0},{1,5},{5,1},{2,6},{6,2},{3,7},{7,3},{8,12},{12,8},{9,1... | collective-permute-start | bytes 3538952 | tf_op jit(solution)/shard_map/ppermute | solution.py:35
  637.1 28.0 %collective-permute-start.36 = (bf16[384,1536]{1,0:T(8,128)(2,1)}, bf16[384,1536]{1,0:T(8,128)(2,1)}, u32[]{:S(2)}, u32[]{:S(2)}) collective-permute-start(bf16[384,1536]{1,0:T(8,128)(2,1)} %add_convert_fusion.6), channel_id=1, source_target_pairs={{0,2},{2,0},{1,3},{3,1},{4,6},{6,4},{5,7},{7,5},{8,10},{10,8},{9,1... | collective-permute-start | bytes 3538952 | tf_op jit(solution)/shard_map/ppermute | solution.py:35
  (64 other events, 610.5 us)
Sparse Core Ops, SparseCore 0:
  11.3 54.7 all-gather.5
  68.3 39.0 all-gather.7
  109.6 49.3 all-gather.11
  160.4 88.2 all-gather.9
  250.0 48.6 all-gather.13
  337.8 82.4 reduce-scatter.5
  497.6 45.1 reduce-scatter.7
  545.1 84.7 reduce-scatter.13
  632.7 41.3 reduce-scatter.9
  676.3 47.2 reduce-scatter.11
